TPU v7x, 256 devices: a whole 4x4x8 slice. The times are simulated.
256 devices in a mesh: grid: 256 (over x, y, z, core).
Axes of the slice: x: 4, y: 4, z: 8, core: 2. Of those that a mesh axis runs over, the one named last changes fastest.
Arguments:
- right_sides: float32 [32, 256, 48, 128], P(None, 'grid'), may hold values from -54 to 54, as said below
- recycle: float32 [2, 24, 256, 48, 128], P(None, None, 'grid'), may hold values from -6 to 6
- medium: float32 [256, 48, 128], P('grid'), may hold values from 0.05 to 1
- shift_table: float32 [8], replicated, may hold values from 0.25 to 2
- shift_index: int32 [2], replicated, may hold values from 0 to 7
Outputs:
- solution: float32 [32, 256, 48, 128], P(None, 'grid')
- residue: float32 [32, 256, 48, 128], P(None, 'grid')
Inputs may be any that keep to these rules, and one draw needn't show every extreme that they name: `right_sides`: finite real values.
All inputs are finite; a program needn't handle non-finite values.
Results may differ from a plain program's by a relative error of at most 0.0003.
Values sent between devices are 32-bit elements; how exact they have to be, the bound alone decides.
No kernel may reach another device: no remote copies, remote signals or barrier semaphores. Data moves between devices by JAX's collectives and lax.ppermute only.
A program may use at most 64 MiB of HBM per device.

v0:
```python
import jax
import jax.numpy as jnp
from jax import lax
from jax.experimental import pallas as pl
from jax.experimental.pallas import tpu as pltpu
from jax.sharding import Mesh
from jax.sharding import PartitionSpec as P

GRID = ("grid_0", "grid_1", "grid_2", "grid_3")
STAGES = (("grid_0", "grid_1", "grid_3"), ("grid_2",))
NX = 48
NY = 128
K = 24
B = 16
SHIFT = 0.5
HIGH = lax.Precision.HIGHEST
F32 = jnp.float32
BF16 = jnp.bfloat16
PARAMS = pltpu.CompilerParams(vmem_limit_bytes=56 << 20)
VMEM = pl.BlockSpec(memory_space=pltpu.VMEM)
SMEM = pl.BlockSpec(memory_space=pltpu.SMEM)


def iota(shape, dim):
    return lax.broadcasted_iota(jnp.int32, shape, dim)


def small(left, right):
    return jnp.dot(left, right, precision=HIGH, preferred_element_type=F32)


def halves(values):
    top = values.astype(BF16)
    return top, (values - top.astype(F32)).astype(BF16)


def row_products(left, right):
    dims = (((1,), (1,)), ((), ()))
    n = left.shape[0]
    l_top, l_rest = halves(left)
    r_top, r_rest = halves(right)
    both = lax.dot_general(
        jnp.concatenate([l_top, l_rest], axis=0), r_top, dims, preferred_element_type=F32
    )
    last = lax.dot_general(l_top, r_rest, dims, preferred_element_type=F32)
    return both[:n] + both[n:] + last


def combination(coeffs, fields):
    c_both, c_top = coeffs
    n = c_top.shape[0]
    f_top, f_rest = halves(fields)
    both = jnp.dot(c_both, f_top, preferred_element_type=F32)
    last = jnp.dot(c_top, f_rest, preferred_element_type=F32)
    return both[:n] + both[n:] + last


def split_coeffs(coeffs):
    top, rest = halves(coeffs)
    return jnp.concatenate([top, rest], axis=0), top


def neighbours(x, read, before, after):
    f = read(x)
    total = before + after
    if x > 0:
        total = total + read(x - 1)
    if x < NX - 1:
        total = total + read(x + 1)
    lane = iota(f.shape, 1)
    total = total + jnp.where(lane == 0, 0.0, pltpu.roll(f, 1, 1))
    return total + jnp.where(lane == NY - 1, 0.0, pltpu.roll(f, NY - 1, 1))


def transposed(values):
    rows = values.shape[0]
    return jnp.concatenate([values, jnp.zeros((128 - rows, 128), F32)], axis=0).T


def eliminate(system, count):
    lane = iota((1, 128), 1)
    row = iota(system.shape, 0)
    for k in range(count):
        pivot_row = system[k : k + 1]
        pivot = jnp.where(lane < 64, pivot_row[:, k : k + 1], pivot_row[:, 64 + k : 65 + k])
        scaled = pivot_row / pivot
        column = jnp.where(lane < 64, system[:, k : k + 1], system[:, 64 + k : 65 + k])
        system = jnp.where(row == k, scaled, system - column * scaled)
    return system


def apply_kernel(table, index, u, u_before, u_after, medium, f_out):
    for g in range(2):
        rows = slice(K * g, K * g + K)
        base = 6.0 + table[index[g]]
        for x in range(NX):
            diagonal = medium[x : x + 1, :] + base
            f_out[x, rows] = diagonal * u[x, rows] - neighbours(
                x, lambda i: u[i, rows], u_before[x, rows], u_after[x, rows]
            )


def first_gram_kernel(f, b, b_before, b_after, medium, b1_out, gram_out):
    total = jnp.zeros((2 * K, 128), F32)
    zeros = jnp.zeros((8, 2 * NY), F32)
    tops = [jnp.zeros((B, NY), F32) for _ in range(2)]
    squares = [jnp.zeros((B, NY), F32) for _ in range(2)]

    def next_field(x):
        out = (medium[x : x + 1, :] - SHIFT) * b[x] - neighbours(
            x, lambda i: b[i], b_before[x], b_after[x]
        )
        b1_out[x] = out
        return out

    for x in range(0, NX, 2):
        fields = jnp.concatenate([f[x], f[x + 1]], axis=1)
        b_pair = jnp.concatenate([b[x], b[x + 1]], axis=1)
        b1_pair = jnp.concatenate([next_field(x), next_field(x + 1)], axis=1)
        right = []
        for g in range(2):
            bg = b_pair[B * g : B * g + B]
            b1g = b1_pair[B * g : B * g + B]
            right += [fields[K * g : K * g + K], bg, b1g, zeros]
            top = bg * b1g
            square = bg * bg
            tops[g] = tops[g] + top[:, :NY] + top[:, NY:]
            squares[g] = squares[g] + square[:, :NY] + square[:, NY:]
        total = total + row_products(fields, jnp.concatenate(right, axis=0))
    lane = iota((K, 128), 1)
    row = iota((K, 128), 0)
    packed = jnp.where(lane < 64, total[:K], total[K:])
    for g in range(2):
        here = (row == 0) & (lane == 64 * g + 56)
        packed = jnp.where(here, jnp.sum(tops[g], keepdims=True), packed)
        here = (row == 0) & (lane == 64 * g + 57)
        packed = jnp.where(here, jnp.sum(squares[g], keepdims=True), packed)
    gram_out[...] = packed


def inverse_kernel(gram, out):
    lane = iota((K, 128), 1)
    row = iota((K, 128), 0)
    place = lane & 63
    unit = jnp.where(place == row + K, 1.0, 0.0)
    out[...] = eliminate(jnp.where(place < K, gram[...], unit), K)


def second_gram_kernel(f, f_before, f_after, b1, medium, fields_out, gram_out):
    total = jnp.zeros((2 * K, 128), F32)

    def next_field(x):
        return (medium[x : x + 1, :] - SHIFT) * f[x] - neighbours(
            x, lambda i: f[i], f_before[x], f_after[x]
        )

    for x in range(0, NX, 2):
        nexts = [next_field(x), next_field(x + 1)]
        for i in range(2):
            for g in range(2):
                at = 40 * g
                fields_out[x + i, at : at + K] = nexts[i][K * g : K * g + K]
                fields_out[x + i, at + K : at + K + B] = b1[x + i, B * g : B * g + B]
        f_pair = jnp.concatenate([f[x], f[x + 1]], axis=1)
        f1_pair = jnp.concatenate(nexts, axis=1)
        b1_pair = jnp.concatenate([b1[x], b1[x + 1]], axis=1)
        right = []
        for g in range(2):
            right += [
                f_pair[K * g : K * g + K],
                f1_pair[K * g : K * g + K],
                b1_pair[B * g : B * g + B],
            ]
        total = total + row_products(f1_pair, jnp.concatenate(right, axis=0))
    lane = iota((K, 128), 1)
    gram_out[...] = jnp.where(lane < 64, total[:K], total[K:])


def krylov_kernel(
    first, inverse, second, f, b, fields, before, after, medium, q_out, last_out, coef_out, shift_out
):
    first_t = transposed(first[...])
    second_t = transposed(second[...])
    inverse_t = transposed(inverse[...])
    coeffs = []
    thetas = []
    for g in range(2):
        at = 64 * g
        ginv = inverse_t[at + K : at + 2 * K, :K]
        fb = first_t[at + K : at + K + B, :K]
        fb1 = first_t[at + K + B : at + K + 2 * B, :K]
        ff1 = second_t[at : at + K, :K]
        f1f1 = second_t[at + K : at + 2 * K, :K]
        f1b1 = second_t[at + 2 * K : at + 2 * K + B, :K]
        theta = first_t[at + 56 : at + 57, :1] / first_t[at + 57 : at + 58, :1]
        z0 = small(fb, ginv)
        z1 = small(fb1 - small(z0, ff1), ginv)
        z2 = small(f1b1 - small(z0, f1f1) - small(z1, ff1), ginv)
        z2 = z2 - theta * z1
        mixed = z1 - theta * z0
        zero = jnp.zeros((B, K), F32)
        pad = jnp.zeros((B, 8), F32)
        table = jnp.concatenate(
            [
                jnp.concatenate([z0, zero, zero, pad], axis=1),
                jnp.concatenate([mixed, z0, zero, pad], axis=1),
                jnp.concatenate([z2 - theta * mixed, mixed, z0, pad], axis=1),
            ],
            axis=0,
        )
        coeffs.append(split_coeffs(-table))
        thetas.append(theta)
        for i, z in enumerate((z0, z1, z2, ginv)):
            coef_out[g, 24 * i : 24 * i + z.shape[0], :K] = z
        shift_out[8 * g : 8 * g + 8, :] = jnp.broadcast_to(theta, (8, 128))

    def next_field(x, g):
        rows = slice(40 * g, 40 * g + 40)
        return (medium[x : x + 1, :] - SHIFT - thetas[g]) * fields[x, rows] - neighbours(
            x, lambda i: fields[i, rows], before[x, rows], after[x, rows]
        )

    zeros = jnp.zeros((8, 2 * NY), F32)
    for x in range(0, NX, 2):
        for g in range(2):
            nexts = jnp.concatenate([next_field(x, g), next_field(x + 1, g)], axis=1)
            rows = slice(40 * g, 40 * g + 40)
            firsts = jnp.concatenate([fields[x, rows], fields[x + 1, rows]], axis=1)
            frows = slice(K * g, K * g + K)
            brows = slice(B * g, B * g + B)
            f_pair = jnp.concatenate([f[x, frows], f[x + 1, frows]], axis=1)
            b0 = jnp.concatenate([b[x, brows], b[x + 1, brows]], axis=1)
            theta = thetas[g]
            made = combination(
                coeffs[g], jnp.concatenate([f_pair, firsts[:K], nexts[:K], zeros], axis=0)
            )
            b1 = firsts[K:]
            q1 = b1 - theta * b0
            made = made + jnp.concatenate([b0, q1, nexts[K:] - theta * q1], axis=0)
            for i in range(2):
                part = made[:, NY * i : NY * i + NY]
                q_out[x + i, 48 * g : 48 * g + 48] = part
                last_out[x + i, brows] = part[2 * B :]


def moment_kernel(q, last, last_before, last_after, fields, medium, shift, t_out, gram_out):
    zeros = jnp.zeros((40, 2 * NY), F32)
    grams = []
    for g in range(2):
        theta = shift[8 * g : 8 * g + 1, :]
        brows = slice(B * g, B * g + B)

        def next_field(x):
            out = (medium[x : x + 1, :] - SHIFT - theta) * last[x, brows] - neighbours(
                x, lambda i: last[i, brows], last_before[x, brows], last_after[x, brows]
            )
            t_out[x, brows] = out
            return out

        qrows = slice(48 * g, 48 * g + 48)
        frows = slice(40 * g, 40 * g + K)
        total = jnp.zeros((64, 128), F32)
        for x in range(0, NX, 2):
            left = jnp.concatenate(
                [
                    jnp.concatenate([q[x, qrows], q[x + 1, qrows]], axis=1),
                    jnp.concatenate([next_field(x), next_field(x + 1)], axis=1),
                ],
                axis=0,
            )
            f1 = jnp.concatenate([fields[x, frows], fields[x + 1, frows]], axis=1)
            total = total + row_products(left, jnp.concatenate([left, f1, zeros], axis=0))
        grams.append(total)
    lane = iota((B, 128), 1)
    row = iota((B, 128), 0)
    column = lane & 15
    strips = []
    for gram in grams:
        strips.append(
            jnp.where(
                lane < 32,
                gram[:16],
                jnp.where(
                    lane < 64,
                    pltpu.roll(gram[16:32], 16, 1),
                    jnp.where(
                        lane < 96, pltpu.roll(gram[32:48], 32, 1), pltpu.roll(gram[48:64], 48, 1)
                    ),
                ),
            )
        )
    packed = jnp.where(row <= column, strips[0], strips[1])
    packed = jnp.where(lane < 112, packed, 0.0)
    on_diagonal = jnp.where((row == column) & (lane < 112), strips[1], 0.0)
    for k in range(7):
        inside = (lane >= 16 * k) & (lane < 16 * k + 16)
        own = jnp.sum(jnp.where(inside, on_diagonal, 0.0), axis=1, keepdims=True)
        packed = jnp.where(lane == 112 + k, own, packed)
    low = jnp.zeros((8, 128), F32)
    lane8 = iota((8, 128), 1)
    for g in range(2):
        for half in range(2):
            at = 24 * (2 * g + half)
            piece = pltpu.roll(grams[g][32 + 8 * half : 40 + 8 * half], (at - 64) % 128, 1)
            low = jnp.where((lane8 >= at) & (lane8 < at + K), piece, low)
    gram_out[:B] = packed
    gram_out[B:] = low


def finish_kernel(table, index, moments, coef, shift, u, f, q, t, solution_out, residue_out):
    packed = moments[:B]
    turned = transposed(packed)
    lane = iota((B, 128), 1)
    row = iota((B, 128), 0)
    column = lane & 15
    flipped = turned[:B]
    for k in range(1, 7):
        flipped = flipped + pltpu.roll(turned[16 * k : 16 * k + 16], 16 * k, 1)
    diagonal = packed
    for k in range(7):
        diagonal = jnp.where(
            (lane >= 16 * k) & (lane < 16 * k + 16), packed[:, 112 + k : 113 + k], diagonal
        )
    strips = [
        jnp.where(row <= column, packed, flipped),
        jnp.where(row == column, diagonal, jnp.where(row > column, packed, flipped)),
    ]
    shifts = []
    thirds = []
    blocks = [[], [], []]
    parts = []
    for g in range(2):
        c = 6.0 + SHIFT + table[index[g]] + shift[8 * g : 8 * g + 1, :]
        shifts.append(c)
        at = 48 * g
        f1q2 = jnp.concatenate(
            [moments[B:, at : at + K], moments[B:, at + K : at + 2 * K]], axis=0
        )
        z3 = small(f1q2, coef[g, 72 : 72 + K, :K])
        thirds.append(z3)
        taken = lax.dot_general(
            z3, f1q2, (((1,), (1,)), ((), ())), precision=HIGH, preferred_element_type=F32
        )
        wide = jnp.concatenate([taken, jnp.zeros((B, 112), F32)], axis=1)
        strip = strips[g] - pltpu.roll(wide, 96, 1)
        once = pltpu.roll(strip, 16, 1)
        twice = pltpu.roll(strip, 32, 1)
        squared = strip + 2.0 * c * once + c * c * twice
        right = strip + c * once
        parts.append(
            [
                jnp.where(
                    lane < 48,
                    pltpu.roll(squared, 128 - 16 * (i + 1), 1),
                    pltpu.roll(right, 48 - 16 * i, 1),
                )
                for i in (1, 2, 3)
            ]
        )
    system = jnp.concatenate(
        [jnp.where(lane < 64, parts[0][i], pltpu.roll(parts[1][i], 64, 1)) for i in range(3)],
        axis=0,
    )
    solved = transposed(eliminate(system, 48))
    coeffs = []
    for g in range(2):
        c = shifts[g][:, :1]
        ys = solved[64 * g + 48 : 64 * g + 64]
        y1, y2, y3 = (ys[:, 16 * i : 16 * i + 16] for i in range(3))
        z0, z1, z2 = (coef[g, 24 * i : 24 * i + B, :K] for i in range(3))
        on_f = small(y3, thirds[g])
        on_u = z0 - small(y1, z1) - small(y2, z2) - on_f
        none = jnp.zeros((B, K), F32)
        rows = jnp.concatenate(
            [
                jnp.concatenate([on_u, none, y1, y2, y3, jnp.zeros((B, B), F32)], axis=1),
                jnp.concatenate(
                    [none, on_f, -c * y1, -y1 - c * y2, -y2 - c * y3, -y3], axis=1
                ),
            ],
            axis=0,
        )
        coeffs.append(split_coeffs(rows))
    for x in range(0, NX, 2):
        for g in range(2):
            krows = slice(K * g, K * g + K)
            brows = slice(B * g, B * g + B)
            qrows = slice(48 * g, 48 * g + 48)

            def stack(x):
                return jnp.concatenate(
                    [u[x, krows], f[x, krows], q[x, qrows], t[x, brows]], axis=0
                )

            made = combination(
                coeffs[g], jnp.concatenate([stack(x), stack(x + 1)], axis=1)
            )
            for i in range(2):
                part = made[:, NY * i : NY * i + NY]
                solution_out[x + i, brows] = part[:B]
                residue_out[x + i, brows] = part[B:] + q[x + i, 48 * g : 48 * g + B]


def call(kernel, shapes, scalars, *arrays):
    out = [jax.ShapeDtypeStruct(s, F32) for s in shapes]
    count = len(arrays) - scalars
    return pl.pallas_call(
        kernel,
        out_shape=out,
        in_specs=[SMEM] * scalars + [VMEM] * count,
        out_specs=[VMEM] * len(out),
        compiler_params=PARAMS,
        name=kernel.__name__,
    )(*arrays)


def everyone(values):
    for axes in STAGES:
        size = lax.axis_size(axes)
        spread = jnp.broadcast_to(values[None], (size, *values.shape))
        values = jnp.sum(lax.all_to_all(spread, axes, 0, 0, tiled=True), axis=0)
    return values


def beside(values):
    count = lax.axis_size(GRID)
    ends = count - 1
    before = lax.ppermute(values, GRID, [(i, i + 1) for i in range(ends)])
    after = lax.ppermute(values, GRID, [(i + 1, i) for i in range(ends)])
    return before, after


def on_device(right_sides, recycle, medium, shift_table, shift_index):
    med = medium[0]
    u = jnp.transpose(recycle.reshape(2 * K, NX, NY), (1, 0, 2))
    b = jnp.transpose(right_sides.reshape(2 * B, NX, NY), (1, 0, 2))
    u_sides = beside(u)
    b_sides = beside(b)
    (f,) = call(apply_kernel, [(NX, 2 * K, NY)], 2, shift_table, shift_index, u, *u_sides, med)
    f_sides = beside(f)
    b1, gram = call(
        first_gram_kernel, [(NX, 2 * B, NY), (K, 128)], 0, f, b, *b_sides, med
    )
    first = everyone(gram)
    (inverse,) = call(inverse_kernel, [(K, 128)], 0, first)
    fields, gram = call(
        second_gram_kernel, [(NX, 80, NY), (K, 128)], 0, f, *f_sides, b1, med
    )
    field_sides = beside(fields)
    second = everyone(gram)
    q, last, coef, shift = call(
        krylov_kernel,
        [(NX, 96, NY), (NX, 2 * B, NY), (2, 96, 128), (16, 128)],
        0,
        first,
        inverse,
        second,
        f,
        b,
        fields,
        *field_sides,
        med,
    )
    last_sides = beside(last)
    t, gram = call(
        moment_kernel,
        [(NX, 2 * B, NY), (K, 128)],
        0,
        q,
        last,
        *last_sides,
        fields,
        med,
        shift,
    )
    moments = everyone(gram)
    solution, residue = call(
        finish_kernel,
        [(NX, 2 * B, NY)] * 2,
        2,
        shift_table,
        shift_index,
        moments,
        coef,
        shift,
        u,
        f,
        q,
        t,
    )
    shape = right_sides.shape
    return (
        jnp.transpose(solution, (1, 0, 2)).reshape(shape),
        jnp.transpose(residue, (1, 0, 2)).reshape(shape),
    )


def solution(mesh):
    torus = Mesh(mesh.devices.reshape(4, 4, 8, 2), GRID)
    in_specs = (
        P(None, GRID, None, None),
        P(None, None, GRID, None, None),
        P(GRID, None, None),
        P(),
        P(),
    )
    out_specs = (P(None, GRID, None, None), P(None, GRID, None, None))
    return jax.shard_map(
        on_device, mesh=torus, in_specs=in_specs, out_specs=out_specs, check_vma=False
    )
```

profile of v0, /device:TPU:8, one launch (start us, length us, event | category | flops | bytes accessed | tf_op | source)
XLA Modules:
  0.0 237.3 jit_solution(15848227342758612059)
XLA Ops:
  0.6 1.7 copy.11
  2.3 0.0 copy-start
  2.3 7.1 %collective-permute-start.1 = (f32[48,48,128]{2,1,0:T(8,128)S(1)}, f32[48,48,128]{2,1,0:T(8,128)S(1)}, u32[]{:S(2)}, u32[]{:S(2)}) collective-permute-start(f32[48,48,128]{2,1,0:T(8,128)S(1)} %bitcast.15), channel_id=1, source_target_pairs={{1,0},{2,1},{3,2},{4,3},{5,4},{6,5},{7,6},{8,7},{9,8},{10,9},{11,1... | collective-permute-start | bytes 3538952 | tf_op jit(solution)/shard_map/ppermute | solution.py:429
  9.4 1.9 collective-permute-start
  11.3 11.8 %collective-permute-done.1.u_after = f32[48,48,128]{2,1,0:T(8,128)S(1)} collective-permute-done((f32[48,48,128]{2,1,0:T(8,128)S(1)}, f32[48,48,128]{2,1,0:T(8,128)S(1)}, u32[]{:S(2)}, u32[]{:S(2)}) %collective-permute-start.1) | collective-permute-done | bytes 1179680 | tf_op jit(solution)/shard_map/ppermute | solution.py:429
  23.1 5.9 %collective-permute-done.u_before = f32[48,48,128]{2,1,0:T(8,128)S(1)} collective-permute-done((f32[48,48,128]{2,1,0:T(8,128)S(1)}, f32[48,48,128]{2,1,0:T(8,128)S(1)}, u32[]{:S(2)}, u32[]{:S(2)}) %collective-permute-start) | collective-permute-done | bytes 1179680 | tf_op jit(solution)/shard_map/ppermute | solution.py:428
  29.0 0.0 copy-done
  29.0 0.0 copy-done.5
  29.0 1.0 copy-done.6
  30.1 3.8 %apply_kernel.1.f = f32[48,48,128]{2,1,0:T(8,128)} custom-call(f32[8]{0:T(128)} %table.3, s32[2]{0:T(128)} %index.3, f32[48,48,128]{2,1,0:T(8,128)} %bitcast.17, f32[48,48,128]{2,1,0:T(8,128)} %copy-done.6, f32[48,48,128]{2,1,0:T(8,128)} %copy-done.5, f32[48,128]{1,0:T(8,128)} %bitcast.25), custom_call_target="tpu_custom_call" | custom-call | tf_op jit(solution)/shard_map/apply_kernel/pallas_call | solution.py:407
  33.9 1.9 collective-permute-start.5
  35.8 2.4 %collective-permute-start.4 = (f32[48,48,128]{2,1,0:T(8,128)}, f32[48,48,128]{2,1,0:T(8,128)S(1)}, u32[]{:S(2)}, u32[]{:S(2)}) collective-permute-start(f32[48,48,128]{2,1,0:T(8,128)} %apply_kernel.1.f), channel_id=1, source_target_pairs={{0,1},{1,2},{2,3},{3,4},{4,5},{5,6},{6,7},{7,8},{8,9},{9,10},{10,1... | collective-permute-start | bytes 3538952 | tf_op jit(solution)/shard_map/ppermute | solution.py:428
  38.2 0.0 copy-done.11
  38.2 0.3 copy.16
  38.5 0.0 copy-start.1
  38.5 5.3 %collective-permute-start.3 = (f32[48,32,128]{2,1,0:T(8,128)S(1)}, f32[48,32,128]{2,1,0:T(8,128)S(1)}, u32[]{:S(2)}, u32[]{:S(2)}) collective-permute-start(f32[48,32,128]{2,1,0:T(8,128)S(1)} %bitcast.19), channel_id=1, source_target_pairs={{1,0},{2,1},{3,2},{4,3},{5,4},{6,5},{7,6},{8,7},{9,8},{10,9},{11,1... | collective-permute-start | bytes 2359304 | tf_op jit(solution)/shard_map/ppermute | solution.py:429
  43.8 1.9 collective-permute-start.2
  45.7 12.4 %collective-permute-done.3.b_after = f32[48,32,128]{2,1,0:T(8,128)S(1)} collective-permute-done((f32[48,32,128]{2,1,0:T(8,128)S(1)}, f32[48,32,128]{2,1,0:T(8,128)S(1)}, u32[]{:S(2)}, u32[]{:S(2)}) %collective-permute-start.3) | collective-permute-done | bytes 786464 | tf_op jit(solution)/shard_map/ppermute | solution.py:429
  58.1 5.9 %collective-permute-done.2.b_before = f32[48,32,128]{2,1,0:T(8,128)S(1)} collective-permute-done((f32[48,32,128]{2,1,0:T(8,128)S(1)}, f32[48,32,128]{2,1,0:T(8,128)S(1)}, u32[]{:S(2)}, u32[]{:S(2)}) %collective-permute-start.2) | collective-permute-done | bytes 786464 | tf_op jit(solution)/shard_map/ppermute | solution.py:428
  64.1 0.0 copy-done.1
  64.1 0.0 copy-done.8
  64.1 0.9 copy-done.10
  64.9 3.8 %first_gram_kernel.1 = (f32[48,32,128]{2,1,0:T(8,128)}, f32[24,128]{1,0:T(8,128)}) custom-call(f32[48,48,128]{2,1,0:T(8,128)} %apply_kernel.1.f, f32[48,32,128]{2,1,0:T(8,128)} %bitcast.21, f32[48,32,128]{2,1,0:T(8,128)} %copy-done.10, f32[48,32,128]{2,1,0:T(8,128)} %copy-done.8, f32[48,128]{1,0:T(8,128)} %bitcast.26), custom_call_target="tpu_custom_call" | custom-call | tf_op jit(solution)/shard_map/first_gram_kernel/pallas_call | solution.py:407
  68.8 0.0 collective-permute-done.5.f_after
  68.8 0.0 collective-permute-done.4.f_before
  68.8 0.0 copy-start.4
  68.8 1.0 copy-done.3
  69.8 0.4 copy-done.4
  70.2 4.7 %second_gram_kernel.1 = (f32[48,80,128]{2,1,0:T(8,128)}, f32[24,128]{1,0:T(8,128)}) custom-call(f32[48,48,128]{2,1,0:T(8,128)} %apply_kernel.1.f, f32[48,48,128]{2,1,0:T(8,128)} %copy-done.4, f32[48,48,128]{2,1,0:T(8,128)} %copy-done.3, f32[48,32,128]{2,1,0:T(8,128)} %get-tuple-element.15.b1, f32[48,128]{1,0:T(8,128)} %bitcast.27), custom_call_target="tpu_custom_call" | custom-call | tf_op jit(solution)/shard_map/second_gram_kernel/pallas_call | solution.py:407
  74.9 2.0 collective-permute-start.7
  76.9 2.4 %collective-permute-start.6 = (f32[48,80,128]{2,1,0:T(8,128)}, f32[48,80,128]{2,1,0:T(8,128)}, u32[]{:S(2)}, u32[]{:S(2)}) collective-permute-start(f32[48,80,128]{2,1,0:T(8,128)} %get-tuple-element.17.fields), channel_id=1, source_target_pairs={{0,1},{1,2},{2,3},{3,4},{4,5},{5,6},{6,7},{7,8},{8,9},{9,10},{10,1... | collective-permute-start | bytes 5898248 | tf_op jit(solution)/shard_map/ppermute | solution.py:428
  79.3 0.0 copy-done.13
  79.4 41.1 %all_to_all.30 = f32[32,24,128]{2,1,0:T(8,128)S(1)} all-to-all(f32[32,24,128]{2,1,0:T(8,128)S(1)} %broadcast_in_dim.12), channel_id=1, replica_groups=mesh['grid_0'=4,'grid_1'=4,'grid_2'=8,'grid_3'=2] {'grid_0','grid_1','gr..., dimensions={0} | all-to-all | bytes 786432 | tf_op jit(solution)/shard_map/all_to_all | solution.py:421
  120.4 0.0 copy-done.14
  120.4 0.8 broadcast_in_dim.14
  121.2 5.8 %all-to-all-start.2 = ((f32[32,24,128]{2,1,0:T(8,128)}), f32[32,24,128]{2,1,0:T(8,128)S(1)}, u32[]{:S(2)}, u32[]{:S(2)}) async-start(f32[32,24,128]{2,1,0:T(8,128)} %broadcast_in_dim.14), calls=%async_computation.2 | async-start | bytes 786432 | tf_op jit(solution)/shard_map/all_to_all | solution.py:421
  127.0 8.7 %all-to-all-done.2 = f32[32,24,128]{2,1,0:T(8,128)S(1)} async-done(((f32[32,24,128]{2,1,0:T(8,128)}), f32[32,24,128]{2,1,0:T(8,128)S(1)}, u32[]{:S(2)}, u32[]{:S(2)}) %all-to-all-start.2) | async-done | bytes 393248 | tf_op jit(solution)/shard_map/all_to_all | solution.py:421
  135.8 0.6 broadcast_in_dim.13
  136.4 3.4 %all-to-all-start.1 = ((f32[8,24,128]{2,1,0:T(8,128)}), f32[8,24,128]{2,1,0:T(8,128)S(1)}, u32[]{:S(2)}, u32[]{:S(2)}) async-start(f32[8,24,128]{2,1,0:T(8,128)} %broadcast_in_dim.13), calls=%async_computation.1 | async-start | bytes 196608 | tf_op jit(solution)/shard_map/all_to_all | solution.py:421
  139.8 9.2 %all-to-all-done.1 = f32[8,24,128]{2,1,0:T(8,128)S(1)} async-done(((f32[8,24,128]{2,1,0:T(8,128)}), f32[8,24,128]{2,1,0:T(8,128)S(1)}, u32[]{:S(2)}, u32[]{:S(2)}) %all-to-all-start.1) | async-done | bytes 98336 | tf_op jit(solution)/shard_map/all_to_all | solution.py:421
  149.1 0.6 broadcast_in_dim.15
  149.7 3.4 %all-to-all-start.3 = ((f32[8,24,128]{2,1,0:T(8,128)}), f32[8,24,128]{2,1,0:T(8,128)S(1)}, u32[]{:S(2)}, u32[]{:S(2)}) async-start(f32[8,24,128]{2,1,0:T(8,128)} %broadcast_in_dim.15), calls=%async_computation.3 | async-start | bytes 196608 | tf_op jit(solution)/shard_map/all_to_all | solution.py:421
  153.1 0.6 reduce_sum.55.gram.first
  153.7 3.3 %inverse_kernel.1.inverse = f32[24,128]{1,0:T(8,128)} custom-call(f32[24,128]{1,0:T(8,128)} %reduce_sum.55.gram.first), custom_call_target="tpu_custom_call" | custom-call | tf_op jit(solution)/shard_map/inverse_kernel/pallas_call | solution.py:407
  157.0 4.7 %all-to-all-done.3 = f32[8,24,128]{2,1,0:T(8,128)S(1)} async-done(((f32[8,24,128]{2,1,0:T(8,128)}), f32[8,24,128]{2,1,0:T(8,128)S(1)}, u32[]{:S(2)}, u32[]{:S(2)}) %all-to-all-start.3) | async-done | bytes 98336 | tf_op jit(solution)/shard_map/all_to_all | solution.py:421
  161.7 0.6 reduce_sum.57.second
  162.3 0.0 collective-permute-done.7.after
  162.3 0.0 collective-permute-done.6.before
  162.3 1.3 copy-done.2
  163.6 7.6 %krylov_kernel.1 = (f32[48,96,128]{2,1,0:T(8,128)}, f32[48,32,128]{2,1,0:T(8,128)}, f32[2,96,128]{2,1,0:T(8,128)}, f32[16,128]{1,0:T(8,128)}) custom-call(f32[24,128]{1,0:T(8,128)} %reduce_sum.55.gram.first, f32[24,128]{1,0:T(8,128)} %inverse_kernel.1.inverse, f32[24,128]{1,0:T(8,128)} %reduce_sum.57.second, f32[48,48,128]{2,1,0:T(8,128)} %apply_kernel.1.f, ...), custom_call_target="tpu_custom_call" | custom-call | tf_op jit(solution)/shard_map/krylov_kernel/pallas_call | solution.py:407
  171.3 1.9 collective-permute-start.9
  173.2 2.4 %collective-permute-start.8 = (f32[48,32,128]{2,1,0:T(8,128)}, f32[48,32,128]{2,1,0:T(8,128)S(1)}, u32[]{:S(2)}, u32[]{:S(2)}) collective-permute-start(f32[48,32,128]{2,1,0:T(8,128)} %get-tuple-element.19.last), channel_id=1, source_target_pairs={{0,1},{1,2},{2,3},{3,4},{4,5},{5,6},{6,7},{7,8},{8,9},{9,10},{10,1... | collective-permute-start | bytes 2359304 | tf_op jit(solution)/shard_map/ppermute | solution.py:428
  175.6 7.4 %collective-permute-done.9.last_after = f32[48,32,128]{2,1,0:T(8,128)S(1)} collective-permute-done((f32[48,32,128]{2,1,0:T(8,128)}, f32[48,32,128]{2,1,0:T(8,128)S(1)}, u32[]{:S(2)}, u32[]{:S(2)}) %collective-permute-start.9) | collective-permute-done | bytes 786464 | tf_op jit(solution)/shard_map/ppermute | solution.py:429
  183.0 5.8 %collective-permute-done.8.last_before = f32[48,32,128]{2,1,0:T(8,128)S(1)} collective-permute-done((f32[48,32,128]{2,1,0:T(8,128)}, f32[48,32,128]{2,1,0:T(8,128)S(1)}, u32[]{:S(2)}, u32[]{:S(2)}) %collective-permute-start.8) | collective-permute-done | bytes 786464 | tf_op jit(solution)/shard_map/ppermute | solution.py:428
  188.8 0.0 copy-done.7
  188.8 0.9 copy-done.9
  189.7 5.5 %moment_kernel.1 = (f32[48,32,128]{2,1,0:T(8,128)}, f32[24,128]{1,0:T(8,128)}) custom-call(f32[48,96,128]{2,1,0:T(8,128)} %get-tuple-element.18.q, f32[48,32,128]{2,1,0:T(8,128)} %get-tuple-element.19.last, f32[48,32,128]{2,1,0:T(8,128)} %copy-done.9, f32[48,32,128]{2,1,0:T(8,128)} %copy-done.7, f32[48,80,128]{2,1,0:T(8,128)} %get-tuple-element.17.fields, ...), custom_call_target="tpu_custom_call" | custom-call | tf_op jit(solution)/shard_map/moment_kernel/pallas_call | solution.py:407
  195.2 0.7 broadcast_in_dim.16
  195.9 15.0 %all_to_all.31 = f32[32,24,128]{2,1,0:T(8,128)S(1)} all-to-all(f32[32,24,128]{2,1,0:T(8,128)S(1)} %broadcast_in_dim.16), channel_id=1, replica_groups=mesh['grid_0'=4,'grid_1'=4,'grid_2'=8,'grid_3'=2] {'grid_0','grid_1','gr..., dimensions={0} | all-to-all | bytes 786432 | tf_op jit(solution)/shard_map/all_to_all | solution.py:421
  211.0 11.7 %all_to_all.32 = f32[8,24,128]{2,1,0:T(8,128)S(1)} all-to-all(f32[8,24,128]{2,1,0:T(8,128)S(1)} %broadcast_in_dim.17), channel_id=1, replica_groups=mesh['grid_0'=4,'grid_1'=4,'grid_2'=8,'grid_3'=2] {'grid_2'}, dimensions={0} | all-to-all | bytes 196608 | tf_op jit(solution)/shard_map/all_to_all | solution.py:421
  222.7 0.6 reduce_sum.59.moments
  223.3 10.1 %finish_kernel.1 = (f32[48,32,128]{2,1,0:T(8,128)}, f32[48,32,128]{2,1,0:T(8,128)}) custom-call(f32[8]{0:T(128)} %table.3, s32[2]{0:T(128)} %index.3, f32[24,128]{1,0:T(8,128)} %reduce_sum.59.moments, f32[2,96,128]{2,1,0:T(8,128)} %get-tuple-element.22.coef, f32[16,128]{1,0:T(8,128)} %get-tuple-element.20.shift, f32[48,48,128]{2,1,0:T(8,128)} %bitcast.18, ...), custom_call_target="tpu_custom_call" | custom-call | tf_op jit(solution)/shard_map/finish_kernel/pallas_call | solution.py:407
  233.4 2.5 %copy.13 = f32[32,1,48,128]{3,2,1,0:T(8,128)} copy(f32[32,1,48,128]{3,0,2,1:T(8,128)} %bitcast.24) | data formatting | bytes 1572864
  236.0 1.3 copy.14
  (18 shorter events, 0.2 us)
Async XLA Ops:
  2.3 26.7 %copy-start = (f32[2,24,1,48,128]{4,1,0,3,2:T(8,128)}, f32[2,24,1,48,128]{4,1,0,3,2:T(8,128)S(1)}, u32[]{:S(2)}) copy-start(f32[2,24,1,48,128]{4,1,0,3,2:T(8,128)S(1)} %copy.11) | copy-start | bytes 3538948
  2.3 20.8 %collective-permute-start.1 = (f32[48,48,128]{2,1,0:T(8,128)S(1)}, f32[48,48,128]{2,1,0:T(8,128)S(1)}, u32[]{:S(2)}, u32[]{:S(2)}) collective-permute-start(f32[48,48,128]{2,1,0:T(8,128)S(1)} %bitcast.15), channel_id=1, source_target_pairs={{1,0},{2,1},{3,2},{4,3},{5,4},{6,5},{7,6},{8,7},{9,8},{10,9},{11,1... | collective-permute-start | bytes 3538952 | tf_op jit(solution)/shard_map/ppermute | solution.py:429
  9.4 19.6 %collective-permute-start = (f32[48,48,128]{2,1,0:T(8,128)S(1)}, f32[48,48,128]{2,1,0:T(8,128)S(1)}, u32[]{:S(2)}, u32[]{:S(2)}) collective-permute-start(f32[48,48,128]{2,1,0:T(8,128)S(1)} %bitcast.16), channel_id=1, source_target_pairs={{0,1},{1,2},{2,3},{3,4},{4,5},{5,6},{6,7},{7,8},{8,9},{9,10},{10,1... | collective-permute-start | bytes 3538952 | tf_op jit(solution)/shard_map/ppermute | solution.py:428
  23.1 5.9 %copy-start.5 = (f32[48,48,128]{2,1,0:T(8,128)}, f32[48,48,128]{2,1,0:T(8,128)S(1)}, u32[]{:S(2)}) copy-start(f32[48,48,128]{2,1,0:T(8,128)S(1)} %collective-permute-done.1.u_after) | copy-start | bytes 3538948
  29.0 1.1 copy-start.6
  30.1 8.1 %copy-start.11 = (f32[32,1,48,128]{3,2,1,0:T(8,128)S(1)}, f32[32,1,48,128]{3,2,1,0:T(8,128)}, u32[]{:S(2)}) copy-start(f32[32,1,48,128]{3,2,1,0:T(8,128)} %param.5) | copy-start | bytes 2359300
  33.9 34.9 %collective-permute-start.5 = (f32[48,48,128]{2,1,0:T(8,128)}, f32[48,48,128]{2,1,0:T(8,128)S(1)}, u32[]{:S(2)}, u32[]{:S(2)}) collective-permute-start(f32[48,48,128]{2,1,0:T(8,128)} %apply_kernel.1.f), channel_id=1, source_target_pairs={{1,0},{2,1},{3,2},{4,3},{5,4},{6,5},{7,6},{8,7},{9,8},{10,9},{11,1... | collective-permute-start | bytes 3538952 | tf_op jit(solution)/shard_map/ppermute | solution.py:429
  35.8 33.0 %collective-permute-start.4 = (f32[48,48,128]{2,1,0:T(8,128)}, f32[48,48,128]{2,1,0:T(8,128)S(1)}, u32[]{:S(2)}, u32[]{:S(2)}) collective-permute-start(f32[48,48,128]{2,1,0:T(8,128)} %apply_kernel.1.f), channel_id=1, source_target_pairs={{0,1},{1,2},{2,3},{3,4},{4,5},{5,6},{6,7},{7,8},{8,9},{9,10},{10,1... | collective-permute-start | bytes 3538952 | tf_op jit(solution)/shard_map/ppermute | solution.py:428
  38.5 25.6 %copy-start.1 = (f32[32,1,48,128]{3,0,2,1:T(8,128)}, f32[32,1,48,128]{3,0,2,1:T(8,128)S(1)}, u32[]{:S(2)}) copy-start(f32[32,1,48,128]{3,0,2,1:T(8,128)S(1)} %copy.16) | copy-start | bytes 2359300
  38.5 19.6 %collective-permute-start.3 = (f32[48,32,128]{2,1,0:T(8,128)S(1)}, f32[48,32,128]{2,1,0:T(8,128)S(1)}, u32[]{:S(2)}, u32[]{:S(2)}) collective-permute-start(f32[48,32,128]{2,1,0:T(8,128)S(1)} %bitcast.19), channel_id=1, source_target_pairs={{1,0},{2,1},{3,2},{4,3},{5,4},{6,5},{7,6},{8,7},{9,8},{10,9},{11,1... | collective-permute-start | bytes 2359304 | tf_op jit(solution)/shard_map/ppermute | solution.py:429
  43.8 20.3 %collective-permute-start.2 = (f32[48,32,128]{2,1,0:T(8,128)S(1)}, f32[48,32,128]{2,1,0:T(8,128)S(1)}, u32[]{:S(2)}, u32[]{:S(2)}) collective-permute-start(f32[48,32,128]{2,1,0:T(8,128)S(1)} %bitcast.20), channel_id=1, source_target_pairs={{0,1},{1,2},{2,3},{3,4},{4,5},{5,6},{6,7},{7,8},{8,9},{9,10},{10,1... | collective-permute-start | bytes 2359304 | tf_op jit(solution)/shard_map/ppermute | solution.py:428
  58.1 5.9 %copy-start.8 = (f32[48,32,128]{2,1,0:T(8,128)}, f32[48,32,128]{2,1,0:T(8,128)S(1)}, u32[]{:S(2)}) copy-start(f32[48,32,128]{2,1,0:T(8,128)S(1)} %collective-permute-done.3.b_after) | copy-start | bytes 2359300
  64.1 0.9 copy-start.10
  68.8 1.0 copy-start.3
  68.8 1.4 copy-start.4
  70.2 9.1 %copy-start.13 = (f32[24,128]{1,0:T(8,128)S(1)}, f32[24,128]{1,0:T(8,128)}, u32[]{:S(2)}) copy-start(f32[24,128]{1,0:T(8,128)} %get-tuple-element.14) | copy-start | bytes 36868
  74.9 45.6 %copy-start.14 = (f32[24,128]{1,0:T(8,128)S(1)}, f32[24,128]{1,0:T(8,128)}, u32[]{:S(2)}) copy-start(f32[24,128]{1,0:T(8,128)} %get-tuple-element.16) | copy-start | bytes 36868
  74.9 87.5 %collective-permute-start.7 = (f32[48,80,128]{2,1,0:T(8,128)}, f32[48,80,128]{2,1,0:T(8,128)S(1)}, u32[]{:S(2)}, u32[]{:S(2)}) collective-permute-start(f32[48,80,128]{2,1,0:T(8,128)} %get-tuple-element.17.fields), channel_id=1, source_target_pairs={{1,0},{2,1},{3,2},{4,3},{5,4},{6,5},{7,6},{8,7},{9,8},{10,9},{11,1... | collective-permute-start | bytes 5898248 | tf_op jit(solution)/shard_map/ppermute | solution.py:429
  76.9 85.4 %collective-permute-start.6 = (f32[48,80,128]{2,1,0:T(8,128)}, f32[48,80,128]{2,1,0:T(8,128)}, u32[]{:S(2)}, u32[]{:S(2)}) collective-permute-start(f32[48,80,128]{2,1,0:T(8,128)} %get-tuple-element.17.fields), channel_id=1, source_target_pairs={{0,1},{1,2},{2,3},{3,4},{4,5},{5,6},{6,7},{7,8},{8,9},{9,10},{10,1... | collective-permute-start | bytes 5898248 | tf_op jit(solution)/shard_map/ppermute | solution.py:428
  121.2 14.6 %all-to-all-start.2 = ((f32[32,24,128]{2,1,0:T(8,128)}), f32[32,24,128]{2,1,0:T(8,128)S(1)}, u32[]{:S(2)}, u32[]{:S(2)}) async-start(f32[32,24,128]{2,1,0:T(8,128)} %broadcast_in_dim.14), calls=%async_computation.2 | async-start | bytes 786432 | tf_op jit(solution)/shard_map/all_to_all | solution.py:421
  136.4 12.6 %all-to-all-start.1 = ((f32[8,24,128]{2,1,0:T(8,128)}), f32[8,24,128]{2,1,0:T(8,128)S(1)}, u32[]{:S(2)}, u32[]{:S(2)}) async-start(f32[8,24,128]{2,1,0:T(8,128)} %broadcast_in_dim.13), calls=%async_computation.1 | async-start | bytes 196608 | tf_op jit(solution)/shard_map/all_to_all | solution.py:421
  149.7 12.0 %all-to-all-start.3 = ((f32[8,24,128]{2,1,0:T(8,128)}), f32[8,24,128]{2,1,0:T(8,128)S(1)}, u32[]{:S(2)}, u32[]{:S(2)}) async-start(f32[8,24,128]{2,1,0:T(8,128)} %broadcast_in_dim.15), calls=%async_computation.3 | async-start | bytes 196608 | tf_op jit(solution)/shard_map/all_to_all | solution.py:421
  162.3 1.3 copy-start.2
  171.3 11.7 %collective-permute-start.9 = (f32[48,32,128]{2,1,0:T(8,128)}, f32[48,32,128]{2,1,0:T(8,128)S(1)}, u32[]{:S(2)}, u32[]{:S(2)}) collective-permute-start(f32[48,32,128]{2,1,0:T(8,128)} %get-tuple-element.19.last), channel_id=1, source_target_pairs={{1,0},{2,1},{3,2},{4,3},{5,4},{6,5},{7,6},{8,7},{9,8},{10,9},{11,1... | collective-permute-start | bytes 2359304 | tf_op jit(solution)/shard_map/ppermute | solution.py:429
  173.2 15.6 %collective-permute-start.8 = (f32[48,32,128]{2,1,0:T(8,128)}, f32[48,32,128]{2,1,0:T(8,128)S(1)}, u32[]{:S(2)}, u32[]{:S(2)}) collective-permute-start(f32[48,32,128]{2,1,0:T(8,128)} %get-tuple-element.19.last), channel_id=1, source_target_pairs={{0,1},{1,2},{2,3},{3,4},{4,5},{5,6},{6,7},{7,8},{8,9},{9,10},{10,1... | collective-permute-start | bytes 2359304 | tf_op jit(solution)/shard_map/ppermute | solution.py:428
  183.0 5.8 %copy-start.7 = (f32[48,32,128]{2,1,0:T(8,128)}, f32[48,32,128]{2,1,0:T(8,128)S(1)}, u32[]{:S(2)}) copy-start(f32[48,32,128]{2,1,0:T(8,128)S(1)} %collective-permute-done.9.last_after) | copy-start | bytes 2359300
  188.8 0.9 copy-start.9
  233.4 2.5 %copy-start.12 = (f32[48,32,128]{2,1,0:T(8,128)S(1)}, f32[48,32,128]{2,1,0:T(8,128)}, u32[]{:S(2)}) copy-start(f32[48,32,128]{2,1,0:T(8,128)} %get-tuple-element.25) | copy-start | bytes 2359300
where the time goes:
time: 240 us; the launch traced here: 237 us
  waiting for transfers between devices  71.9 us (30%)
  blocking collectives  67.7 us (28%)
  starting transfers between devices  41.8 us (17%)
  Pallas kernels  38.9 us (16%)
  local copies, waits for them, and re-layouts  14.2 us (6%)
    all_to_all x3, blocking collectives, everyone(): values = jnp.sum(lax.all_to_all(spread, axes, 0, 0, tiled=True), axis=0)  67.7 us
    pallas_call x7, Pallas kernels, call(): pl.pallas_call(kernel, out_shape=out, in_specs=[SMEM] * scalars + [VMEM]...  38.9 us
    ppermute x5, waiting for transfers between devices, beside(): after = lax.ppermute(values, GRID, [(i + 1, i) for i in range(ends)])  31.6 us
    all_to_all x3, waiting for transfers between devices, everyone(): values = jnp.sum(lax.all_to_all(spread, axes, 0, 0, tiled=True), axis=0)  22.7 us
    ppermute x5, starting transfers between devices, beside(): after = lax.ppermute(values, GRID, [(i + 1, i) for i in range(ends)])  18.2 us
    ppermute x5, waiting for transfers between devices, beside(): before = lax.ppermute(values, GRID, [(i, i + 1) for i in range(ends)])  17.7 us
    all_to_all x3, starting transfers between devices, everyone(): values = jnp.sum(lax.all_to_all(spread, axes, 0, 0, tiled=True), axis=0)  12.5 us
    unnamed x34, local copies, waits for them, and re-layouts  11.3 us
  transfers between devices with their start and end apart: 13, of which 9 were waited for; matrix products, arithmetic and copies ran while one was open for 2% of the time, Pallas kernels for 3%

commit v1 on v0

--- a/solution.py
+++ b/solution.py
@@ -7,7 +7,8 @@
 from jax.sharding import PartitionSpec as P
 
 GRID = ("grid_0", "grid_1", "grid_2", "grid_3")
-STAGES = (("grid_0", "grid_1", "grid_3"), ("grid_2",))
+CORES = "grid_3"
+STAGES = (("grid_0", "grid_1"), "grid_2")
 NX = 48
 NY = 128
 K = 24
@@ -16,7 +17,7 @@
 HIGH = lax.Precision.HIGHEST
 F32 = jnp.float32
 BF16 = jnp.bfloat16
-PARAMS = pltpu.CompilerParams(vmem_limit_bytes=56 << 20)
+PARAMS = pltpu.CompilerParams(vmem_limit_bytes=24 << 20)
 VMEM = pl.BlockSpec(memory_space=pltpu.VMEM)
 SMEM = pl.BlockSpec(memory_space=pltpu.SMEM)
 
@@ -80,13 +81,30 @@
 def eliminate(system, count):
     lane = iota((1, 128), 1)
     row = iota(system.shape, 0)
-    for k in range(count):
-        pivot_row = system[k : k + 1]
-        pivot = jnp.where(lane < 64, pivot_row[:, k : k + 1], pivot_row[:, 64 + k : 65 + k])
-        scaled = pivot_row / pivot
-        column = jnp.where(lane < 64, system[:, k : k + 1], system[:, 64 + k : 65 + k])
-        system = jnp.where(row == k, scaled, system - column * scaled)
+
+    def column(k):
+        return jnp.where(lane < 64, system[:, k : k + 1], system[:, 64 + k : 65 + k])
+
+    for k in range(0, count, 2):
+        one = system[k : k + 1]
+        two = system[k + 1 : k + 2]
+        left = column(k)
+        right = column(k + 1)
+        a, b = left[k : k + 1], right[k : k + 1]
+        c, d = left[k + 1 : k + 2], right[k + 1 : k + 2]
+        inverse = 1.0 / (a * d - b * c)
+        new_one = (d * inverse) * one - (b * inverse) * two
+        new_two = (a * inverse) * two - (c * inverse) * one
+        changed = system - left * new_one - right * new_two
+        system = jnp.where(row == k, new_one, jnp.where(row == k + 1, new_two, changed))
     return system
+
+
+def over_copies(parts):
+    total = parts[0]
+    for i in range(1, parts.shape[0]):
+        total = total + parts[i]
+    return total
 
 
 def apply_kernel(table, index, u, u_before, u_after, medium, f_out):
@@ -138,15 +156,7 @@
     gram_out[...] = packed
 
 
-def inverse_kernel(gram, out):
-    lane = iota((K, 128), 1)
-    row = iota((K, 128), 0)
-    place = lane & 63
-    unit = jnp.where(place == row + K, 1.0, 0.0)
-    out[...] = eliminate(jnp.where(place < K, gram[...], unit), K)
-
-
-def second_gram_kernel(f, f_before, f_after, b1, medium, fields_out, gram_out):
+def second_gram_kernel(f, f_before, f_after, b1, first, medium, fields_out, gram_out):
     total = jnp.zeros((2 * K, 128), F32)
 
     def next_field(x):
@@ -173,15 +183,22 @@
             ]
         total = total + row_products(f1_pair, jnp.concatenate(right, axis=0))
     lane = iota((K, 128), 1)
-    gram_out[...] = jnp.where(lane < 64, total[:K], total[K:])
+    gram_out[:K] = first[...]
+    gram_out[K:] = jnp.where(lane < 64, total[:K], total[K:])
 
 
 def krylov_kernel(
-    first, inverse, second, f, b, fields, before, after, medium, q_out, last_out, coef_out, shift_out
+    grams, f, b, fields, before, after, medium, q_out, last_out, coef_out, shift_out
 ):
-    first_t = transposed(first[...])
-    second_t = transposed(second[...])
-    inverse_t = transposed(inverse[...])
+    gram = over_copies(grams)
+    first = gram[:K]
+    lane = iota((K, 128), 1)
+    row = iota((K, 128), 0)
+    place = lane & 63
+    unit = jnp.where(place == row + K, 1.0, 0.0)
+    inverse_t = transposed(eliminate(jnp.where(place < K, first, unit), K))
+    first_t = transposed(first)
+    second_t = transposed(gram[K:])
     coeffs = []
     thetas = []
     for g in range(2):
@@ -243,52 +260,53 @@
                 last_out[x + i, brows] = part[2 * B :]
 
 
-def moment_kernel(q, last, last_before, last_after, fields, medium, shift, t_out, gram_out):
-    zeros = jnp.zeros((40, 2 * NY), F32)
-    grams = []
-    for g in range(2):
+def basis_gram_kernel(q, fields, gram_out):
+    for g in range(2):
+        qrows = slice(48 * g, 48 * g + 48)
+        frows = slice(40 * g, 40 * g + K)
+        total = jnp.zeros((48, 128), F32)
+        none = jnp.zeros((B, 2 * NY), F32)
+        pad = jnp.zeros((40, 2 * NY), F32)
+        for x in range(0, NX, 2):
+            left = jnp.concatenate([q[x, qrows], q[x + 1, qrows]], axis=1)
+            f1 = jnp.concatenate([fields[x, frows], fields[x + 1, frows]], axis=1)
+            total = total + row_products(left, jnp.concatenate([left, none, f1, pad], axis=0))
+        gram_out[g] = total
+
+
+def moment_kernel(last, last_before, last_after, basis_gram, medium, shift, t_out, gram_out):
+    def next_field(x, g):
         theta = shift[8 * g : 8 * g + 1, :]
         brows = slice(B * g, B * g + B)
-
-        def next_field(x):
-            out = (medium[x : x + 1, :] - SHIFT - theta) * last[x, brows] - neighbours(
-                x, lambda i: last[i, brows], last_before[x, brows], last_after[x, brows]
-            )
-            t_out[x, brows] = out
-            return out
-
-        qrows = slice(48 * g, 48 * g + 48)
-        frows = slice(40 * g, 40 * g + K)
-        total = jnp.zeros((64, 128), F32)
-        for x in range(0, NX, 2):
-            left = jnp.concatenate(
-                [
-                    jnp.concatenate([q[x, qrows], q[x + 1, qrows]], axis=1),
-                    jnp.concatenate([next_field(x), next_field(x + 1)], axis=1),
-                ],
-                axis=0,
-            )
-            f1 = jnp.concatenate([fields[x, frows], fields[x + 1, frows]], axis=1)
-            total = total + row_products(left, jnp.concatenate([left, f1, zeros], axis=0))
-        grams.append(total)
+        out = (medium[x : x + 1, :] - SHIFT - theta) * last[x, brows] - neighbours(
+            x, lambda i: last[i, brows], last_before[x, brows], last_after[x, brows]
+        )
+        t_out[x, brows] = out
+        return out
+
+    total = jnp.zeros((2 * B, 128), F32)
+    pad = jnp.zeros((64, 2 * NY), F32)
+    for x in range(0, NX, 2):
+        left = []
+        right = []
+        for g in range(2):
+            brows = slice(B * g, B * g + B)
+            made = jnp.concatenate([next_field(x, g), next_field(x + 1, g)], axis=1)
+            left.append(made)
+            right.append(jnp.concatenate([last[x, brows], last[x + 1, brows]], axis=1))
+            right.append(made)
+        total = total + row_products(
+            jnp.concatenate(left, axis=0), jnp.concatenate(right + [pad], axis=0)
+        )
+    grams = [basis_gram[0], basis_gram[1]]
+    ends = [pltpu.roll(total[:B], 80, 1), pltpu.roll(total[B:], 48, 1)]
     lane = iota((B, 128), 1)
     row = iota((B, 128), 0)
     column = lane & 15
     strips = []
-    for gram in grams:
-        strips.append(
-            jnp.where(
-                lane < 32,
-                gram[:16],
-                jnp.where(
-                    lane < 64,
-                    pltpu.roll(gram[16:32], 16, 1),
-                    jnp.where(
-                        lane < 96, pltpu.roll(gram[32:48], 32, 1), pltpu.roll(gram[48:64], 48, 1)
-                    ),
-                ),
-            )
-        )
+    for gram, end in zip(grams, ends):
+        middle = jnp.where(lane < 64, pltpu.roll(gram[16:32], 16, 1), pltpu.roll(gram[32:48], 32, 1))
+        strips.append(jnp.where(lane < 32, gram[:16], jnp.where(lane < 80, middle, end)))
     packed = jnp.where(row <= column, strips[0], strips[1])
     packed = jnp.where(lane < 112, packed, 0.0)
     on_diagonal = jnp.where((row == column) & (lane < 112), strips[1], 0.0)
@@ -308,7 +326,8 @@
 
 
 def finish_kernel(table, index, moments, coef, shift, u, f, q, t, solution_out, residue_out):
-    packed = moments[:B]
+    summed = over_copies(moments)
+    packed = summed[:B]
     turned = transposed(packed)
     lane = iota((B, 128), 1)
     row = iota((B, 128), 0)
@@ -334,7 +353,7 @@
         shifts.append(c)
         at = 48 * g
         f1q2 = jnp.concatenate(
-            [moments[B:, at : at + K], moments[B:, at + K : at + 2 * K]], axis=0
+            [summed[B:, at : at + K], summed[B:, at + K : at + 2 * K]], axis=0
         )
         z3 = small(f1q2, coef[g, 72 : 72 + K, :K])
         thirds.append(z3)
@@ -397,37 +416,43 @@
             )
             for i in range(2):
                 part = made[:, NY * i : NY * i + NY]
-                solution_out[x + i, brows] = part[:B]
-                residue_out[x + i, brows] = part[B:] + q[x + i, 48 * g : 48 * g + B]
-
-
-def call(kernel, shapes, scalars, *arrays):
-    out = [jax.ShapeDtypeStruct(s, F32) for s in shapes]
-    count = len(arrays) - scalars
+                solution_out[brows, x + i, :] = part[:B]
+                residue_out[brows, x + i, :] = part[B:] + q[x + i, 48 * g : 48 * g + B]
+
+
+def call(kernel, shapes, scalars, *arrays, final=False):
+    if final:
+        out = [jax.ShapeDtypeStruct(s, F32) for s in shapes]
+    else:
+        out = [pltpu.VMEM(s, F32) for s in shapes]
+    here = [pltpu.with_memory_space_constraint(a, pltpu.VMEM) for a in arrays[scalars:]]
     return pl.pallas_call(
         kernel,
         out_shape=out,
-        in_specs=[SMEM] * scalars + [VMEM] * count,
+        in_specs=[SMEM] * scalars + [VMEM] * len(here),
         out_specs=[VMEM] * len(out),
         compiler_params=PARAMS,
         name=kernel.__name__,
-    )(*arrays)
+    )(*arrays[:scalars], *here)
 
 
 def everyone(values):
-    for axes in STAGES:
+    values = values + lax.ppermute(values, CORES, [(0, 1), (1, 0)])
+    for number, axes in enumerate(STAGES):
+        if number:
+            values = jnp.sum(values, axis=0)
         size = lax.axis_size(axes)
         spread = jnp.broadcast_to(values[None], (size, *values.shape))
-        values = jnp.sum(lax.all_to_all(spread, axes, 0, 0, tiled=True), axis=0)
+        values = lax.all_to_all(spread, axes, 0, 0, tiled=True)
     return values
 
 
 def beside(values):
     count = lax.axis_size(GRID)
-    ends = count - 1
-    before = lax.ppermute(values, GRID, [(i, i + 1) for i in range(ends)])
-    after = lax.ppermute(values, GRID, [(i + 1, i) for i in range(ends)])
-    return before, after
+    edges = [(i, i + 1) for i in range(1, count - 1, 2)]
+    across = lax.ppermute(values, GRID, edges + [(j, i) for i, j in edges])
+    sibling = lax.ppermute(values, CORES, [(0, 1), (1, 0)])
+    return across, sibling
 
 
 def on_device(right_sides, recycle, medium, shift_table, shift_index):
@@ -437,24 +462,18 @@
     u_sides = beside(u)
     b_sides = beside(b)
     (f,) = call(apply_kernel, [(NX, 2 * K, NY)], 2, shift_table, shift_index, u, *u_sides, med)
+    f, b_sides = lax.optimization_barrier((f, b_sides))
     f_sides = beside(f)
-    b1, gram = call(
-        first_gram_kernel, [(NX, 2 * B, NY), (K, 128)], 0, f, b, *b_sides, med
-    )
-    first = everyone(gram)
-    (inverse,) = call(inverse_kernel, [(K, 128)], 0, first)
+    b1, first = call(first_gram_kernel, [(NX, 2 * B, NY), (K, 128)], 0, f, b, *b_sides, med)
     fields, gram = call(
-        second_gram_kernel, [(NX, 80, NY), (K, 128)], 0, f, *f_sides, b1, med
+        second_gram_kernel, [(NX, 80, NY), (2 * K, 128)], 0, f, *f_sides, b1, first, med
     )
     field_sides = beside(fields)
-    second = everyone(gram)
     q, last, coef, shift = call(
         krylov_kernel,
         [(NX, 96, NY), (NX, 2 * B, NY), (2, 96, 128), (16, 128)],
         0,
-        first,
-        inverse,
-        second,
+        everyone(gram),
         f,
         b,
         fields,
@@ -462,37 +481,26 @@
         med,
     )
     last_sides = beside(last)
+    (basis_gram,) = call(basis_gram_kernel, [(2, 48, 128)], 0, q, fields)
     t, gram = call(
-        moment_kernel,
-        [(NX, 2 * B, NY), (K, 128)],
-        0,
-        q,
-        last,
-        *last_sides,
-        fields,
-        med,
-        shift,
-    )
-    moments = everyone(gram)
+        moment_kernel, [(NX, 2 * B, NY), (K, 128)], 0, last, *last_sides, basis_gram, med, shift
+    )
     solution, residue = call(
         finish_kernel,
-        [(NX, 2 * B, NY)] * 2,
+        [(2 * B, NX, NY)] * 2,
         2,
         shift_table,
         shift_index,
-        moments,
+        everyone(gram),
         coef,
         shift,
         u,
         f,
         q,
         t,
-    )
-    shape = right_sides.shape
-    return (
-        jnp.transpose(solution, (1, 0, 2)).reshape(shape),
-        jnp.transpose(residue, (1, 0, 2)).reshape(shape),
-    )
+        final=True,
+    )
+    return solution.reshape(right_sides.shape), residue.reshape(right_sides.shape)
 
 
 def solution(mesh):

time: 240 us -> 170 us (0.71)
  waiting for transfers between devices: 71.9 us -> 42.4 us
  starting transfers between devices: 41.8 us -> 24.8 us
  Pallas kernels: 38.9 us -> 23.5 us
  local copies, waits for them, and re-layouts: 14.2 us -> 3.74 us
  blocking collectives: 67.7 us -> 73.1 us
    all_to_all x3 -> x0, waiting for transfers between devices: 22.7 us -> none  [everyone(): values = jnp.sum(lax.all_to_all(spread, axes, 0, 0, tiled=True), axis=0)]
    pallas_call x7, Pallas kernels: 38.9 us -> 23.5 us  [call(): pl.pallas_call(kernel, out_shape=out, in_specs=[SMEM] * scalars + [VMEM]...]
    all_to_all x3 -> x0, starting transfers between devices: 12.5 us -> none  [everyone(): values = jnp.sum(lax.all_to_all(spread, axes, 0, 0, tiled=True), axis=0)]
    unnamed x34 -> x14, local copies, waits for them, and re-layouts: 11.3 us -> 3.67 us
    ppermute x10 -> x12, waiting for transfers between devices: 49.3 us -> 42.4 us  [the longest x5 40 us: beside(): across = lax.ppermute(values, GRID, edges + [(j, i) for i, j in edges])]
    all_to_all x3 -> x4, blocking collectives: 67.7 us -> 73.1 us  [everyone(): values = lax.all_to_all(spread, axes, 0, 0, tiled=True)]
    ppermute x10 -> x12, starting transfers between devices: 29.3 us -> 24.8 us  [the longest x5 24.3 us: beside(): across = lax.ppermute(values, GRID, edges + [(j, i) for i, j in edges])]
    broadcast_in_dim x6 -> x4, local copies, waits for them, and re-layouts: 2.84 us -> 0.07 us  [everyone(): spread = jnp.broadcast_to(values[None], (size, *values.shape))]
  transfers between devices with their start and end apart: 13 -> 12, of which waited for: 9 -> 6; matrix products, arithmetic and copies ran while one was open for 2% -> 1% of each run, Pallas kernels for 3% -> 4%
where the time goes in v1:
time: 170 us
  blocking collectives  73.1 us (43%)
  waiting for transfers between devices  42.4 us (25%)
  starting transfers between devices  24.8 us (15%)
  Pallas kernels  23.5 us (14%)
  local copies, waits for them, and re-layouts  3.74 us (2%)
    all_to_all x4, blocking collectives, everyone(): values = lax.all_to_all(spread, axes, 0, 0, tiled=True)  73.1 us
    ppermute x5, waiting for transfers between devices, beside(): across = lax.ppermute(values, GRID, edges + [(j, i) for i, j in edges])  40 us
    ppermute x5, starting transfers between devices, beside(): across = lax.ppermute(values, GRID, edges + [(j, i) for i, j in edges])  24.3 us
    pallas_call x7, Pallas kernels, call(): pl.pallas_call(kernel, out_shape=out, in_specs=[SMEM] * scalars + [VMEM]...  23.5 us
    unnamed x14, local copies, waits for them, and re-layouts  3.67 us
  transfers between devices with their start and end apart: 12, of which 6 were waited for; matrix products, arithmetic and copies ran while one was open for 1% of the time, Pallas kernels for 4%

profile of v1, /device:TPU:8, one launch (start us, length us, event | category | flops | bytes accessed | tf_op | source)
XLA Modules:
  0.0 169.5 jit_solution(5337811451456370106)
XLA Ops:
  0.6 0.0 copy-start.5
  0.6 1.7 %copy.11 = f32[2,24,1,48,128]{4,1,0,3,2:T(8,128)S(1)} copy(f32[2,24,1,48,128]{4,3,2,1,0:T(8,128)} %param.6) | data formatting | bytes 2359296 | tf_op args[1]
  2.4 0.0 copy-start.2
  2.4 0.0 copy-start.3
  2.4 0.0 copy-start.4
  2.4 0.1 collective-permute-start.1
  2.5 7.7 %collective-permute-start = (f32[48,48,128]{2,1,0:T(8,128)S(1)}, f32[48,48,128]{2,1,0:T(8,128)S(1)}, u32[]{:S(2)}, u32[]{:S(2)}) collective-permute-start(f32[48,48,128]{2,1,0:T(8,128)S(1)} %bitcast.16), channel_id=1, source_target_pairs={{1,2},{3,4},{5,6},{7,8},{9,10},{11,12},{13,14},{15,16},{17,18},{19... | collective-permute-start | bytes 3538952 | tf_op jit(solution)/shard_map/ppermute | solution.py:453
  10.3 0.0 copy-done.5
  10.3 0.3 copy.16
  10.5 0.1 collective-permute-start.3
  10.6 3.0 %collective-permute-start.2 = (f32[48,32,128]{2,1,0:T(8,128)S(1)}, f32[48,32,128]{2,1,0:T(8,128)S(1)}, u32[]{:S(2)}, u32[]{:S(2)}) collective-permute-start(f32[48,32,128]{2,1,0:T(8,128)S(1)} %bitcast.20), channel_id=1, source_target_pairs={{1,2},{3,4},{5,6},{7,8},{9,10},{11,12},{13,14},{15,16},{17,18},{19... | collective-permute-start | bytes 2359304 | tf_op jit(solution)/shard_map/ppermute | solution.py:453
  13.6 0.0 collective-permute-done.1.u_after
  13.6 10.5 %collective-permute-done.u_before = f32[48,48,128]{2,1,0:T(8,128)S(1)} collective-permute-done((f32[48,48,128]{2,1,0:T(8,128)S(1)}, f32[48,48,128]{2,1,0:T(8,128)S(1)}, u32[]{:S(2)}, u32[]{:S(2)}) %collective-permute-start) | collective-permute-done | bytes 1179680 | tf_op jit(solution)/shard_map/ppermute | solution.py:453
  24.1 0.0 copy-done.2
  24.1 0.0 copy-done.3
  24.1 0.0 copy-done.4
  24.1 1.2 apply_kernel.1.f
  25.4 0.0 collective-permute-done.3.b_after
  25.4 7.2 %collective-permute-done.2.b_before = f32[48,32,128]{2,1,0:T(8,128)S(1)} collective-permute-done((f32[48,32,128]{2,1,0:T(8,128)S(1)}, f32[48,32,128]{2,1,0:T(8,128)S(1)}, u32[]{:S(2)}, u32[]{:S(2)}) %collective-permute-start.2) | collective-permute-done | bytes 786464 | tf_op jit(solution)/shard_map/ppermute | solution.py:453
  32.5 0.0 collective-permute-start.5
  32.6 5.7 %collective-permute-start.4 = (f32[48,48,128]{2,1,0:T(8,128)S(1)}, f32[48,48,128]{2,1,0:T(8,128)S(1)}, u32[]{:S(2)}, u32[]{:S(2)}) collective-permute-start(f32[48,48,128]{2,1,0:T(8,128)S(1)} %apply_kernel.1.f), channel_id=1, source_target_pairs={{1,2},{3,4},{5,6},{7,8},{9,10},{11,12},{13,14},{15,16},{17,18},{19... | collective-permute-start | bytes 3538952 | tf_op jit(solution)/shard_map/ppermute | solution.py:453
  38.3 1.4 first_gram_kernel.1
  39.7 0.0 collective-permute-done.5.f_after
  39.7 12.5 %collective-permute-done.4.f_before = f32[48,48,128]{2,1,0:T(8,128)S(1)} collective-permute-done((f32[48,48,128]{2,1,0:T(8,128)S(1)}, f32[48,48,128]{2,1,0:T(8,128)S(1)}, u32[]{:S(2)}, u32[]{:S(2)}) %collective-permute-start.4) | collective-permute-done | bytes 1179680 | tf_op jit(solution)/shard_map/ppermute | solution.py:453
  52.2 2.6 %second_gram_kernel.1 = (f32[48,80,128]{2,1,0:T(8,128)}, f32[48,128]{1,0:T(8,128)S(1)}) custom-call(f32[48,48,128]{2,1,0:T(8,128)S(1)} %apply_kernel.1.f, f32[48,48,128]{2,1,0:T(8,128)S(1)} %collective-permute-done.4.f_before, f32[48,48,128]{2,1,0:T(8,128)S(1)} %collective-permute-done.5.f_after, f32[48,32,128]{2,1,0:T(8,128)S(1)} %get-tuple-element.20.b1, ...), custom_call_target="tpu_custom_call" | custom-call | tf_op jit(solution)/shard_map/second_gram_kernel/pallas_call | solution.py:429
  54.8 0.0 collective-permute-start.8
  54.8 5.7 %collective-permute-start.7 = (f32[48,80,128]{2,1,0:T(8,128)}, f32[48,80,128]{2,1,0:T(8,128)}, u32[]{:S(2)}, u32[]{:S(2)}) collective-permute-start(f32[48,80,128]{2,1,0:T(8,128)} %get-tuple-element.23.fields), channel_id=1, source_target_pairs={{1,2},{3,4},{5,6},{7,8},{9,10},{11,12},{13,14},{15,16},{17,18},{19... | collective-permute-start | bytes 5898248 | tf_op jit(solution)/shard_map/ppermute | solution.py:453
  60.6 0.1 collective-permute-start.6
  60.7 1.2 collective-permute-done.6
  61.9 25.1 %all_to_all.20 = f32[16,48,128]{2,1,0:T(8,128)} all-to-all(f32[16,48,128]{2,1,0:T(8,128)S(1)} %broadcast_in_dim.8), channel_id=1, replica_groups=mesh['grid_0'=4,'grid_1'=4,'grid_2'=8,'grid_3'=2] {'grid_0','grid_1'}, dimensions={0} | all-to-all | bytes 786432 | tf_op jit(solution)/shard_map/all_to_all | solution.py:446
  86.9 1.0 reduce_sum.18
  88.0 22.8 %all_to_all.21.grams = f32[8,48,128]{2,1,0:T(8,128)S(1)} all-to-all(f32[8,48,128]{2,1,0:T(8,128)S(1)} %broadcast_in_dim.9), channel_id=1, replica_groups=mesh['grid_0'=4,'grid_1'=4,'grid_2'=8,'grid_3'=2] {'grid_2'}, dimensions={0} | all-to-all | bytes 393216 | tf_op jit(solution)/shard_map/all_to_all | solution.py:446
  110.7 0.0 collective-permute-done.8.after
  110.7 0.0 collective-permute-done.7.before
  110.7 6.7 %krylov_kernel.1 = (f32[48,96,128]{2,1,0:T(8,128)S(1)}, f32[48,32,128]{2,1,0:T(8,128)S(1)}, f32[2,96,128]{2,1,0:T(8,128)S(1)}, f32[16,128]{1,0:T(8,128)S(1)}) custom-call(f32[8,48,128]{2,1,0:T(8,128)S(1)} %all_to_all.21.grams, f32[48,48,128]{2,1,0:T(8,128)S(1)} %apply_kernel.1.f, f32[48,32,128]{2,1,0:T(8,128)S(1)} %bitcast.22, ...), custom_call_target="tpu_custom_call" | custom-call | tf_op jit(solution)/shard_map/krylov_kernel/pallas_call | solution.py:429
  117.5 0.0 copy-start
  117.5 0.1 collective-permute-start.10
  117.6 2.1 %collective-permute-start.9 = (f32[48,32,128]{2,1,0:T(8,128)S(1)}, f32[48,32,128]{2,1,0:T(8,128)S(1)}, u32[]{:S(2)}, u32[]{:S(2)}) collective-permute-start(f32[48,32,128]{2,1,0:T(8,128)S(1)} %get-tuple-element.24.last), channel_id=1, source_target_pairs={{1,2},{3,4},{5,6},{7,8},{9,10},{11,12},{13,14},{15,16},{17,18},{19... | collective-permute-start | bytes 2359304 | tf_op jit(solution)/shard_map/ppermute | solution.py:453
  119.7 3.3 %basis_gram_kernel.1.basis_gram = f32[2,48,128]{2,1,0:T(8,128)S(1)} custom-call(f32[48,96,128]{2,1,0:T(8,128)S(1)} %get-tuple-element.25.q, f32[48,80,128]{2,1,0:T(8,128)} %get-tuple-element.23.fields), custom_call_target="tpu_custom_call" | custom-call | tf_op jit(solution)/shard_map/basis_gram_kernel/pallas_call | solution.py:429
  123.0 0.0 copy-done
  123.0 0.0 collective-permute-done.10.last_after
  123.1 9.9 %collective-permute-done.9.last_before = f32[48,32,128]{2,1,0:T(8,128)S(1)} collective-permute-done((f32[48,32,128]{2,1,0:T(8,128)S(1)}, f32[48,32,128]{2,1,0:T(8,128)S(1)}, u32[]{:S(2)}, u32[]{:S(2)}) %collective-permute-start.9) | collective-permute-done | bytes 786464 | tf_op jit(solution)/shard_map/ppermute | solution.py:453
  133.0 1.0 moment_kernel.1
  134.0 0.1 collective-permute-start.11
  134.1 1.2 collective-permute-done.11
  135.3 14.1 %all_to_all.22 = f32[16,24,128]{2,1,0:T(8,128)S(1)} all-to-all(f32[16,24,128]{2,1,0:T(8,128)S(1)} %broadcast_in_dim.10), channel_id=1, replica_groups=mesh['grid_0'=4,'grid_1'=4,'grid_2'=8,'grid_3'=2] {'grid_0','grid_1'}, dimensions={0} | all-to-all | bytes 393216 | tf_op jit(solution)/shard_map/all_to_all | solution.py:446
  149.5 11.2 %all_to_all.23.moments = f32[8,24,128]{2,1,0:T(8,128)S(1)} all-to-all(f32[8,24,128]{2,1,0:T(8,128)S(1)} %broadcast_in_dim.11), channel_id=1, replica_groups=mesh['grid_0'=4,'grid_1'=4,'grid_2'=8,'grid_3'=2] {'grid_2'}, dimensions={0} | all-to-all | bytes 196608 | tf_op jit(solution)/shard_map/all_to_all | solution.py:446
  160.7 0.0 copy-start.1
  160.7 1.7 copy-done.1
  162.3 7.2 %finish_kernel.1 = (f32[32,48,128]{2,1,0:T(8,128)}, f32[32,48,128]{2,1,0:T(8,128)}) custom-call(f32[8]{0:T(128)S(1)} %copy-done.3, s32[2]{0:T(128)S(1)} %copy-done.4, f32[8,24,128]{2,1,0:T(8,128)S(1)} %all_to_all.23.moments, f32[2,96,128]{2,1,0:T(8,128)S(1)} %get-tuple-element.28.coef, f32[16,128]{1,0:T(8,128)S(1)} %get-tuple-element.26.shift, ...), custom_call_target="tpu_custom_call" | custom-call | tf_op jit(solution)/shard_map/finish_kernel/pallas_call | solution.py:429
  (7 shorter events, 0.1 us)
Async XLA Ops:
  0.6 9.6 %copy-start.5 = (f32[32,1,48,128]{3,2,1,0:T(8,128)S(1)}, f32[32,1,48,128]{3,2,1,0:T(8,128)}, u32[]{:S(2)}) copy-start(f32[32,1,48,128]{3,2,1,0:T(8,128)} %param.5) | copy-start | bytes 2359300
  2.4 21.8 %copy-start.2 = (f32[1,48,128]{2,1,0:T(8,128)S(1)}, f32[1,48,128]{2,1,0:T(8,128)}, u32[]{:S(2)}) copy-start(f32[1,48,128]{2,1,0:T(8,128)} %param.7) | copy-start | bytes 73732
  2.4 21.8 %copy-start.3 = (f32[8]{0:T(128)S(1)}, f32[8]{0:T(128)}, u32[]{:S(2)}) copy-start(f32[8]{0:T(128)} %table.3) | copy-start | bytes 100
  2.4 21.7 %copy-start.4 = (s32[2]{0:T(128)S(1)}, s32[2]{0:T(128)}, u32[]{:S(2)}) copy-start(s32[2]{0:T(128)} %index.3) | copy-start | bytes 28
  2.4 11.2 %collective-permute-start.1 = (f32[48,48,128]{2,1,0:T(8,128)S(1)}, f32[48,48,128]{2,1,0:T(8,128)S(1)}, u32[]{:S(2)}, u32[]{:S(2)}) collective-permute-start(f32[48,48,128]{2,1,0:T(8,128)S(1)} %bitcast.15), channel_id=1, source_target_pairs={{0,1},{1,0},{2,3},{3,2},{4,5},{5,4},{6,7},{7,6},{8,9},{9,8},{10,11... | collective-permute-start | bytes 3538952 | tf_op jit(solution)/shard_map/ppermute | solution.py:454
  2.5 21.6 %collective-permute-start = (f32[48,48,128]{2,1,0:T(8,128)S(1)}, f32[48,48,128]{2,1,0:T(8,128)S(1)}, u32[]{:S(2)}, u32[]{:S(2)}) collective-permute-start(f32[48,48,128]{2,1,0:T(8,128)S(1)} %bitcast.16), channel_id=1, source_target_pairs={{1,2},{3,4},{5,6},{7,8},{9,10},{11,12},{13,14},{15,16},{17,18},{19... | collective-permute-start | bytes 3538952 | tf_op jit(solution)/shard_map/ppermute | solution.py:453
  10.5 14.9 %collective-permute-start.3 = (f32[48,32,128]{2,1,0:T(8,128)S(1)}, f32[48,32,128]{2,1,0:T(8,128)S(1)}, u32[]{:S(2)}, u32[]{:S(2)}) collective-permute-start(f32[48,32,128]{2,1,0:T(8,128)S(1)} %bitcast.19), channel_id=1, source_target_pairs={{0,1},{1,0},{2,3},{3,2},{4,5},{5,4},{6,7},{7,6},{8,9},{9,8},{10,11... | collective-permute-start | bytes 2359304 | tf_op jit(solution)/shard_map/ppermute | solution.py:454
  10.6 21.9 %collective-permute-start.2 = (f32[48,32,128]{2,1,0:T(8,128)S(1)}, f32[48,32,128]{2,1,0:T(8,128)S(1)}, u32[]{:S(2)}, u32[]{:S(2)}) collective-permute-start(f32[48,32,128]{2,1,0:T(8,128)S(1)} %bitcast.20), channel_id=1, source_target_pairs={{1,2},{3,4},{5,6},{7,8},{9,10},{11,12},{13,14},{15,16},{17,18},{19... | collective-permute-start | bytes 2359304 | tf_op jit(solution)/shard_map/ppermute | solution.py:453
  32.5 7.1 %collective-permute-start.5 = (f32[48,48,128]{2,1,0:T(8,128)S(1)}, f32[48,48,128]{2,1,0:T(8,128)S(1)}, u32[]{:S(2)}, u32[]{:S(2)}) collective-permute-start(f32[48,48,128]{2,1,0:T(8,128)S(1)} %apply_kernel.1.f), channel_id=1, source_target_pairs={{0,1},{1,0},{2,3},{3,2},{4,5},{5,4},{6,7},{7,6},{8,9},{9,8},{10,11... | collective-permute-start | bytes 3538952 | tf_op jit(solution)/shard_map/ppermute | solution.py:454
  32.6 19.6 %collective-permute-start.4 = (f32[48,48,128]{2,1,0:T(8,128)S(1)}, f32[48,48,128]{2,1,0:T(8,128)S(1)}, u32[]{:S(2)}, u32[]{:S(2)}) collective-permute-start(f32[48,48,128]{2,1,0:T(8,128)S(1)} %apply_kernel.1.f), channel_id=1, source_target_pairs={{1,2},{3,4},{5,6},{7,8},{9,10},{11,12},{13,14},{15,16},{17,18},{19... | collective-permute-start | bytes 3538952 | tf_op jit(solution)/shard_map/ppermute | solution.py:453
  54.8 55.9 %collective-permute-start.8 = (f32[48,80,128]{2,1,0:T(8,128)}, f32[48,80,128]{2,1,0:T(8,128)}, u32[]{:S(2)}, u32[]{:S(2)}) collective-permute-start(f32[48,80,128]{2,1,0:T(8,128)} %get-tuple-element.23.fields), channel_id=1, source_target_pairs={{0,1},{1,0},{2,3},{3,2},{4,5},{5,4},{6,7},{7,6},{8,9},{9,8},{10,11... | collective-permute-start | bytes 5898248 | tf_op jit(solution)/shard_map/ppermute | solution.py:454
  54.8 55.9 %collective-permute-start.7 = (f32[48,80,128]{2,1,0:T(8,128)}, f32[48,80,128]{2,1,0:T(8,128)}, u32[]{:S(2)}, u32[]{:S(2)}) collective-permute-start(f32[48,80,128]{2,1,0:T(8,128)} %get-tuple-element.23.fields), channel_id=1, source_target_pairs={{1,2},{3,4},{5,6},{7,8},{9,10},{11,12},{13,14},{15,16},{17,18},{19... | collective-permute-start | bytes 5898248 | tf_op jit(solution)/shard_map/ppermute | solution.py:453
  60.6 1.3 collective-permute-start.6
  117.5 5.6 %copy-start = (f32[48,96,128]{2,1,0:T(8,128)}, f32[48,96,128]{2,1,0:T(8,128)S(1)}, u32[]{:S(2)}) copy-start(f32[48,96,128]{2,1,0:T(8,128)S(1)} %get-tuple-element.25.q) | copy-start | bytes 7077892
  117.5 5.6 %collective-permute-start.10 = (f32[48,32,128]{2,1,0:T(8,128)S(1)}, f32[48,32,128]{2,1,0:T(8,128)S(1)}, u32[]{:S(2)}, u32[]{:S(2)}) collective-permute-start(f32[48,32,128]{2,1,0:T(8,128)S(1)} %get-tuple-element.24.last), channel_id=1, source_target_pairs={{0,1},{1,0},{2,3},{3,2},{4,5},{5,4},{6,7},{7,6},{8,9},{9,8},{10,11... | collective-permute-start | bytes 2359304 | tf_op jit(solution)/shard_map/ppermute | solution.py:454
  117.6 15.4 %collective-permute-start.9 = (f32[48,32,128]{2,1,0:T(8,128)S(1)}, f32[48,32,128]{2,1,0:T(8,128)S(1)}, u32[]{:S(2)}, u32[]{:S(2)}) collective-permute-start(f32[48,32,128]{2,1,0:T(8,128)S(1)} %get-tuple-element.24.last), channel_id=1, source_target_pairs={{1,2},{3,4},{5,6},{7,8},{9,10},{11,12},{13,14},{15,16},{17,18},{19... | collective-permute-start | bytes 2359304 | tf_op jit(solution)/shard_map/ppermute | solution.py:453
  134.0 1.3 collective-permute-start.11
  160.7 1.7 copy-start.1

commit v2 on v1

--- a/solution.py
+++ b/solution.py
@@ -8,7 +8,7 @@
 
 GRID = ("grid_0", "grid_1", "grid_2", "grid_3")
 CORES = "grid_3"
-STAGES = (("grid_0", "grid_1"), "grid_2")
+STAGES = ("grid_2", ("grid_0", "grid_1"))
 NX = 48
 NY = 128
 K = 24
@@ -17,9 +17,10 @@
 HIGH = lax.Precision.HIGHEST
 F32 = jnp.float32
 BF16 = jnp.bfloat16
-PARAMS = pltpu.CompilerParams(vmem_limit_bytes=24 << 20)
 VMEM = pl.BlockSpec(memory_space=pltpu.VMEM)
 SMEM = pl.BlockSpec(memory_space=pltpu.SMEM)
+ANY = pl.BlockSpec(memory_space=pl.ANY)
+CHUNK = 8
 
 
 def iota(shape, dim):
@@ -78,7 +79,7 @@
     return jnp.concatenate([values, jnp.zeros((128 - rows, 128), F32)], axis=0).T
 
 
-def eliminate(system, count):
+def eliminate(system, count, meanwhile=None):
     lane = iota((1, 128), 1)
     row = iota(system.shape, 0)
 
@@ -86,6 +87,8 @@
         return jnp.where(lane < 64, system[:, k : k + 1], system[:, 64 + k : 65 + k])
 
     for k in range(0, count, 2):
+        if meanwhile is not None:
+            meanwhile(k // 2)
         one = system[k : k + 1]
         two = system[k + 1 : k + 2]
         left = column(k)
@@ -107,44 +110,72 @@
     return total
 
 
-def apply_kernel(table, index, u, u_before, u_after, medium, f_out):
-    for g in range(2):
-        rows = slice(K * g, K * g + K)
-        base = 6.0 + table[index[g]]
-        for x in range(NX):
-            diagonal = medium[x : x + 1, :] + base
-            f_out[x, rows] = diagonal * u[x, rows] - neighbours(
-                x, lambda i: u[i, rows], u_before[x, rows], u_after[x, rows]
-            )
-
-
-def first_gram_kernel(f, b, b_before, b_after, medium, b1_out, gram_out):
+def planes(ref, start, count):
+    return lambda x: ref[start : start + count, x, :]
+
+
+def stencil(diagonal, own, across, sibling):
+    def at(x):
+        return diagonal(x) * own(x) - neighbours(x, own, across(x), sibling(x))
+
+    return at
+
+
+def applied(g, table, index, medium, own, across, sibling):
+    base = 6.0 + table[index[g]]
+    return stencil(lambda x: medium[x : x + 1, :] + base, own, across, sibling)
+
+
+def front_kernel(table, index, u, across, sibling, medium, f_out):
+    made = applied(
+        0, table, index, medium, planes(u, 0, K), planes(across, 0, K), planes(sibling, 0, K)
+    )
+    for x in range(NX):
+        f_out[x] = made(x)
+
+
+def back_kernel(table, index, ub, across, sibling, medium, f_out, b_out, b1_out):
+    made = applied(
+        1, table, index, medium, planes(ub, 0, K), planes(across, 0, K), planes(sibling, 0, K)
+    )
+    own = planes(ub, K, 2 * B)
+    shifted = stencil(
+        lambda x: medium[x : x + 1, :] - SHIFT,
+        own,
+        planes(across, K, 2 * B),
+        planes(sibling, K, 2 * B),
+    )
+    for x in range(NX):
+        f_out[x] = made(x)
+        b_out[x] = own(x)
+        b1_out[x] = shifted(x)
+
+
+def pair(ref, x, rows=slice(None)):
+    return jnp.concatenate([ref[x, rows], ref[x + 1, rows]], axis=1)
+
+
+def first_gram_kernel(f0, f1, b, b1, gram_out):
     total = jnp.zeros((2 * K, 128), F32)
     zeros = jnp.zeros((8, 2 * NY), F32)
     tops = [jnp.zeros((B, NY), F32) for _ in range(2)]
     squares = [jnp.zeros((B, NY), F32) for _ in range(2)]
-
-    def next_field(x):
-        out = (medium[x : x + 1, :] - SHIFT) * b[x] - neighbours(
-            x, lambda i: b[i], b_before[x], b_after[x]
-        )
-        b1_out[x] = out
-        return out
-
     for x in range(0, NX, 2):
-        fields = jnp.concatenate([f[x], f[x + 1]], axis=1)
-        b_pair = jnp.concatenate([b[x], b[x + 1]], axis=1)
-        b1_pair = jnp.concatenate([next_field(x), next_field(x + 1)], axis=1)
+        fields = [pair(f0, x), pair(f1, x)]
+        b_pair = pair(b, x)
+        b1_pair = pair(b1, x)
         right = []
         for g in range(2):
             bg = b_pair[B * g : B * g + B]
             b1g = b1_pair[B * g : B * g + B]
-            right += [fields[K * g : K * g + K], bg, b1g, zeros]
+            right += [fields[g], bg, b1g, zeros]
             top = bg * b1g
             square = bg * bg
             tops[g] = tops[g] + top[:, :NY] + top[:, NY:]
             squares[g] = squares[g] + square[:, :NY] + square[:, NY:]
-        total = total + row_products(fields, jnp.concatenate(right, axis=0))
+        total = total + row_products(
+            jnp.concatenate(fields, axis=0), jnp.concatenate(right, axis=0)
+        )
     lane = iota((K, 128), 1)
     row = iota((K, 128), 0)
     packed = jnp.where(lane < 64, total[:K], total[K:])
@@ -156,47 +187,81 @@
     gram_out[...] = packed
 
 
-def second_gram_kernel(f, f_before, f_after, b1, first, medium, fields_out, gram_out):
+def rows_of(ref):
+    return lambda x: ref[x]
+
+
+def second_gram_kernel(
+    f0, f0_across, f0_sibling, f1, f1_across, f1_sibling, b1, first, medium, fields_out, gram_out
+):
     total = jnp.zeros((2 * K, 128), F32)
-
-    def next_field(x):
-        return (medium[x : x + 1, :] - SHIFT) * f[x] - neighbours(
-            x, lambda i: f[i], f_before[x], f_after[x]
-        )
-
+    made = [
+        stencil(
+            lambda x: medium[x : x + 1, :] - SHIFT, rows_of(own), rows_of(across), rows_of(sibling)
+        )
+        for own, across, sibling in ((f0, f0_across, f0_sibling), (f1, f1_across, f1_sibling))
+    ]
     for x in range(0, NX, 2):
-        nexts = [next_field(x), next_field(x + 1)]
-        for i in range(2):
-            for g in range(2):
-                at = 40 * g
-                fields_out[x + i, at : at + K] = nexts[i][K * g : K * g + K]
-                fields_out[x + i, at + K : at + K + B] = b1[x + i, B * g : B * g + B]
-        f_pair = jnp.concatenate([f[x], f[x + 1]], axis=1)
-        f1_pair = jnp.concatenate(nexts, axis=1)
-        b1_pair = jnp.concatenate([b1[x], b1[x + 1]], axis=1)
-        right = []
+        nexts = []
         for g in range(2):
-            right += [
-                f_pair[K * g : K * g + K],
-                f1_pair[K * g : K * g + K],
-                b1_pair[B * g : B * g + B],
-            ]
-        total = total + row_products(f1_pair, jnp.concatenate(right, axis=0))
+            ends = [made[g](x), made[g](x + 1)]
+            for i in range(2):
+                fields_out[x + i, K * g : K * g + K] = ends[i]
+            nexts.append(jnp.concatenate(ends, axis=1))
+        b1_pair = pair(b1, x)
+        right = [
+            pair(f0, x),
+            nexts[0],
+            b1_pair[:B],
+            pair(f1, x),
+            nexts[1],
+            b1_pair[B:],
+        ]
+        total = total + row_products(
+            jnp.concatenate(nexts, axis=0), jnp.concatenate(right, axis=0)
+        )
     lane = iota((K, 128), 1)
     gram_out[:K] = first[...]
     gram_out[K:] = jnp.where(lane < 64, total[:K], total[K:])
 
 
 def krylov_kernel(
-    grams, f, b, fields, before, after, medium, q_out, last_out, coef_out, shift_out
+    grams,
+    f0,
+    f1,
+    b,
+    b1,
+    b1_across,
+    b1_sibling,
+    fields,
+    fields_across,
+    fields_sibling,
+    medium,
+    q_out,
+    last_out,
+    coef_out,
+    shift_out,
+    f_next,
+    b_next,
 ):
+    def plain(x):
+        return medium[x : x + 1, :] - SHIFT
+
+    next_f = stencil(plain, rows_of(fields), rows_of(fields_across), rows_of(fields_sibling))
+    next_b = stencil(plain, rows_of(b1), rows_of(b1_across), rows_of(b1_sibling))
+
+    def meanwhile(step):
+        for x in range(4 * step, 4 * step + 4):
+            f_next[x] = next_f(x)
+            b_next[x] = next_b(x)
+
     gram = over_copies(grams)
     first = gram[:K]
     lane = iota((K, 128), 1)
     row = iota((K, 128), 0)
     place = lane & 63
     unit = jnp.where(place == row + K, 1.0, 0.0)
-    inverse_t = transposed(eliminate(jnp.where(place < K, first, unit), K))
+    inverse_t = transposed(eliminate(jnp.where(place < K, first, unit), K, meanwhile))
     first_t = transposed(first)
     second_t = transposed(gram[K:])
     coeffs = []
@@ -221,7 +286,7 @@
             [
                 jnp.concatenate([z0, zero, zero, pad], axis=1),
                 jnp.concatenate([mixed, z0, zero, pad], axis=1),
-                jnp.concatenate([z2 - theta * mixed, mixed, z0, pad], axis=1),
+                jnp.concatenate([z2 - theta * mixed, mixed - theta * z0, z0, pad], axis=1),
             ],
             axis=0,
         )
@@ -230,30 +295,24 @@
         for i, z in enumerate((z0, z1, z2, ginv)):
             coef_out[g, 24 * i : 24 * i + z.shape[0], :K] = z
         shift_out[8 * g : 8 * g + 8, :] = jnp.broadcast_to(theta, (8, 128))
-
-    def next_field(x, g):
-        rows = slice(40 * g, 40 * g + 40)
-        return (medium[x : x + 1, :] - SHIFT - thetas[g]) * fields[x, rows] - neighbours(
-            x, lambda i: fields[i, rows], before[x, rows], after[x, rows]
-        )
-
     zeros = jnp.zeros((8, 2 * NY), F32)
     for x in range(0, NX, 2):
         for g in range(2):
-            nexts = jnp.concatenate([next_field(x, g), next_field(x + 1, g)], axis=1)
-            rows = slice(40 * g, 40 * g + 40)
-            firsts = jnp.concatenate([fields[x, rows], fields[x + 1, rows]], axis=1)
             frows = slice(K * g, K * g + K)
             brows = slice(B * g, B * g + B)
-            f_pair = jnp.concatenate([f[x, frows], f[x + 1, frows]], axis=1)
-            b0 = jnp.concatenate([b[x, brows], b[x + 1, brows]], axis=1)
             theta = thetas[g]
             made = combination(
-                coeffs[g], jnp.concatenate([f_pair, firsts[:K], nexts[:K], zeros], axis=0)
+                coeffs[g],
+                jnp.concatenate(
+                    [pair((f0, f1)[g], x), pair(fields, x, frows), pair(f_next, x, frows), zeros],
+                    axis=0,
+                ),
             )
-            b1 = firsts[K:]
-            q1 = b1 - theta * b0
-            made = made + jnp.concatenate([b0, q1, nexts[K:] - theta * q1], axis=0)
+            b_own = pair(b, x, brows)
+            b_one = pair(b1, x, brows)
+            q1 = b_one - theta * b_own
+            q2 = (pair(b_next, x, brows) - theta * b_one) - theta * q1
+            made = made + jnp.concatenate([b_own, q1, q2], axis=0)
             for i in range(2):
                 part = made[:, NY * i : NY * i + NY]
                 q_out[x + i, 48 * g : 48 * g + 48] = part
@@ -263,7 +322,7 @@
 def basis_gram_kernel(q, fields, gram_out):
     for g in range(2):
         qrows = slice(48 * g, 48 * g + 48)
-        frows = slice(40 * g, 40 * g + K)
+        frows = slice(K * g, K * g + K)
         total = jnp.zeros((48, 128), F32)
         none = jnp.zeros((B, 2 * NY), F32)
         pad = jnp.zeros((40, 2 * NY), F32)
@@ -325,7 +384,32 @@
     gram_out[B:] = low
 
 
-def finish_kernel(table, index, moments, coef, shift, u, f, q, t, solution_out, residue_out):
+def finish_kernel(
+    table,
+    index,
+    moments,
+    coef,
+    shift,
+    f0,
+    f1,
+    t,
+    u_far,
+    q_far,
+    solution_far,
+    residue_far,
+    u,
+    q,
+    solution_out,
+    residue_out,
+    arrived,
+    left,
+):
+    copies = [
+        pltpu.make_async_copy(u_far, u, arrived.at[0]),
+        pltpu.make_async_copy(q_far, q, arrived.at[1]),
+    ]
+    for copy in copies:
+        copy.start()
     summed = over_copies(moments)
     packed = summed[:B]
     turned = transposed(packed)
@@ -400,51 +484,87 @@
             axis=0,
         )
         coeffs.append(split_coeffs(rows))
+    for copy in copies:
+        copy.wait()
+    leaving = []
     for x in range(0, NX, 2):
         for g in range(2):
-            krows = slice(K * g, K * g + K)
             brows = slice(B * g, B * g + B)
             qrows = slice(48 * g, 48 * g + 48)
-
-            def stack(x):
-                return jnp.concatenate(
-                    [u[x, krows], f[x, krows], q[x, qrows], t[x, brows]], axis=0
-                )
-
+            us = jnp.concatenate([u[g, :, x, :], u[g, :, x + 1, :]], axis=1)
             made = combination(
-                coeffs[g], jnp.concatenate([stack(x), stack(x + 1)], axis=1)
+                coeffs[g],
+                jnp.concatenate(
+                    [us, pair((f0, f1)[g], x), pair(q, x, qrows), pair(t, x, brows)], axis=0
+                ),
             )
             for i in range(2):
                 part = made[:, NY * i : NY * i + NY]
                 solution_out[brows, x + i, :] = part[:B]
                 residue_out[brows, x + i, :] = part[B:] + q[x + i, 48 * g : 48 * g + B]
-
-
-def call(kernel, shapes, scalars, *arrays, final=False):
-    if final:
-        out = [jax.ShapeDtypeStruct(s, F32) for s in shapes]
-    else:
-        out = [pltpu.VMEM(s, F32) for s in shapes]
-    here = [pltpu.with_memory_space_constraint(a, pltpu.VMEM) for a in arrays[scalars:]]
+        if (x + 2) % CHUNK == 0:
+            rows = pl.ds(x + 2 - CHUNK, CHUNK)
+            for near, far in ((solution_out, solution_far), (residue_out, residue_far)):
+                copy = pltpu.make_async_copy(
+                    near.at[:, rows, :], far.at[:, rows, :], left.at[len(leaving)]
+                )
+                copy.start()
+                leaving.append(copy)
+    for copy in leaving:
+        copy.wait()
+
+
+def here(values):
+    return pltpu.with_memory_space_constraint(values, pltpu.VMEM)
+
+
+def call(kernel, shapes, scalars, *arrays, scratch=(), limit=8):
+    count = len(arrays) - scalars
     return pl.pallas_call(
         kernel,
-        out_shape=out,
-        in_specs=[SMEM] * scalars + [VMEM] * len(here),
-        out_specs=[VMEM] * len(out),
-        compiler_params=PARAMS,
+        out_shape=[pltpu.VMEM(s, F32) for s in shapes],
+        in_specs=[SMEM] * scalars + [VMEM] * count,
+        out_specs=[VMEM] * len(shapes),
+        scratch_shapes=[pltpu.VMEM(s, F32) for s in scratch],
+        compiler_params=pltpu.CompilerParams(vmem_limit_bytes=limit << 20),
         name=kernel.__name__,
-    )(*arrays[:scalars], *here)
+    )(*arrays[:scalars], *(here(a) for a in arrays[scalars:]))
+
+
+def finish(scalars, near, far, shape):
+    copies = 2 * NX // CHUNK
+    return pl.pallas_call(
+        finish_kernel,
+        out_shape=[jax.ShapeDtypeStruct(shape, F32)] * 2,
+        in_specs=[SMEM] * len(scalars) + [VMEM] * len(near) + [ANY] * len(far),
+        out_specs=[ANY] * 2,
+        scratch_shapes=[pltpu.VMEM(a.shape, F32) for a in far]
+        + [pltpu.VMEM(shape, F32)] * 2
+        + [pltpu.SemaphoreType.DMA((len(far),)), pltpu.SemaphoreType.DMA((copies,))],
+        compiler_params=pltpu.CompilerParams(vmem_limit_bytes=14 << 20),
+        name="finish_kernel",
+    )(*scalars, *(here(a) for a in near), *far)
+
+
+def add_kernel(one, two, out):
+    total = one[...] + two[...]
+    for i in range(out.shape[0]):
+        out[i] = total
+
+
+def respread_kernel(parts, out):
+    total = over_copies(parts)
+    for i in range(out.shape[0]):
+        out[i] = total
 
 
 def everyone(values):
-    values = values + lax.ppermute(values, CORES, [(0, 1), (1, 0)])
-    for number, axes in enumerate(STAGES):
-        if number:
-            values = jnp.sum(values, axis=0)
-        size = lax.axis_size(axes)
-        spread = jnp.broadcast_to(values[None], (size, *values.shape))
-        values = lax.all_to_all(spread, axes, 0, 0, tiled=True)
-    return values
+    far, near = STAGES
+    other = lax.ppermute(values, CORES, [(0, 1), (1, 0)])
+    (spread,) = call(add_kernel, [(lax.axis_size(far), *values.shape)], 0, values, other)
+    parts = lax.all_to_all(spread, far, 0, 0, tiled=True)
+    (spread,) = call(respread_kernel, [(lax.axis_size(near), *values.shape)], 0, parts)
+    return lax.all_to_all(spread, near, 0, 0, tiled=True)
 
 
 def beside(values):
@@ -457,16 +577,41 @@
 
 def on_device(right_sides, recycle, medium, shift_table, shift_index):
     med = medium[0]
-    u = jnp.transpose(recycle.reshape(2 * K, NX, NY), (1, 0, 2))
-    b = jnp.transpose(right_sides.reshape(2 * B, NX, NY), (1, 0, 2))
-    u_sides = beside(u)
-    b_sides = beside(b)
-    (f,) = call(apply_kernel, [(NX, 2 * K, NY)], 2, shift_table, shift_index, u, *u_sides, med)
-    f, b_sides = lax.optimization_barrier((f, b_sides))
-    f_sides = beside(f)
-    b1, first = call(first_gram_kernel, [(NX, 2 * B, NY), (K, 128)], 0, f, b, *b_sides, med)
+    u = recycle.reshape(2, K, NX, NY)
+    b = right_sides.reshape(2 * B, NX, NY)
+    scalars = (shift_table, shift_index)
+    back = jnp.concatenate([u[1], b], axis=0)
+    back_sides = beside(back)
+    front = u[0]
+    front_across, front_sibling = beside(front)
+    f1, b, b1 = call(
+        back_kernel,
+        [(NX, K, NY), (NX, 2 * B, NY), (NX, 2 * B, NY)],
+        2,
+        *scalars,
+        back,
+        *back_sides,
+        med,
+    )
+    f1_sides = beside(f1)
+    front_across, b1 = lax.optimization_barrier((front_across, b1))
+    (f0,) = call(
+        front_kernel, [(NX, K, NY)], 2, *scalars, front, front_across, front_sibling, med
+    )
+    f0_sides = beside(f0)
+    b1_sides = beside(b1)
+    (first,) = call(first_gram_kernel, [(K, 128)], 0, f0, f1, b, b1)
     fields, gram = call(
-        second_gram_kernel, [(NX, 80, NY), (2 * K, 128)], 0, f, *f_sides, b1, first, med
+        second_gram_kernel,
+        [(NX, 2 * K, NY), (2 * K, 128)],
+        0,
+        f0,
+        *f0_sides,
+        f1,
+        *f1_sides,
+        b1,
+        first,
+        med,
     )
     field_sides = beside(fields)
     q, last, coef, shift = call(
@@ -474,31 +619,23 @@
         [(NX, 96, NY), (NX, 2 * B, NY), (2, 96, 128), (16, 128)],
         0,
         everyone(gram),
-        f,
+        f0,
+        f1,
         b,
+        b1,
+        *b1_sides,
         fields,
         *field_sides,
         med,
+        scratch=[(NX, 2 * K, NY), (NX, 2 * B, NY)],
     )
     last_sides = beside(last)
     (basis_gram,) = call(basis_gram_kernel, [(2, 48, 128)], 0, q, fields)
     t, gram = call(
         moment_kernel, [(NX, 2 * B, NY), (K, 128)], 0, last, *last_sides, basis_gram, med, shift
     )
-    solution, residue = call(
-        finish_kernel,
-        [(2 * B, NX, NY)] * 2,
-        2,
-        shift_table,
-        shift_index,
-        everyone(gram),
-        coef,
-        shift,
-        u,
-        f,
-        q,
-        t,
-        final=True,
+    solution, residue = finish(
+        scalars, (everyone(gram), coef, shift, f0, f1, t), (u, q), (2 * B, NX, NY)
     )
     return solution.reshape(right_sides.shape), residue.reshape(right_sides.shape)
 

time: 170 us -> 169 us (level)
  blocking collectives: 73.1 us -> 46.8 us
  starting transfers between devices: 24.8 us -> 43 us
  waiting for transfers between devices: 42.4 us -> 47.6 us
  Pallas kernels: 23.5 us -> 25.5 us
    all_to_all x4 -> x3, blocking collectives: 73.1 us -> 46.8 us  [the longest x2 33.9 us: everyone(): parts = lax.all_to_all(spread, far, 0, 0, tiled=True)]
    all_to_all x0 -> x1, starting transfers between devices: none -> 11.6 us  [everyone(): return lax.all_to_all(spread, near, 0, 0, tiled=True)]
    all_to_all x0 -> x1, waiting for transfers between devices: none -> 9.18 us  [everyone(): return lax.all_to_all(spread, near, 0, 0, tiled=True)]
    ppermute x5 -> x7, starting transfers between devices: 24.3 us -> 29.9 us  [beside(): across = lax.ppermute(values, GRID, edges + [(j, i) for i, j in edges])]
    ppermute x5 -> x7, waiting for transfers between devices: 40 us -> 36 us  [beside(): across = lax.ppermute(values, GRID, edges + [(j, i) for i, j in edges])]
    pallas_call x7 -> x12, Pallas kernels: 23.5 us -> 25.5 us  [the longest x11 17.5 us: call(): pl.pallas_call(kernel, out_shape=[pltpu.VMEM(s, F32) for s in shapes], in...]
    unnamed x14 -> x20, local copies, waits for them, and re-layouts: 3.67 us -> 2.72 us
  transfers between devices with their start and end apart: 12 -> 17, of which waited for: 6 -> 8; matrix products, arithmetic and copies ran while one was open for 1% -> 0% of each run, Pallas kernels for 4% -> 4%
where the time goes in v2:
time: 169 us; the launch traced here: 168 us
  waiting for transfers between devices  47.6 us (28%)
  blocking collectives  46.8 us (28%)
  starting transfers between devices  43 us (25%)
  Pallas kernels  25.5 us (15%)
  local copies, waits for them, and re-layouts  4.12 us (2%)
    ppermute x7, waiting for transfers between devices, beside(): across = lax.ppermute(values, GRID, edges + [(j, i) for i, j in edges])  36 us
    all_to_all x2, blocking collectives, everyone(): parts = lax.all_to_all(spread, far, 0, 0, tiled=True)  33.9 us
    ppermute x7, starting transfers between devices, beside(): across = lax.ppermute(values, GRID, edges + [(j, i) for i, j in edges])  29.9 us
    pallas_call x11, Pallas kernels, call(): pl.pallas_call(kernel, out_shape=[pltpu.VMEM(s, F32) for s in shapes], in...  17.5 us
    all_to_all x1, blocking collectives, everyone(): return lax.all_to_all(spread, near, 0, 0, tiled=True)  12.9 us
    all_to_all x1, starting transfers between devices, everyone(): return lax.all_to_all(spread, near, 0, 0, tiled=True)  11.6 us
    all_to_all x1, waiting for transfers between devices, everyone(): return lax.all_to_all(spread, near, 0, 0, tiled=True)  9.18 us
    pallas_call x1, Pallas kernels, finish(): pl.pallas_call(finish_kernel, out_shape=[jax.ShapeDtypeStruct(shape, F32)...  8 us
  transfers between devices with their start and end apart: 17, of which 8 were waited for; matrix products, arithmetic and copies ran while one was open for 0% of the time, Pallas kernels for 4%

profile of v2, /device:TPU:8, one launch (start us, length us, event | category | flops | bytes accessed | tf_op | source)
XLA Modules:
  0.0 168.0 jit_solution(7037030317359815131)
XLA Ops:
  0.6 0.0 copy-start.9
  0.6 1.4 slice_bitcast_fusion
  2.0 0.1 copy-done.9
  2.1 0.0 copy-start.4
  2.1 0.0 copy-start.7
  2.1 0.0 copy-start.8
  2.1 0.1 pad_maximum_fusion.ub
  2.2 0.1 collective-permute-start.2
  2.3 7.7 %collective-permute-start.1 = (f32[56,48,128]{2,1,0:T(8,128)S(1)}, f32[56,48,128]{2,1,0:T(8,128)S(1)}, u32[]{:S(2)}, u32[]{:S(2)}) collective-permute-start(f32[56,48,128]{2,1,0:T(8,128)S(1)} %pad_maximum_fusion.ub), channel_id=1, source_target_pairs={{1,2},{3,4},{5,6},{7,8},{9,10},{11,12},{13,14},{15,16},{17,18},{19... | collective-permute-start | bytes 4128776 | tf_op jit(solution)/shard_map/ppermute | solution.py:573
  10.1 1.9 %collective-permute-start = (f32[24,48,128]{2,1,0:T(8,128)S(1)}, f32[24,48,128]{2,1,0:T(8,128)S(1)}, u32[]{:S(2)}, u32[]{:S(2)}) collective-permute-start(f32[24,48,128]{2,1,0:T(8,128)S(1)} %get-tuple-element.35.u), channel_id=1, source_target_pairs={{1,2},{3,4},{5,6},{7,8},{9,10},{11,12},{13,14},{15,16},{17,18},{19... | collective-permute-start | bytes 1769480 | tf_op jit(solution)/shard_map/ppermute | solution.py:573
  12.0 0.1 collective-permute-start.3
  12.1 0.0 collective-permute-done.2.sibling
  12.1 13.9 %collective-permute-done.1.across = f32[56,48,128]{2,1,0:T(8,128)S(1)} collective-permute-done((f32[56,48,128]{2,1,0:T(8,128)S(1)}, f32[56,48,128]{2,1,0:T(8,128)S(1)}, u32[]{:S(2)}, u32[]{:S(2)}) %collective-permute-start.1) | collective-permute-done | bytes 1376288 | tf_op jit(solution)/shard_map/ppermute | solution.py:573
  26.0 0.0 copy-done.4
  26.0 0.0 copy-done.7
  26.1 0.0 copy-done.8
  26.1 4.0 %back_kernel.1 = (f32[48,24,128]{2,1,0:T(8,128)S(1)}, f32[48,32,128]{2,1,0:T(8,128)S(1)}, f32[48,32,128]{2,1,0:T(8,128)S(1)}) custom-call(f32[8]{0:T(128)S(1)} %copy-done.7, s32[2]{0:T(128)S(1)} %copy-done.8, f32[56,48,128]{2,1,0:T(8,128)S(1)} %pad_maximum_fusion.ub, f32[56,48,128]{2,1,0:T(8,128)S(1)} %collective-permute-done.1.across, ...), custom_call_target="tpu_custom_call" | custom-call | tf_op jit(solution)/shard_map/back_kernel/pallas_call | solution.py:523
  30.1 0.0 copy-start.1
  30.1 2.3 %collective-permute-done.across = f32[24,48,128]{2,1,0:T(8,128)S(1)} collective-permute-done((f32[24,48,128]{2,1,0:T(8,128)S(1)}, f32[24,48,128]{2,1,0:T(8,128)S(1)}, u32[]{:S(2)}, u32[]{:S(2)}) %collective-permute-start) | collective-permute-done | bytes 589856 | tf_op jit(solution)/shard_map/ppermute | solution.py:573
  32.4 0.0 collective-permute-done.3.sibling
  32.4 1.9 %front_kernel.1.f0 = f32[48,24,128]{2,1,0:T(8,128)S(1)} custom-call(f32[8]{0:T(128)S(1)} %copy-done.7, s32[2]{0:T(128)S(1)} %copy-done.8, f32[24,48,128]{2,1,0:T(8,128)S(1)} %get-tuple-element.35.u, f32[24,48,128]{2,1,0:T(8,128)S(1)} %collective-permute-done.across, f32[24,48,128]{2,1,0:T(8,128)S(1)} %collective-permute-done.3.sibling, f32[48,128]{1,0:T(8,128)S(1)} %bitcast.17), custom_call_target="tpu_custom_call" | custom-call | tf_op jit(solution)/shard_map/front_kernel/pallas_call | solution.py:523
  34.3 0.1 collective-permute-start.5
  34.4 5.8 %collective-permute-start.4 = (f32[48,24,128]{2,1,0:T(8,128)S(1)}, f32[48,24,128]{2,1,0:T(8,128)S(1)}, u32[]{:S(2)}, u32[]{:S(2)}) collective-permute-start(f32[48,24,128]{2,1,0:T(8,128)S(1)} %front_kernel.1.f0), channel_id=1, source_target_pairs={{1,2},{3,4},{5,6},{7,8},{9,10},{11,12},{13,14},{15,16},{17,18},{19... | collective-permute-start | bytes 1769480 | tf_op jit(solution)/shard_map/ppermute | solution.py:573
  40.2 0.1 collective-permute-start.7
  40.3 2.4 %collective-permute-start.6 = (f32[48,24,128]{2,1,0:T(8,128)S(1)}, f32[48,24,128]{2,1,0:T(8,128)S(1)}, u32[]{:S(2)}, u32[]{:S(2)}) collective-permute-start(f32[48,24,128]{2,1,0:T(8,128)S(1)} %get-tuple-element.19.f1), channel_id=1, source_target_pairs={{1,2},{3,4},{5,6},{7,8},{9,10},{11,12},{13,14},{15,16},{17,18},{19... | collective-permute-start | bytes 1769480 | tf_op jit(solution)/shard_map/ppermute | solution.py:573
  42.7 1.1 first_gram_kernel.1.first
  43.8 0.0 copy-done.1
  43.8 0.0 collective-permute-done.5.f0_sibling
  43.8 3.9 %collective-permute-done.4.f0_across = f32[48,24,128]{2,1,0:T(8,128)S(1)} collective-permute-done((f32[48,24,128]{2,1,0:T(8,128)S(1)}, f32[48,24,128]{2,1,0:T(8,128)S(1)}, u32[]{:S(2)}, u32[]{:S(2)}) %collective-permute-start.4) | collective-permute-done | bytes 589856 | tf_op jit(solution)/shard_map/ppermute | solution.py:573
  47.7 0.0 collective-permute-done.7.f1_sibling
  47.7 6.3 %collective-permute-done.6.f1_across = f32[48,24,128]{2,1,0:T(8,128)S(1)} collective-permute-done((f32[48,24,128]{2,1,0:T(8,128)S(1)}, f32[48,24,128]{2,1,0:T(8,128)S(1)}, u32[]{:S(2)}, u32[]{:S(2)}) %collective-permute-start.6) | collective-permute-done | bytes 589856 | tf_op jit(solution)/shard_map/ppermute | solution.py:573
  54.0 1.4 second_gram_kernel.1
  55.4 0.1 collective-permute-start.12
  55.5 5.8 %collective-permute-start.11 = (f32[48,48,128]{2,1,0:T(8,128)S(1)}, f32[48,48,128]{2,1,0:T(8,128)}, u32[]{:S(2)}, u32[]{:S(2)}) collective-permute-start(f32[48,48,128]{2,1,0:T(8,128)S(1)} %get-tuple-element.23.fields), channel_id=1, source_target_pairs={{1,2},{3,4},{5,6},{7,8},{9,10},{11,12},{13,14},{15,16},{17,18},{19... | collective-permute-start | bytes 3538952 | tf_op jit(solution)/shard_map/ppermute | solution.py:573
  61.3 0.1 collective-permute-start.10
  61.4 2.4 %collective-permute-start.9 = (f32[48,32,128]{2,1,0:T(8,128)S(1)}, f32[48,32,128]{2,1,0:T(8,128)}, u32[]{:S(2)}, u32[]{:S(2)}) collective-permute-start(f32[48,32,128]{2,1,0:T(8,128)S(1)} %get-tuple-element.20.b1), channel_id=1, source_target_pairs={{1,2},{3,4},{5,6},{7,8},{9,10},{11,12},{13,14},{15,16},{17,18},{19... | collective-permute-start | bytes 2359304 | tf_op jit(solution)/shard_map/ppermute | solution.py:573
  63.8 0.1 collective-permute-start.8
  63.9 1.2 collective-permute-done.8.two
  65.1 22.5 %all_to_all.20.parts = f32[8,48,128]{2,1,0:T(8,128)S(1)} all-to-all(f32[8,48,128]{2,1,0:T(8,128)S(1)} %add_kernel.2), channel_id=1, replica_groups=mesh['grid_0'=4,'grid_1'=4,'grid_2'=8,'grid_3'=2] {'grid_2'}, dimensions={0} | all-to-all | bytes 393216 | tf_op jit(solution)/shard_map/all_to_all | solution.py:565
  87.7 0.0 copy-start.3
  87.7 0.7 copy-done.3
  88.4 11.6 %all-to-all-start.1 = ((f32[16,48,128]{2,1,0:T(8,128)}), f32[16,48,128]{2,1,0:T(8,128)S(1)}, u32[]{:S(2)}, u32[]{:S(2)}) async-start(f32[16,48,128]{2,1,0:T(8,128)} %copy-done.3), calls=%async_computation.1 | async-start | bytes 786432 | tf_op jit(solution)/shard_map/all_to_all | solution.py:567
  100.0 0.0 collective-permute-done.10.b1_sibling
  100.0 0.0 collective-permute-done.9.b1_across
  100.0 9.2 %all-to-all-done.1.grams = f32[16,48,128]{2,1,0:T(8,128)S(1)} async-done(((f32[16,48,128]{2,1,0:T(8,128)}), f32[16,48,128]{2,1,0:T(8,128)S(1)}, u32[]{:S(2)}, u32[]{:S(2)}) %all-to-all-start.1) | async-done | bytes 393248 | tf_op jit(solution)/shard_map/all_to_all | solution.py:567
  109.2 0.0 collective-permute-done.12.fields_sibling
  109.2 0.0 collective-permute-done.11.fields_across
  109.2 1.1 copy-done.2
  110.3 0.7 copy-done.5
  111.0 6.1 %krylov_kernel.1 = (f32[48,96,128]{2,1,0:T(8,128)S(1)}, f32[48,32,128]{2,1,0:T(8,128)S(1)}, f32[2,96,128]{2,1,0:T(8,128)S(1)}, f32[16,128]{1,0:T(8,128)S(1)}) custom-call(f32[16,48,128]{2,1,0:T(8,128)S(1)} %all-to-all-done.1.grams, f32[48,24,128]{2,1,0:T(8,128)S(1)} %front_kernel.1.f0, f32[48,24,128]{2,1,0:T(8,128)S(1)} %get-tuple-element.19.f1, ...), custom_call_target="tpu_custom_call" | custom-call | tf_op jit(solution)/shard_map/krylov_kernel/pallas_call | solution.py:523
  117.1 0.8 collective-permute-start.14
  117.9 4.0 %collective-permute-start.13 = (f32[48,32,128]{2,1,0:T(8,128)S(1)}, f32[48,32,128]{2,1,0:T(8,128)S(1)}, u32[]{:S(2)}, u32[]{:S(2)}) collective-permute-start(f32[48,32,128]{2,1,0:T(8,128)S(1)} %get-tuple-element.24.last), channel_id=1, source_target_pairs={{1,2},{3,4},{5,6},{7,8},{9,10},{11,12},{13,14},{15,16},{17,18},{19... | collective-permute-start | bytes 2359304 | tf_op jit(solution)/shard_map/ppermute | solution.py:573
  121.9 0.0 copy-start.6
  121.9 1.8 %basis_gram_kernel.1.basis_gram = f32[2,48,128]{2,1,0:T(8,128)S(1)} custom-call(f32[48,96,128]{2,1,0:T(8,128)S(1)} %get-tuple-element.25.q.q_far, f32[48,48,128]{2,1,0:T(8,128)S(1)} %get-tuple-element.23.fields), custom_call_target="tpu_custom_call" | custom-call | tf_op jit(solution)/shard_map/basis_gram_kernel/pallas_call | solution.py:523
  123.7 0.0 collective-permute-done.14.last_after
  123.7 9.6 %collective-permute-done.13.last_before = f32[48,32,128]{2,1,0:T(8,128)S(1)} collective-permute-done((f32[48,32,128]{2,1,0:T(8,128)S(1)}, f32[48,32,128]{2,1,0:T(8,128)S(1)}, u32[]{:S(2)}, u32[]{:S(2)}) %collective-permute-start.13) | collective-permute-done | bytes 786464 | tf_op jit(solution)/shard_map/ppermute | solution.py:573
  133.3 0.0 copy-done.6
  133.3 1.0 moment_kernel.1
  134.4 0.1 collective-permute-start.15
  134.5 1.2 collective-permute-done.15.two
  135.6 11.4 %all_to_all.21.parts = f32[8,24,128]{2,1,0:T(8,128)S(1)} all-to-all(f32[8,24,128]{2,1,0:T(8,128)S(1)} %add_kernel.3), channel_id=1, replica_groups=mesh['grid_0'=4,'grid_1'=4,'grid_2'=8,'grid_3'=2] {'grid_2'}, dimensions={0} | all-to-all | bytes 196608 | tf_op jit(solution)/shard_map/all_to_all | solution.py:565
  147.0 12.9 %all_to_all.22.moments = f32[16,24,128]{2,1,0:T(8,128)S(1)} all-to-all(f32[16,24,128]{2,1,0:T(8,128)S(1)} %respread_kernel.3), channel_id=1, replica_groups=mesh['grid_0'=4,'grid_1'=4,'grid_2'=8,'grid_3'=2] {'grid_0','grid_1'}, dimensions={0} | all-to-all | bytes 393216 | tf_op jit(solution)/shard_map/all_to_all | solution.py:567
  159.9 0.0 copy-done
  159.9 8.0 %finish_kernel.1 = (f32[32,48,128]{2,1,0:T(8,128)}, f32[32,48,128]{2,1,0:T(8,128)}) custom-call(f32[8]{0:T(128)S(1)} %copy-done.7, s32[2]{0:T(128)S(1)} %copy-done.8, f32[16,24,128]{2,1,0:T(8,128)S(1)} %all_to_all.22.moments, f32[2,96,128]{2,1,0:T(8,128)S(1)} %get-tuple-element.28.coef, f32[16,128]{1,0:T(8,128)S(1)} %get-tuple-element.26.shift, ...), custom_call_target="tpu_custom_call" | custom-call | tf_op jit(solution)/shard_map/finish_kernel/pallas_call | solution.py:536
  (7 shorter events, 0.1 us)
Async XLA Ops:
  0.6 1.5 copy-start.9
  2.1 23.9 %copy-start.4 = (f32[1,48,128]{2,1,0:T(8,128)S(1)}, f32[1,48,128]{2,1,0:T(8,128)}, u32[]{:S(2)}) copy-start(f32[1,48,128]{2,1,0:T(8,128)} %param.7) | copy-start | bytes 73732
  2.1 23.9 %copy-start.7 = (f32[8]{0:T(128)S(1)}, f32[8]{0:T(128)}, u32[]{:S(2)}) copy-start(f32[8]{0:T(128)} %table.5) | copy-start | bytes 100
  2.1 23.9 %copy-start.8 = (s32[2]{0:T(128)S(1)}, s32[2]{0:T(128)}, u32[]{:S(2)}) copy-start(s32[2]{0:T(128)} %index.5) | copy-start | bytes 28
  2.2 9.9 %collective-permute-start.2 = (f32[56,48,128]{2,1,0:T(8,128)S(1)}, f32[56,48,128]{2,1,0:T(8,128)S(1)}, u32[]{:S(2)}, u32[]{:S(2)}) collective-permute-start(f32[56,48,128]{2,1,0:T(8,128)S(1)} %pad_maximum_fusion.ub), channel_id=1, source_target_pairs={{0,1},{1,0},{2,3},{3,2},{4,5},{5,4},{6,7},{7,6},{8,9},{9,8},{10,11... | collective-permute-start | bytes 4128776 | tf_op jit(solution)/shard_map/ppermute | solution.py:574
  2.3 23.7 %collective-permute-start.1 = (f32[56,48,128]{2,1,0:T(8,128)S(1)}, f32[56,48,128]{2,1,0:T(8,128)S(1)}, u32[]{:S(2)}, u32[]{:S(2)}) collective-permute-start(f32[56,48,128]{2,1,0:T(8,128)S(1)} %pad_maximum_fusion.ub), channel_id=1, source_target_pairs={{1,2},{3,4},{5,6},{7,8},{9,10},{11,12},{13,14},{15,16},{17,18},{19... | collective-permute-start | bytes 4128776 | tf_op jit(solution)/shard_map/ppermute | solution.py:573
  10.1 22.3 %collective-permute-start = (f32[24,48,128]{2,1,0:T(8,128)S(1)}, f32[24,48,128]{2,1,0:T(8,128)S(1)}, u32[]{:S(2)}, u32[]{:S(2)}) collective-permute-start(f32[24,48,128]{2,1,0:T(8,128)S(1)} %get-tuple-element.35.u), channel_id=1, source_target_pairs={{1,2},{3,4},{5,6},{7,8},{9,10},{11,12},{13,14},{15,16},{17,18},{19... | collective-permute-start | bytes 1769480 | tf_op jit(solution)/shard_map/ppermute | solution.py:573
  12.0 20.4 %collective-permute-start.3 = (f32[24,48,128]{2,1,0:T(8,128)S(1)}, f32[24,48,128]{2,1,0:T(8,128)S(1)}, u32[]{:S(2)}, u32[]{:S(2)}) collective-permute-start(f32[24,48,128]{2,1,0:T(8,128)S(1)} %get-tuple-element.35.u), channel_id=1, source_target_pairs={{0,1},{1,0},{2,3},{3,2},{4,5},{5,4},{6,7},{7,6},{8,9},{9,8},{10,11... | collective-permute-start | bytes 1769480 | tf_op jit(solution)/shard_map/ppermute | solution.py:574
  30.1 13.7 %copy-start.1 = (f32[48,32,128]{2,1,0:T(8,128)}, f32[48,32,128]{2,1,0:T(8,128)S(1)}, u32[]{:S(2)}) copy-start(f32[48,32,128]{2,1,0:T(8,128)S(1)} %get-tuple-element.21.b) | copy-start | bytes 2359300
  34.3 9.5 %collective-permute-start.5 = (f32[48,24,128]{2,1,0:T(8,128)S(1)}, f32[48,24,128]{2,1,0:T(8,128)S(1)}, u32[]{:S(2)}, u32[]{:S(2)}) collective-permute-start(f32[48,24,128]{2,1,0:T(8,128)S(1)} %front_kernel.1.f0), channel_id=1, source_target_pairs={{0,1},{1,0},{2,3},{3,2},{4,5},{5,4},{6,7},{7,6},{8,9},{9,8},{10,11... | collective-permute-start | bytes 1769480 | tf_op jit(solution)/shard_map/ppermute | solution.py:574
  34.4 13.3 %collective-permute-start.4 = (f32[48,24,128]{2,1,0:T(8,128)S(1)}, f32[48,24,128]{2,1,0:T(8,128)S(1)}, u32[]{:S(2)}, u32[]{:S(2)}) collective-permute-start(f32[48,24,128]{2,1,0:T(8,128)S(1)} %front_kernel.1.f0), channel_id=1, source_target_pairs={{1,2},{3,4},{5,6},{7,8},{9,10},{11,12},{13,14},{15,16},{17,18},{19... | collective-permute-start | bytes 1769480 | tf_op jit(solution)/shard_map/ppermute | solution.py:573
  40.2 7.6 %collective-permute-start.7 = (f32[48,24,128]{2,1,0:T(8,128)S(1)}, f32[48,24,128]{2,1,0:T(8,128)S(1)}, u32[]{:S(2)}, u32[]{:S(2)}) collective-permute-start(f32[48,24,128]{2,1,0:T(8,128)S(1)} %get-tuple-element.19.f1), channel_id=1, source_target_pairs={{0,1},{1,0},{2,3},{3,2},{4,5},{5,4},{6,7},{7,6},{8,9},{9,8},{10,11... | collective-permute-start | bytes 1769480 | tf_op jit(solution)/shard_map/ppermute | solution.py:574
  40.3 13.8 %collective-permute-start.6 = (f32[48,24,128]{2,1,0:T(8,128)S(1)}, f32[48,24,128]{2,1,0:T(8,128)S(1)}, u32[]{:S(2)}, u32[]{:S(2)}) collective-permute-start(f32[48,24,128]{2,1,0:T(8,128)S(1)} %get-tuple-element.19.f1), channel_id=1, source_target_pairs={{1,2},{3,4},{5,6},{7,8},{9,10},{11,12},{13,14},{15,16},{17,18},{19... | collective-permute-start | bytes 1769480 | tf_op jit(solution)/shard_map/ppermute | solution.py:573
  55.4 53.7 %collective-permute-start.12 = (f32[48,48,128]{2,1,0:T(8,128)S(1)}, f32[48,48,128]{2,1,0:T(8,128)}, u32[]{:S(2)}, u32[]{:S(2)}) collective-permute-start(f32[48,48,128]{2,1,0:T(8,128)S(1)} %get-tuple-element.23.fields), channel_id=1, source_target_pairs={{0,1},{1,0},{2,3},{3,2},{4,5},{5,4},{6,7},{7,6},{8,9},{9,8},{10,11... | collective-permute-start | bytes 3538952 | tf_op jit(solution)/shard_map/ppermute | solution.py:574
  55.5 53.6 %collective-permute-start.11 = (f32[48,48,128]{2,1,0:T(8,128)S(1)}, f32[48,48,128]{2,1,0:T(8,128)}, u32[]{:S(2)}, u32[]{:S(2)}) collective-permute-start(f32[48,48,128]{2,1,0:T(8,128)S(1)} %get-tuple-element.23.fields), channel_id=1, source_target_pairs={{1,2},{3,4},{5,6},{7,8},{9,10},{11,12},{13,14},{15,16},{17,18},{19... | collective-permute-start | bytes 3538952 | tf_op jit(solution)/shard_map/ppermute | solution.py:573
  61.3 38.7 %collective-permute-start.10 = (f32[48,32,128]{2,1,0:T(8,128)S(1)}, f32[48,32,128]{2,1,0:T(8,128)}, u32[]{:S(2)}, u32[]{:S(2)}) collective-permute-start(f32[48,32,128]{2,1,0:T(8,128)S(1)} %get-tuple-element.20.b1), channel_id=1, source_target_pairs={{0,1},{1,0},{2,3},{3,2},{4,5},{5,4},{6,7},{7,6},{8,9},{9,8},{10,11... | collective-permute-start | bytes 2359304 | tf_op jit(solution)/shard_map/ppermute | solution.py:574
  61.4 38.6 %collective-permute-start.9 = (f32[48,32,128]{2,1,0:T(8,128)S(1)}, f32[48,32,128]{2,1,0:T(8,128)}, u32[]{:S(2)}, u32[]{:S(2)}) collective-permute-start(f32[48,32,128]{2,1,0:T(8,128)S(1)} %get-tuple-element.20.b1), channel_id=1, source_target_pairs={{1,2},{3,4},{5,6},{7,8},{9,10},{11,12},{13,14},{15,16},{17,18},{19... | collective-permute-start | bytes 2359304 | tf_op jit(solution)/shard_map/ppermute | solution.py:573
  63.8 1.3 collective-permute-start.8
  87.7 0.7 copy-start.3
  88.4 20.7 %all-to-all-start.1 = ((f32[16,48,128]{2,1,0:T(8,128)}), f32[16,48,128]{2,1,0:T(8,128)S(1)}, u32[]{:S(2)}, u32[]{:S(2)}) async-start(f32[16,48,128]{2,1,0:T(8,128)} %copy-done.3), calls=%async_computation.1 | async-start | bytes 786432 | tf_op jit(solution)/shard_map/all_to_all | solution.py:567
  109.2 1.1 copy-start.2
  110.3 0.7 copy-start.5
  117.1 6.6 %collective-permute-start.14 = (f32[48,32,128]{2,1,0:T(8,128)S(1)}, f32[48,32,128]{2,1,0:T(8,128)S(1)}, u32[]{:S(2)}, u32[]{:S(2)}) collective-permute-start(f32[48,32,128]{2,1,0:T(8,128)S(1)} %get-tuple-element.24.last), channel_id=1, source_target_pairs={{0,1},{1,0},{2,3},{3,2},{4,5},{5,4},{6,7},{7,6},{8,9},{9,8},{10,11... | collective-permute-start | bytes 2359304 | tf_op jit(solution)/shard_map/ppermute | solution.py:574
  117.9 15.4 %collective-permute-start.13 = (f32[48,32,128]{2,1,0:T(8,128)S(1)}, f32[48,32,128]{2,1,0:T(8,128)S(1)}, u32[]{:S(2)}, u32[]{:S(2)}) collective-permute-start(f32[48,32,128]{2,1,0:T(8,128)S(1)} %get-tuple-element.24.last), channel_id=1, source_target_pairs={{1,2},{3,4},{5,6},{7,8},{9,10},{11,12},{13,14},{15,16},{17,18},{19... | collective-permute-start | bytes 2359304 | tf_op jit(solution)/shard_map/ppermute | solution.py:573
  121.9 11.4 %copy-start.6 = (f32[1,48,128]{2,1,0:T(8,128)S(1)}, f32[1,48,128]{2,1,0:T(8,128)}, u32[]{:S(2)}) copy-start(f32[1,48,128]{2,1,0:T(8,128)} %param.7) | copy-start | bytes 73732
  133.3 26.6 %copy-start = (f32[2,24,1,48,128]{4,3,2,1,0:T(8,128)S(1)}, f32[2,24,1,48,128]{4,3,2,1,0:T(8,128)}, u32[]{:S(2)}) copy-start(f32[2,24,1,48,128]{4,3,2,1,0:T(8,128)} %param.6) | copy-start | bytes 3538948
  134.4 1.3 collective-permute-start.15

commit v3 on v2

--- a/solution.py
+++ b/solution.py
@@ -111,7 +111,7 @@
 
 
 def planes(ref, start, count):
-    return lambda x: ref[start : start + count, x, :]
+    return lambda x: ref[x, start : start + count]
 
 
 def stencil(diagonal, own, across, sibling):
@@ -393,11 +393,13 @@
     f0,
     f1,
     t,
-    u_far,
+    u0_far,
+    u1_far,
     q_far,
     solution_far,
     residue_far,
-    u,
+    u0,
+    u1,
     q,
     solution_out,
     residue_out,
@@ -405,8 +407,9 @@
     left,
 ):
     copies = [
-        pltpu.make_async_copy(u_far, u, arrived.at[0]),
-        pltpu.make_async_copy(q_far, q, arrived.at[1]),
+        pltpu.make_async_copy(u0_far, u0, arrived.at[0]),
+        pltpu.make_async_copy(u1_far, u1, arrived.at[1]),
+        pltpu.make_async_copy(q_far, q, arrived.at[2]),
     ]
     for copy in copies:
         copy.start()
@@ -491,11 +494,10 @@
         for g in range(2):
             brows = slice(B * g, B * g + B)
             qrows = slice(48 * g, 48 * g + 48)
-            us = jnp.concatenate([u[g, :, x, :], u[g, :, x + 1, :]], axis=1)
             made = combination(
                 coeffs[g],
                 jnp.concatenate(
-                    [us, pair((f0, f1)[g], x), pair(q, x, qrows), pair(t, x, brows)], axis=0
+                    [pair((u0, u1)[g], x, slice(0, K)), pair((f0, f1)[g], x), pair(q, x, qrows), pair(t, x, brows)], axis=0
                 ),
             )
             for i in range(2):
@@ -580,9 +582,9 @@
     u = recycle.reshape(2, K, NX, NY)
     b = right_sides.reshape(2 * B, NX, NY)
     scalars = (shift_table, shift_index)
-    back = jnp.concatenate([u[1], b], axis=0)
+    back = jnp.transpose(jnp.concatenate([u[1], b], axis=0), (1, 0, 2))
     back_sides = beside(back)
-    front = u[0]
+    front = jnp.transpose(u[0], (1, 0, 2))
     front_across, front_sibling = beside(front)
     f1, b, b1 = call(
         back_kernel,
@@ -594,7 +596,8 @@
         med,
     )
     f1_sides = beside(f1)
-    front_across, b1 = lax.optimization_barrier((front_across, b1))
+    front_across, f1, f1_sibling = lax.optimization_barrier((front_across, f1, f1_sides[1]))
+    f1_sides = (f1_sides[0], f1_sibling)
     (f0,) = call(
         front_kernel, [(NX, K, NY)], 2, *scalars, front, front_across, front_sibling, med
     )
@@ -614,6 +617,7 @@
         med,
     )
     field_sides = beside(fields)
+    gram, b1_sides = lax.optimization_barrier((gram, b1_sides))
     q, last, coef, shift = call(
         krylov_kernel,
         [(NX, 96, NY), (NX, 2 * B, NY), (2, 96, 128), (16, 128)],
@@ -635,7 +639,7 @@
         moment_kernel, [(NX, 2 * B, NY), (K, 128)], 0, last, *last_sides, basis_gram, med, shift
     )
     solution, residue = finish(
-        scalars, (everyone(gram), coef, shift, f0, f1, t), (u, q), (2 * B, NX, NY)
+        scalars, (everyone(gram), coef, shift, f0, f1, t), (front, back, q), (2 * B, NX, NY)
     )
     return solution.reshape(right_sides.shape), residue.reshape(right_sides.shape)
 

time: 169 us -> 149 us (0.88)
  waiting for transfers between devices: 47.6 us -> 31.7 us
  blocking collectives: 46.8 us -> 60.4 us
  starting transfers between devices: 43 us -> 34.1 us
  Pallas kernels: 25.5 us -> 19.4 us
  local copies, waits for them, and re-layouts: 4.12 us -> 1.98 us
    all_to_all x1 -> x2, blocking collectives: 12.9 us -> 33.9 us  [everyone(): return lax.all_to_all(spread, near, 0, 0, tiled=True)]
    all_to_all x1 -> x0, starting transfers between devices: 11.6 us -> none  [everyone(): return lax.all_to_all(spread, near, 0, 0, tiled=True)]
    all_to_all x1 -> x0, waiting for transfers between devices: 9.18 us -> none  [everyone(): return lax.all_to_all(spread, near, 0, 0, tiled=True)]
    all_to_all x2, blocking collectives: 33.9 us -> 26.5 us  [everyone(): parts = lax.all_to_all(spread, far, 0, 0, tiled=True)]
    ppermute x7, waiting for transfers between devices: 36 us -> 29.4 us  [beside(): across = lax.ppermute(values, GRID, edges + [(j, i) for i, j in edges])]
    pallas_call x11, Pallas kernels: 17.5 us -> 12 us  [call(): pl.pallas_call(kernel, out_shape=[pltpu.VMEM(s, F32) for s in shapes], in...]
    ppermute x7, starting transfers between devices: 29.9 us -> 32.3 us  [beside(): across = lax.ppermute(values, GRID, edges + [(j, i) for i, j in edges])]
  transfers between devices with their start and end apart: 17 -> 16, of which waited for: 8 -> 6; matrix products, arithmetic and copies ran while one was open for 0% -> 0% of each run, Pallas kernels for 4% -> 5%
where the time goes in v3:
time: 149 us
  blocking collectives  60.4 us (41%)
  starting transfers between devices  34.1 us (23%)
  waiting for transfers between devices  31.7 us (21%)
  Pallas kernels  19.4 us (13%)
  local copies, waits for them, and re-layouts  1.98 us (1%)
    all_to_all x2, blocking collectives, everyone(): return lax.all_to_all(spread, near, 0, 0, tiled=True)  33.9 us
    ppermute x7, starting transfers between devices, beside(): across = lax.ppermute(values, GRID, edges + [(j, i) for i, j in edges])  32.3 us
    ppermute x7, waiting for transfers between devices, beside(): across = lax.ppermute(values, GRID, edges + [(j, i) for i, j in edges])  29.4 us
    all_to_all x2, blocking collectives, everyone(): parts = lax.all_to_all(spread, far, 0, 0, tiled=True)  26.5 us
    pallas_call x11, Pallas kernels, call(): pl.pallas_call(kernel, out_shape=[pltpu.VMEM(s, F32) for s in shapes], in...  12 us
    pallas_call x1, Pallas kernels, finish(): pl.pallas_call(finish_kernel, out_shape=[jax.ShapeDtypeStruct(shape, F32)...  7.39 us
  transfers between devices with their start and end apart: 16, of which 6 were waited for; matrix products, arithmetic and copies ran while one was open for 0% of the time, Pallas kernels for 5%

profile of v3, /device:TPU:8, one launch (start us, length us, event | category | flops | bytes accessed | tf_op | source)
XLA Modules:
  0.0 148.8 jit_solution(13620132645055442524)
XLA Ops:
  0.6 0.0 copy-start.3
  0.6 1.5 copy.17
  2.1 0.0 copy-done.3
  2.1 0.1 fusion
  2.2 0.2 copy.18
  2.4 0.0 copy-start
  2.4 0.0 copy-start.1
  2.4 0.0 copy-start.2
  2.5 0.1 maximum_bitcast_fusion.ub.u1_far
  2.6 0.1 collective-permute-start.2
  2.7 7.7 %collective-permute-start.1 = (f32[48,56,128]{2,1,0:T(8,128)S(1)}, f32[48,56,128]{2,1,0:T(8,128)S(1)}, u32[]{:S(2)}, u32[]{:S(2)}) collective-permute-start(f32[48,56,128]{2,1,0:T(8,128)S(1)} %maximum_bitcast_fusion.ub.u1_far), channel_id=1, source_target_pairs={{1,2},{3,4},{5,6},{7,8},{9,10},{11,12},{13,14},{15,16},{17,18},{19... | collective-permute-start | bytes 4128776 | tf_op jit(solution)/shard_map/ppermute | solution.py:575
  10.4 0.2 copy.19
  10.6 1.9 %collective-permute-start = (f32[48,24,128]{2,1,0:T(8,128)S(1)}, f32[48,24,128]{2,1,0:T(8,128)S(1)}, u32[]{:S(2)}, u32[]{:S(2)}) collective-permute-start(f32[48,24,128]{2,1,0:T(8,128)S(1)} %bitcast.20), channel_id=1, source_target_pairs={{1,2},{3,4},{5,6},{7,8},{9,10},{11,12},{13,14},{15,16},{17,18},{19... | collective-permute-start | bytes 1769480 | tf_op jit(solution)/shard_map/ppermute | solution.py:575
  12.5 0.0 collective-permute-done.2.sibling
  12.5 13.8 %collective-permute-done.1.across = f32[48,56,128]{2,1,0:T(8,128)S(1)} collective-permute-done((f32[48,56,128]{2,1,0:T(8,128)S(1)}, f32[48,56,128]{2,1,0:T(8,128)S(1)}, u32[]{:S(2)}, u32[]{:S(2)}) %collective-permute-start.1) | collective-permute-done | bytes 1376288 | tf_op jit(solution)/shard_map/ppermute | solution.py:575
  26.4 0.0 copy-done
  26.4 0.0 copy-done.1
  26.4 0.0 copy-done.2
  26.4 1.4 back_kernel.1
  27.8 0.1 collective-permute-start.3
  27.9 0.5 collective-permute-start.4
  28.4 5.7 %collective-permute-start.7 = (f32[48,24,128]{2,1,0:T(8,128)S(1)}, f32[48,24,128]{2,1,0:T(8,128)S(1)}, u32[]{:S(2)}, u32[]{:S(2)}) collective-permute-start(f32[48,24,128]{2,1,0:T(8,128)S(1)} %get-tuple-element.23.f1), channel_id=1, source_target_pairs={{1,2},{3,4},{5,6},{7,8},{9,10},{11,12},{13,14},{15,16},{17,18},{19... | collective-permute-start | bytes 1769480 | tf_op jit(solution)/shard_map/ppermute | solution.py:575
  34.1 0.0 collective-permute-done.across
  34.1 0.0 collective-permute-done.3.f1_sibling
  34.1 0.0 collective-permute-done.4.sibling
  34.2 0.9 front_kernel.1.f0
  35.1 0.1 collective-permute-start.6
  35.2 4.3 %collective-permute-start.5 = (f32[48,24,128]{2,1,0:T(8,128)S(1)}, f32[48,24,128]{2,1,0:T(8,128)S(1)}, u32[]{:S(2)}, u32[]{:S(2)}) collective-permute-start(f32[48,24,128]{2,1,0:T(8,128)S(1)} %front_kernel.1.f0), channel_id=1, source_target_pairs={{1,2},{3,4},{5,6},{7,8},{9,10},{11,12},{13,14},{15,16},{17,18},{19... | collective-permute-start | bytes 1769480 | tf_op jit(solution)/shard_map/ppermute | solution.py:575
  39.5 0.1 collective-permute-start.9
  39.6 3.4 %collective-permute-start.8 = (f32[48,32,128]{2,1,0:T(8,128)S(1)}, f32[48,32,128]{2,1,0:T(8,128)S(1)}, u32[]{:S(2)}, u32[]{:S(2)}) collective-permute-start(f32[48,32,128]{2,1,0:T(8,128)S(1)} %get-tuple-element.25.b1), channel_id=1, source_target_pairs={{1,2},{3,4},{5,6},{7,8},{9,10},{11,12},{13,14},{15,16},{17,18},{19... | collective-permute-start | bytes 2359304 | tf_op jit(solution)/shard_map/ppermute | solution.py:575
  43.0 1.1 first_gram_kernel.1.first
  44.1 0.0 collective-permute-done.7.f1_across
  44.1 0.0 collective-permute-done.6.f0_sibling
  44.1 4.4 %collective-permute-done.5.f0_across = f32[48,24,128]{2,1,0:T(8,128)S(1)} collective-permute-done((f32[48,24,128]{2,1,0:T(8,128)S(1)}, f32[48,24,128]{2,1,0:T(8,128)S(1)}, u32[]{:S(2)}, u32[]{:S(2)}) %collective-permute-start.5) | collective-permute-done | bytes 589856 | tf_op jit(solution)/shard_map/ppermute | solution.py:575
  48.5 1.5 second_gram_kernel.1
  50.0 0.1 collective-permute-start.12
  50.1 5.3 %collective-permute-start.11 = (f32[48,48,128]{2,1,0:T(8,128)S(1)}, f32[48,48,128]{2,1,0:T(8,128)S(1)}, u32[]{:S(2)}, u32[]{:S(2)}) collective-permute-start(f32[48,48,128]{2,1,0:T(8,128)S(1)} %get-tuple-element.31.fields), channel_id=1, source_target_pairs={{1,2},{3,4},{5,6},{7,8},{9,10},{11,12},{13,14},{15,16},{17,18},{19... | collective-permute-start | bytes 3538952 | tf_op jit(solution)/shard_map/ppermute | solution.py:575
  55.3 0.0 collective-permute-done.9.b1_sibling
  55.3 1.6 %collective-permute-done.8.b1_across = f32[48,32,128]{2,1,0:T(8,128)S(1)} collective-permute-done((f32[48,32,128]{2,1,0:T(8,128)S(1)}, f32[48,32,128]{2,1,0:T(8,128)S(1)}, u32[]{:S(2)}, u32[]{:S(2)}) %collective-permute-start.8) | collective-permute-done | bytes 786464 | tf_op jit(solution)/shard_map/ppermute | solution.py:575
  56.9 0.0 collective-permute-start.10
  56.9 1.2 collective-permute-done.10.two
  58.1 15.1 %all_to_all.20.parts = f32[8,48,128]{2,1,0:T(8,128)S(1)} all-to-all(f32[8,48,128]{2,1,0:T(8,128)S(1)} %add_kernel.2), channel_id=1, replica_groups=mesh['grid_0'=4,'grid_1'=4,'grid_2'=8,'grid_3'=2] {'grid_2'}, dimensions={0} | all-to-all | bytes 393216 | tf_op jit(solution)/shard_map/all_to_all | solution.py:567
  73.3 20.9 %all_to_all.21.grams = f32[16,48,128]{2,1,0:T(8,128)S(1)} all-to-all(f32[16,48,128]{2,1,0:T(8,128)S(1)} %respread_kernel.2), channel_id=1, replica_groups=mesh['grid_0'=4,'grid_1'=4,'grid_2'=8,'grid_3'=2] {'grid_0','grid_1'}, dimensions={0} | all-to-all | bytes 786432 | tf_op jit(solution)/shard_map/all_to_all | solution.py:569
  94.2 0.0 collective-permute-done.12.fields_sibling
  94.2 0.0 collective-permute-done.11.fields_across
  94.2 4.2 %krylov_kernel.1 = (f32[48,96,128]{2,1,0:T(8,128)S(1)}, f32[48,32,128]{2,1,0:T(8,128)S(1)}, f32[2,96,128]{2,1,0:T(8,128)S(1)}, f32[16,128]{1,0:T(8,128)S(1)}) custom-call(f32[16,48,128]{2,1,0:T(8,128)S(1)} %all_to_all.21.grams, f32[48,24,128]{2,1,0:T(8,128)S(1)} %front_kernel.1.f0, f32[48,24,128]{2,1,0:T(8,128)S(1)} %get-tuple-element.23.f1, ...), custom_call_target="tpu_custom_call" | custom-call | tf_op jit(solution)/shard_map/krylov_kernel/pallas_call | solution.py:525
  98.4 0.7 collective-permute-start.14
  99.1 4.0 %collective-permute-start.13 = (f32[48,32,128]{2,1,0:T(8,128)S(1)}, f32[48,32,128]{2,1,0:T(8,128)S(1)}, u32[]{:S(2)}, u32[]{:S(2)}) collective-permute-start(f32[48,32,128]{2,1,0:T(8,128)S(1)} %get-tuple-element.32.last), channel_id=1, source_target_pairs={{1,2},{3,4},{5,6},{7,8},{9,10},{11,12},{13,14},{15,16},{17,18},{19... | collective-permute-start | bytes 2359304 | tf_op jit(solution)/shard_map/ppermute | solution.py:575
  103.1 1.8 %basis_gram_kernel.1.basis_gram = f32[2,48,128]{2,1,0:T(8,128)S(1)} custom-call(f32[48,96,128]{2,1,0:T(8,128)S(1)} %get-tuple-element.33.q.q_far, f32[48,48,128]{2,1,0:T(8,128)S(1)} %get-tuple-element.31.fields), custom_call_target="tpu_custom_call" | custom-call | tf_op jit(solution)/shard_map/basis_gram_kernel/pallas_call | solution.py:525
  104.9 0.0 collective-permute-done.14.last_after
  104.9 9.5 %collective-permute-done.13.last_before = f32[48,32,128]{2,1,0:T(8,128)S(1)} collective-permute-done((f32[48,32,128]{2,1,0:T(8,128)S(1)}, f32[48,32,128]{2,1,0:T(8,128)S(1)}, u32[]{:S(2)}, u32[]{:S(2)}) %collective-permute-start.13) | collective-permute-done | bytes 786464 | tf_op jit(solution)/shard_map/ppermute | solution.py:575
  114.5 1.1 moment_kernel.1
  115.5 0.1 collective-permute-start.15
  115.6 1.2 collective-permute-done.15.two
  116.8 11.4 %all_to_all.22.parts = f32[8,24,128]{2,1,0:T(8,128)S(1)} all-to-all(f32[8,24,128]{2,1,0:T(8,128)S(1)} %add_kernel.3), channel_id=1, replica_groups=mesh['grid_0'=4,'grid_1'=4,'grid_2'=8,'grid_3'=2] {'grid_2'}, dimensions={0} | all-to-all | bytes 196608 | tf_op jit(solution)/shard_map/all_to_all | solution.py:567
  128.2 13.1 %all_to_all.23.moments = f32[16,24,128]{2,1,0:T(8,128)S(1)} all-to-all(f32[16,24,128]{2,1,0:T(8,128)S(1)} %respread_kernel.3), channel_id=1, replica_groups=mesh['grid_0'=4,'grid_1'=4,'grid_2'=8,'grid_3'=2] {'grid_0','grid_1'}, dimensions={0} | all-to-all | bytes 393216 | tf_op jit(solution)/shard_map/all_to_all | solution.py:569
  141.2 7.4 %finish_kernel.1 = (f32[32,48,128]{2,1,0:T(8,128)}, f32[32,48,128]{2,1,0:T(8,128)}) custom-call(f32[8]{0:T(128)S(1)} %copy-done.1, s32[2]{0:T(128)S(1)} %copy-done.2, f32[16,24,128]{2,1,0:T(8,128)S(1)} %all_to_all.23.moments, f32[2,96,128]{2,1,0:T(8,128)S(1)} %get-tuple-element.36.coef, f32[16,128]{1,0:T(8,128)S(1)} %get-tuple-element.34.shift, ...), custom_call_target="tpu_custom_call" | custom-call | tf_op jit(solution)/shard_map/finish_kernel/pallas_call | solution.py:538
  (4 shorter events, 0.1 us)
Async XLA Ops:
  0.6 1.5 %copy-start.3 = (f32[2,24,1,48,128]{4,3,2,1,0:T(8,128)S(1)}, f32[2,24,1,48,128]{4,3,2,1,0:T(8,128)}, u32[]{:S(2)}) copy-start(f32[2,24,1,48,128]{4,3,2,1,0:T(8,128)} %param.6) | copy-start | bytes 3538948
  2.4 24.0 %copy-start = (f32[1,48,128]{2,1,0:T(8,128)S(1)}, f32[1,48,128]{2,1,0:T(8,128)}, u32[]{:S(2)}) copy-start(f32[1,48,128]{2,1,0:T(8,128)} %param.7) | copy-start | bytes 73732
  2.4 24.0 %copy-start.1 = (f32[8]{0:T(128)S(1)}, f32[8]{0:T(128)}, u32[]{:S(2)}) copy-start(f32[8]{0:T(128)} %table.5) | copy-start | bytes 100
  2.4 23.9 %copy-start.2 = (s32[2]{0:T(128)S(1)}, s32[2]{0:T(128)}, u32[]{:S(2)}) copy-start(s32[2]{0:T(128)} %index.5) | copy-start | bytes 28
  2.6 10.0 %collective-permute-start.2 = (f32[48,56,128]{2,1,0:T(8,128)S(1)}, f32[48,56,128]{2,1,0:T(8,128)S(1)}, u32[]{:S(2)}, u32[]{:S(2)}) collective-permute-start(f32[48,56,128]{2,1,0:T(8,128)S(1)} %maximum_bitcast_fusion.ub.u1_far), channel_id=1, source_target_pairs={{0,1},{1,0},{2,3},{3,2},{4,5},{5,4},{6,7},{7,6},{8,9},{9,8},{10,11... | collective-permute-start | bytes 4128776 | tf_op jit(solution)/shard_map/ppermute | solution.py:576
  2.7 23.7 %collective-permute-start.1 = (f32[48,56,128]{2,1,0:T(8,128)S(1)}, f32[48,56,128]{2,1,0:T(8,128)S(1)}, u32[]{:S(2)}, u32[]{:S(2)}) collective-permute-start(f32[48,56,128]{2,1,0:T(8,128)S(1)} %maximum_bitcast_fusion.ub.u1_far), channel_id=1, source_target_pairs={{1,2},{3,4},{5,6},{7,8},{9,10},{11,12},{13,14},{15,16},{17,18},{19... | collective-permute-start | bytes 4128776 | tf_op jit(solution)/shard_map/ppermute | solution.py:575
  10.6 23.5 %collective-permute-start = (f32[48,24,128]{2,1,0:T(8,128)S(1)}, f32[48,24,128]{2,1,0:T(8,128)S(1)}, u32[]{:S(2)}, u32[]{:S(2)}) collective-permute-start(f32[48,24,128]{2,1,0:T(8,128)S(1)} %bitcast.20), channel_id=1, source_target_pairs={{1,2},{3,4},{5,6},{7,8},{9,10},{11,12},{13,14},{15,16},{17,18},{19... | collective-permute-start | bytes 1769480 | tf_op jit(solution)/shard_map/ppermute | solution.py:575
  27.8 6.4 %collective-permute-start.3 = (f32[48,24,128]{2,1,0:T(8,128)S(1)}, f32[48,24,128]{2,1,0:T(8,128)S(1)}, u32[]{:S(2)}, u32[]{:S(2)}) collective-permute-start(f32[48,24,128]{2,1,0:T(8,128)S(1)} %get-tuple-element.23.f1), channel_id=1, source_target_pairs={{0,1},{1,0},{2,3},{3,2},{4,5},{5,4},{6,7},{7,6},{8,9},{9,8},{10,11... | collective-permute-start | bytes 1769480 | tf_op jit(solution)/shard_map/ppermute | solution.py:576
  27.9 6.3 %collective-permute-start.4 = (f32[48,24,128]{2,1,0:T(8,128)S(1)}, f32[48,24,128]{2,1,0:T(8,128)S(1)}, u32[]{:S(2)}, u32[]{:S(2)}) collective-permute-start(f32[48,24,128]{2,1,0:T(8,128)S(1)} %bitcast.21), channel_id=1, source_target_pairs={{0,1},{1,0},{2,3},{3,2},{4,5},{5,4},{6,7},{7,6},{8,9},{9,8},{10,11... | collective-permute-start | bytes 1769480 | tf_op jit(solution)/shard_map/ppermute | solution.py:576
  28.4 15.7 %collective-permute-start.7 = (f32[48,24,128]{2,1,0:T(8,128)S(1)}, f32[48,24,128]{2,1,0:T(8,128)S(1)}, u32[]{:S(2)}, u32[]{:S(2)}) collective-permute-start(f32[48,24,128]{2,1,0:T(8,128)S(1)} %get-tuple-element.23.f1), channel_id=1, source_target_pairs={{1,2},{3,4},{5,6},{7,8},{9,10},{11,12},{13,14},{15,16},{17,18},{19... | collective-permute-start | bytes 1769480 | tf_op jit(solution)/shard_map/ppermute | solution.py:575
  35.1 9.0 %collective-permute-start.6 = (f32[48,24,128]{2,1,0:T(8,128)S(1)}, f32[48,24,128]{2,1,0:T(8,128)S(1)}, u32[]{:S(2)}, u32[]{:S(2)}) collective-permute-start(f32[48,24,128]{2,1,0:T(8,128)S(1)} %front_kernel.1.f0), channel_id=1, source_target_pairs={{0,1},{1,0},{2,3},{3,2},{4,5},{5,4},{6,7},{7,6},{8,9},{9,8},{10,11... | collective-permute-start | bytes 1769480 | tf_op jit(solution)/shard_map/ppermute | solution.py:576
  35.2 13.3 %collective-permute-start.5 = (f32[48,24,128]{2,1,0:T(8,128)S(1)}, f32[48,24,128]{2,1,0:T(8,128)S(1)}, u32[]{:S(2)}, u32[]{:S(2)}) collective-permute-start(f32[48,24,128]{2,1,0:T(8,128)S(1)} %front_kernel.1.f0), channel_id=1, source_target_pairs={{1,2},{3,4},{5,6},{7,8},{9,10},{11,12},{13,14},{15,16},{17,18},{19... | collective-permute-start | bytes 1769480 | tf_op jit(solution)/shard_map/ppermute | solution.py:575
  39.5 15.8 %collective-permute-start.9 = (f32[48,32,128]{2,1,0:T(8,128)S(1)}, f32[48,32,128]{2,1,0:T(8,128)S(1)}, u32[]{:S(2)}, u32[]{:S(2)}) collective-permute-start(f32[48,32,128]{2,1,0:T(8,128)S(1)} %get-tuple-element.25.b1), channel_id=1, source_target_pairs={{0,1},{1,0},{2,3},{3,2},{4,5},{5,4},{6,7},{7,6},{8,9},{9,8},{10,11... | collective-permute-start | bytes 2359304 | tf_op jit(solution)/shard_map/ppermute | solution.py:576
  39.6 17.3 %collective-permute-start.8 = (f32[48,32,128]{2,1,0:T(8,128)S(1)}, f32[48,32,128]{2,1,0:T(8,128)S(1)}, u32[]{:S(2)}, u32[]{:S(2)}) collective-permute-start(f32[48,32,128]{2,1,0:T(8,128)S(1)} %get-tuple-element.25.b1), channel_id=1, source_target_pairs={{1,2},{3,4},{5,6},{7,8},{9,10},{11,12},{13,14},{15,16},{17,18},{19... | collective-permute-start | bytes 2359304 | tf_op jit(solution)/shard_map/ppermute | solution.py:575
  50.0 44.2 %collective-permute-start.12 = (f32[48,48,128]{2,1,0:T(8,128)S(1)}, f32[48,48,128]{2,1,0:T(8,128)S(1)}, u32[]{:S(2)}, u32[]{:S(2)}) collective-permute-start(f32[48,48,128]{2,1,0:T(8,128)S(1)} %get-tuple-element.31.fields), channel_id=1, source_target_pairs={{0,1},{1,0},{2,3},{3,2},{4,5},{5,4},{6,7},{7,6},{8,9},{9,8},{10,11... | collective-permute-start | bytes 3538952 | tf_op jit(solution)/shard_map/ppermute | solution.py:576
  50.1 44.1 %collective-permute-start.11 = (f32[48,48,128]{2,1,0:T(8,128)S(1)}, f32[48,48,128]{2,1,0:T(8,128)S(1)}, u32[]{:S(2)}, u32[]{:S(2)}) collective-permute-start(f32[48,48,128]{2,1,0:T(8,128)S(1)} %get-tuple-element.31.fields), channel_id=1, source_target_pairs={{1,2},{3,4},{5,6},{7,8},{9,10},{11,12},{13,14},{15,16},{17,18},{19... | collective-permute-start | bytes 3538952 | tf_op jit(solution)/shard_map/ppermute | solution.py:575
  56.9 1.2 collective-permute-start.10
  98.4 6.5 %collective-permute-start.14 = (f32[48,32,128]{2,1,0:T(8,128)S(1)}, f32[48,32,128]{2,1,0:T(8,128)S(1)}, u32[]{:S(2)}, u32[]{:S(2)}) collective-permute-start(f32[48,32,128]{2,1,0:T(8,128)S(1)} %get-tuple-element.32.last), channel_id=1, source_target_pairs={{0,1},{1,0},{2,3},{3,2},{4,5},{5,4},{6,7},{7,6},{8,9},{9,8},{10,11... | collective-permute-start | bytes 2359304 | tf_op jit(solution)/shard_map/ppermute | solution.py:576
  99.1 15.4 %collective-permute-start.13 = (f32[48,32,128]{2,1,0:T(8,128)S(1)}, f32[48,32,128]{2,1,0:T(8,128)S(1)}, u32[]{:S(2)}, u32[]{:S(2)}) collective-permute-start(f32[48,32,128]{2,1,0:T(8,128)S(1)} %get-tuple-element.32.last), channel_id=1, source_target_pairs={{1,2},{3,4},{5,6},{7,8},{9,10},{11,12},{13,14},{15,16},{17,18},{19... | collective-permute-start | bytes 2359304 | tf_op jit(solution)/shard_map/ppermute | solution.py:575
  115.5 1.3 collective-permute-start.15

commit v4 on v3

--- a/solution.py
+++ b/solution.py
@@ -191,35 +191,24 @@
     return lambda x: ref[x]
 
 
-def second_gram_kernel(
-    f0, f0_across, f0_sibling, f1, f1_across, f1_sibling, b1, first, medium, fields_out, gram_out
-):
+def next_kernel(f0, f0_across, f0_sibling, f1, f1_across, f1_sibling, medium, fields_out):
+    for g, (own, across, sibling) in enumerate(
+        ((f0, f0_across, f0_sibling), (f1, f1_across, f1_sibling))
+    ):
+        made = stencil(
+            lambda x: medium[x : x + 1, :] - SHIFT, rows_of(own), rows_of(across), rows_of(sibling)
+        )
+        for x in range(NX):
+            fields_out[x, K * g : K * g + K] = made(x)
+
+
+def second_gram_kernel(f0, f1, fields, b1, first, gram_out):
     total = jnp.zeros((2 * K, 128), F32)
-    made = [
-        stencil(
-            lambda x: medium[x : x + 1, :] - SHIFT, rows_of(own), rows_of(across), rows_of(sibling)
-        )
-        for own, across, sibling in ((f0, f0_across, f0_sibling), (f1, f1_across, f1_sibling))
-    ]
     for x in range(0, NX, 2):
-        nexts = []
-        for g in range(2):
-            ends = [made[g](x), made[g](x + 1)]
-            for i in range(2):
-                fields_out[x + i, K * g : K * g + K] = ends[i]
-            nexts.append(jnp.concatenate(ends, axis=1))
+        nexts = pair(fields, x)
         b1_pair = pair(b1, x)
-        right = [
-            pair(f0, x),
-            nexts[0],
-            b1_pair[:B],
-            pair(f1, x),
-            nexts[1],
-            b1_pair[B:],
-        ]
-        total = total + row_products(
-            jnp.concatenate(nexts, axis=0), jnp.concatenate(right, axis=0)
-        )
+        right = [pair(f0, x), nexts[:K], b1_pair[:B], pair(f1, x), nexts[K:], b1_pair[B:]]
+        total = total + row_products(nexts, jnp.concatenate(right, axis=0))
     lane = iota((K, 128), 1)
     gram_out[:K] = first[...]
     gram_out[K:] = jnp.where(lane < 64, total[:K], total[K:])
@@ -604,19 +593,9 @@
     f0_sides = beside(f0)
     b1_sides = beside(b1)
     (first,) = call(first_gram_kernel, [(K, 128)], 0, f0, f1, b, b1)
-    fields, gram = call(
-        second_gram_kernel,
-        [(NX, 2 * K, NY), (2 * K, 128)],
-        0,
-        f0,
-        *f0_sides,
-        f1,
-        *f1_sides,
-        b1,
-        first,
-        med,
-    )
+    (fields,) = call(next_kernel, [(NX, 2 * K, NY)], 0, f0, *f0_sides, f1, *f1_sides, med)
     field_sides = beside(fields)
+    (gram,) = call(second_gram_kernel, [(2 * K, 128)], 0, f0, f1, fields, b1, first)
     gram, b1_sides = lax.optimization_barrier((gram, b1_sides))
     q, last, coef, shift = call(
         krylov_kernel,

time: 149 us -> 149 us (level)
  starting transfers between devices: 34.1 us -> 32.2 us
    pallas_call x11 -> x12, Pallas kernels: 12 us -> 12.5 us  [call(): pl.pallas_call(kernel, out_shape=[pltpu.VMEM(s, F32) for s in shapes], in...]
where the time goes in v4:
time: 149 us
  blocking collectives  60.6 us (41%)
  waiting for transfers between devices  32.8 us (22%)
  starting transfers between devices  32.2 us (22%)
  Pallas kernels  19.8 us (13%)
  local copies, waits for them, and re-layouts  1.98 us (1%)
    all_to_all x2, blocking collectives, everyone(): return lax.all_to_all(spread, near, 0, 0, tiled=True)  34.3 us
    ppermute x7, starting transfers between devices, beside(): across = lax.ppermute(values, GRID, edges + [(j, i) for i, j in edges])  30.9 us
    ppermute x7, waiting for transfers between devices, beside(): across = lax.ppermute(values, GRID, edges + [(j, i) for i, j in edges])  30.4 us
    all_to_all x2, blocking collectives, everyone(): parts = lax.all_to_all(spread, far, 0, 0, tiled=True)  26.3 us
    pallas_call x12, Pallas kernels, call(): pl.pallas_call(kernel, out_shape=[pltpu.VMEM(s, F32) for s in shapes], in...  12.5 us
    pallas_call x1, Pallas kernels, finish(): pl.pallas_call(finish_kernel, out_shape=[jax.ShapeDtypeStruct(shape, F32)...  7.39 us
  transfers between devices with their start and end apart: 16, of which 6 were waited for; matrix products, arithmetic and copies ran while one was open for 0% of the time, Pallas kernels for 5%

profile of v4, /device:TPU:8, one launch (start us, length us, event | category | flops | bytes accessed | tf_op | source)
XLA Modules:
  0.0 148.6 jit_solution(9353056909834544402)
XLA Ops:
  0.6 0.0 copy-start.3
  0.6 1.5 copy.17
  2.1 0.0 copy-done.3
  2.1 0.1 fusion
  2.2 0.2 copy.18
  2.4 0.0 copy-start
  2.4 0.0 copy-start.1
  2.4 0.0 copy-start.2
  2.5 0.1 maximum_bitcast_fusion.ub.u1_far
  2.6 0.1 collective-permute-start.2
  2.7 7.7 %collective-permute-start.1 = (f32[48,56,128]{2,1,0:T(8,128)S(1)}, f32[48,56,128]{2,1,0:T(8,128)S(1)}, u32[]{:S(2)}, u32[]{:S(2)}) collective-permute-start(f32[48,56,128]{2,1,0:T(8,128)S(1)} %maximum_bitcast_fusion.ub.u1_far), channel_id=1, source_target_pairs={{1,2},{3,4},{5,6},{7,8},{9,10},{11,12},{13,14},{15,16},{17,18},{19... | collective-permute-start | bytes 4128776 | tf_op jit(solution)/shard_map/ppermute | solution.py:564
  10.4 0.2 copy.19
  10.6 1.9 %collective-permute-start = (f32[48,24,128]{2,1,0:T(8,128)S(1)}, f32[48,24,128]{2,1,0:T(8,128)S(1)}, u32[]{:S(2)}, u32[]{:S(2)}) collective-permute-start(f32[48,24,128]{2,1,0:T(8,128)S(1)} %bitcast.20), channel_id=1, source_target_pairs={{1,2},{3,4},{5,6},{7,8},{9,10},{11,12},{13,14},{15,16},{17,18},{19... | collective-permute-start | bytes 1769480 | tf_op jit(solution)/shard_map/ppermute | solution.py:564
  12.5 0.0 collective-permute-done.2.sibling
  12.5 13.8 %collective-permute-done.1.across = f32[48,56,128]{2,1,0:T(8,128)S(1)} collective-permute-done((f32[48,56,128]{2,1,0:T(8,128)S(1)}, f32[48,56,128]{2,1,0:T(8,128)S(1)}, u32[]{:S(2)}, u32[]{:S(2)}) %collective-permute-start.1) | collective-permute-done | bytes 1376288 | tf_op jit(solution)/shard_map/ppermute | solution.py:564
  26.4 0.0 copy-done
  26.4 0.0 copy-done.1
  26.4 0.0 copy-done.2
  26.4 1.4 back_kernel.1
  27.8 0.1 collective-permute-start.3
  27.9 0.5 collective-permute-start.4
  28.4 5.7 %collective-permute-start.7 = (f32[48,24,128]{2,1,0:T(8,128)S(1)}, f32[48,24,128]{2,1,0:T(8,128)S(1)}, u32[]{:S(2)}, u32[]{:S(2)}) collective-permute-start(f32[48,24,128]{2,1,0:T(8,128)S(1)} %get-tuple-element.21.f1), channel_id=1, source_target_pairs={{1,2},{3,4},{5,6},{7,8},{9,10},{11,12},{13,14},{15,16},{17,18},{19... | collective-permute-start | bytes 1769480 | tf_op jit(solution)/shard_map/ppermute | solution.py:564
  34.1 0.0 collective-permute-done.across
  34.2 0.0 collective-permute-done.3.f1_sibling
  34.2 0.0 collective-permute-done.4.sibling
  34.2 0.9 front_kernel.1.f0
  35.1 0.1 collective-permute-start.6
  35.2 4.3 %collective-permute-start.5 = (f32[48,24,128]{2,1,0:T(8,128)S(1)}, f32[48,24,128]{2,1,0:T(8,128)S(1)}, u32[]{:S(2)}, u32[]{:S(2)}) collective-permute-start(f32[48,24,128]{2,1,0:T(8,128)S(1)} %front_kernel.1.f0), channel_id=1, source_target_pairs={{1,2},{3,4},{5,6},{7,8},{9,10},{11,12},{13,14},{15,16},{17,18},{19... | collective-permute-start | bytes 1769480 | tf_op jit(solution)/shard_map/ppermute | solution.py:564
  39.5 0.1 collective-permute-start.9
  39.6 3.4 %collective-permute-start.8 = (f32[48,32,128]{2,1,0:T(8,128)S(1)}, f32[48,32,128]{2,1,0:T(8,128)S(1)}, u32[]{:S(2)}, u32[]{:S(2)}) collective-permute-start(f32[48,32,128]{2,1,0:T(8,128)S(1)} %get-tuple-element.23.b1), channel_id=1, source_target_pairs={{1,2},{3,4},{5,6},{7,8},{9,10},{11,12},{13,14},{15,16},{17,18},{19... | collective-permute-start | bytes 2359304 | tf_op jit(solution)/shard_map/ppermute | solution.py:564
  43.0 0.0 collective-permute-done.7.f1_across
  43.0 0.0 collective-permute-done.6.f0_sibling
  43.0 5.5 %collective-permute-done.5.f0_across = f32[48,24,128]{2,1,0:T(8,128)S(1)} collective-permute-done((f32[48,24,128]{2,1,0:T(8,128)S(1)}, f32[48,24,128]{2,1,0:T(8,128)S(1)}, u32[]{:S(2)}, u32[]{:S(2)}) %collective-permute-start.5) | collective-permute-done | bytes 589856 | tf_op jit(solution)/shard_map/ppermute | solution.py:564
  48.5 0.7 next_kernel.1.fields
  49.2 0.1 collective-permute-start.12
  49.3 5.2 %collective-permute-start.11 = (f32[48,48,128]{2,1,0:T(8,128)S(1)}, f32[48,48,128]{2,1,0:T(8,128)S(1)}, u32[]{:S(2)}, u32[]{:S(2)}) collective-permute-start(f32[48,48,128]{2,1,0:T(8,128)S(1)} %next_kernel.1.fields), channel_id=1, source_target_pairs={{1,2},{3,4},{5,6},{7,8},{9,10},{11,12},{13,14},{15,16},{17,18},{19... | collective-permute-start | bytes 3538952 | tf_op jit(solution)/shard_map/ppermute | solution.py:564
  54.6 1.2 first_gram_kernel.1.first
  55.7 1.1 second_gram_kernel.1.one
  56.8 0.0 collective-permute-done.9.b1_sibling
  56.8 0.1 collective-permute-done.8.b1_across
  57.0 0.0 collective-permute-start.10
  57.0 1.2 collective-permute-done.10.two
  58.2 15.0 %all_to_all.20.parts = f32[8,48,128]{2,1,0:T(8,128)S(1)} all-to-all(f32[8,48,128]{2,1,0:T(8,128)S(1)} %add_kernel.2), channel_id=1, replica_groups=mesh['grid_0'=4,'grid_1'=4,'grid_2'=8,'grid_3'=2] {'grid_2'}, dimensions={0} | all-to-all | bytes 393216 | tf_op jit(solution)/shard_map/all_to_all | solution.py:556
  73.2 21.9 %all_to_all.21.grams = f32[16,48,128]{2,1,0:T(8,128)S(1)} all-to-all(f32[16,48,128]{2,1,0:T(8,128)S(1)} %respread_kernel.2), channel_id=1, replica_groups=mesh['grid_0'=4,'grid_1'=4,'grid_2'=8,'grid_3'=2] {'grid_0','grid_1'}, dimensions={0} | all-to-all | bytes 786432 | tf_op jit(solution)/shard_map/all_to_all | solution.py:558
  95.1 0.0 collective-permute-done.12.fields_sibling
  95.1 0.0 collective-permute-done.11.fields_across
  95.1 4.2 %krylov_kernel.1 = (f32[48,96,128]{2,1,0:T(8,128)S(1)}, f32[48,32,128]{2,1,0:T(8,128)S(1)}, f32[2,96,128]{2,1,0:T(8,128)S(1)}, f32[16,128]{1,0:T(8,128)S(1)}) custom-call(f32[16,48,128]{2,1,0:T(8,128)S(1)} %all_to_all.21.grams, f32[48,24,128]{2,1,0:T(8,128)S(1)} %front_kernel.1.f0, f32[48,24,128]{2,1,0:T(8,128)S(1)} %get-tuple-element.21.f1, ...), custom_call_target="tpu_custom_call" | custom-call | tf_op jit(solution)/shard_map/krylov_kernel/pallas_call | solution.py:514
  99.3 0.2 collective-permute-start.14
  99.5 2.6 %collective-permute-start.13 = (f32[48,32,128]{2,1,0:T(8,128)S(1)}, f32[48,32,128]{2,1,0:T(8,128)S(1)}, u32[]{:S(2)}, u32[]{:S(2)}) collective-permute-start(f32[48,32,128]{2,1,0:T(8,128)S(1)} %get-tuple-element.28.last), channel_id=1, source_target_pairs={{1,2},{3,4},{5,6},{7,8},{9,10},{11,12},{13,14},{15,16},{17,18},{19... | collective-permute-start | bytes 2359304 | tf_op jit(solution)/shard_map/ppermute | solution.py:564
  102.2 1.8 %basis_gram_kernel.1.basis_gram = f32[2,48,128]{2,1,0:T(8,128)S(1)} custom-call(f32[48,96,128]{2,1,0:T(8,128)S(1)} %get-tuple-element.29.q.q_far, f32[48,48,128]{2,1,0:T(8,128)S(1)} %next_kernel.1.fields), custom_call_target="tpu_custom_call" | custom-call | tf_op jit(solution)/shard_map/basis_gram_kernel/pallas_call | solution.py:514
  104.0 0.0 collective-permute-done.14.last_after
  104.0 10.9 %collective-permute-done.13.last_before = f32[48,32,128]{2,1,0:T(8,128)S(1)} collective-permute-done((f32[48,32,128]{2,1,0:T(8,128)S(1)}, f32[48,32,128]{2,1,0:T(8,128)S(1)}, u32[]{:S(2)}, u32[]{:S(2)}) %collective-permute-start.13) | collective-permute-done | bytes 786464 | tf_op jit(solution)/shard_map/ppermute | solution.py:564
  115.0 1.1 moment_kernel.1
  116.0 0.1 collective-permute-start.15
  116.1 1.2 collective-permute-done.15.two
  117.3 11.4 %all_to_all.22.parts = f32[8,24,128]{2,1,0:T(8,128)S(1)} all-to-all(f32[8,24,128]{2,1,0:T(8,128)S(1)} %add_kernel.3), channel_id=1, replica_groups=mesh['grid_0'=4,'grid_1'=4,'grid_2'=8,'grid_3'=2] {'grid_2'}, dimensions={0} | all-to-all | bytes 196608 | tf_op jit(solution)/shard_map/all_to_all | solution.py:556
  128.7 12.3 %all_to_all.23.moments = f32[16,24,128]{2,1,0:T(8,128)S(1)} all-to-all(f32[16,24,128]{2,1,0:T(8,128)S(1)} %respread_kernel.3), channel_id=1, replica_groups=mesh['grid_0'=4,'grid_1'=4,'grid_2'=8,'grid_3'=2] {'grid_0','grid_1'}, dimensions={0} | all-to-all | bytes 393216 | tf_op jit(solution)/shard_map/all_to_all | solution.py:558
  141.0 7.4 %finish_kernel.1 = (f32[32,48,128]{2,1,0:T(8,128)}, f32[32,48,128]{2,1,0:T(8,128)}) custom-call(f32[8]{0:T(128)S(1)} %copy-done.1, s32[2]{0:T(128)S(1)} %copy-done.2, f32[16,24,128]{2,1,0:T(8,128)S(1)} %all_to_all.23.moments, f32[2,96,128]{2,1,0:T(8,128)S(1)} %get-tuple-element.32.coef, f32[16,128]{1,0:T(8,128)S(1)} %get-tuple-element.30.shift, ...), custom_call_target="tpu_custom_call" | custom-call | tf_op jit(solution)/shard_map/finish_kernel/pallas_call | solution.py:527
  (4 shorter events, 0.1 us)
Async XLA Ops:
  0.6 1.5 %copy-start.3 = (f32[2,24,1,48,128]{4,3,2,1,0:T(8,128)S(1)}, f32[2,24,1,48,128]{4,3,2,1,0:T(8,128)}, u32[]{:S(2)}) copy-start(f32[2,24,1,48,128]{4,3,2,1,0:T(8,128)} %param.6) | copy-start | bytes 3538948
  2.4 24.0 %copy-start = (f32[1,48,128]{2,1,0:T(8,128)S(1)}, f32[1,48,128]{2,1,0:T(8,128)}, u32[]{:S(2)}) copy-start(f32[1,48,128]{2,1,0:T(8,128)} %param.7) | copy-start | bytes 73732
  2.4 24.0 %copy-start.1 = (f32[8]{0:T(128)S(1)}, f32[8]{0:T(128)}, u32[]{:S(2)}) copy-start(f32[8]{0:T(128)} %table.5) | copy-start | bytes 100
  2.4 23.9 %copy-start.2 = (s32[2]{0:T(128)S(1)}, s32[2]{0:T(128)}, u32[]{:S(2)}) copy-start(s32[2]{0:T(128)} %index.5) | copy-start | bytes 28
  2.6 10.0 %collective-permute-start.2 = (f32[48,56,128]{2,1,0:T(8,128)S(1)}, f32[48,56,128]{2,1,0:T(8,128)S(1)}, u32[]{:S(2)}, u32[]{:S(2)}) collective-permute-start(f32[48,56,128]{2,1,0:T(8,128)S(1)} %maximum_bitcast_fusion.ub.u1_far), channel_id=1, source_target_pairs={{0,1},{1,0},{2,3},{3,2},{4,5},{5,4},{6,7},{7,6},{8,9},{9,8},{10,11... | collective-permute-start | bytes 4128776 | tf_op jit(solution)/shard_map/ppermute | solution.py:565
  2.7 23.7 %collective-permute-start.1 = (f32[48,56,128]{2,1,0:T(8,128)S(1)}, f32[48,56,128]{2,1,0:T(8,128)S(1)}, u32[]{:S(2)}, u32[]{:S(2)}) collective-permute-start(f32[48,56,128]{2,1,0:T(8,128)S(1)} %maximum_bitcast_fusion.ub.u1_far), channel_id=1, source_target_pairs={{1,2},{3,4},{5,6},{7,8},{9,10},{11,12},{13,14},{15,16},{17,18},{19... | collective-permute-start | bytes 4128776 | tf_op jit(solution)/shard_map/ppermute | solution.py:564
  10.6 23.5 %collective-permute-start = (f32[48,24,128]{2,1,0:T(8,128)S(1)}, f32[48,24,128]{2,1,0:T(8,128)S(1)}, u32[]{:S(2)}, u32[]{:S(2)}) collective-permute-start(f32[48,24,128]{2,1,0:T(8,128)S(1)} %bitcast.20), channel_id=1, source_target_pairs={{1,2},{3,4},{5,6},{7,8},{9,10},{11,12},{13,14},{15,16},{17,18},{19... | collective-permute-start | bytes 1769480 | tf_op jit(solution)/shard_map/ppermute | solution.py:564
  27.8 6.4 %collective-permute-start.3 = (f32[48,24,128]{2,1,0:T(8,128)S(1)}, f32[48,24,128]{2,1,0:T(8,128)S(1)}, u32[]{:S(2)}, u32[]{:S(2)}) collective-permute-start(f32[48,24,128]{2,1,0:T(8,128)S(1)} %get-tuple-element.21.f1), channel_id=1, source_target_pairs={{0,1},{1,0},{2,3},{3,2},{4,5},{5,4},{6,7},{7,6},{8,9},{9,8},{10,11... | collective-permute-start | bytes 1769480 | tf_op jit(solution)/shard_map/ppermute | solution.py:565
  27.9 6.3 %collective-permute-start.4 = (f32[48,24,128]{2,1,0:T(8,128)S(1)}, f32[48,24,128]{2,1,0:T(8,128)S(1)}, u32[]{:S(2)}, u32[]{:S(2)}) collective-permute-start(f32[48,24,128]{2,1,0:T(8,128)S(1)} %bitcast.21), channel_id=1, source_target_pairs={{0,1},{1,0},{2,3},{3,2},{4,5},{5,4},{6,7},{7,6},{8,9},{9,8},{10,11... | collective-permute-start | bytes 1769480 | tf_op jit(solution)/shard_map/ppermute | solution.py:565
  28.4 14.6 %collective-permute-start.7 = (f32[48,24,128]{2,1,0:T(8,128)S(1)}, f32[48,24,128]{2,1,0:T(8,128)S(1)}, u32[]{:S(2)}, u32[]{:S(2)}) collective-permute-start(f32[48,24,128]{2,1,0:T(8,128)S(1)} %get-tuple-element.21.f1), channel_id=1, source_target_pairs={{1,2},{3,4},{5,6},{7,8},{9,10},{11,12},{13,14},{15,16},{17,18},{19... | collective-permute-start | bytes 1769480 | tf_op jit(solution)/shard_map/ppermute | solution.py:564
  35.1 7.9 %collective-permute-start.6 = (f32[48,24,128]{2,1,0:T(8,128)S(1)}, f32[48,24,128]{2,1,0:T(8,128)S(1)}, u32[]{:S(2)}, u32[]{:S(2)}) collective-permute-start(f32[48,24,128]{2,1,0:T(8,128)S(1)} %front_kernel.1.f0), channel_id=1, source_target_pairs={{0,1},{1,0},{2,3},{3,2},{4,5},{5,4},{6,7},{7,6},{8,9},{9,8},{10,11... | collective-permute-start | bytes 1769480 | tf_op jit(solution)/shard_map/ppermute | solution.py:565
  35.2 13.3 %collective-permute-start.5 = (f32[48,24,128]{2,1,0:T(8,128)S(1)}, f32[48,24,128]{2,1,0:T(8,128)S(1)}, u32[]{:S(2)}, u32[]{:S(2)}) collective-permute-start(f32[48,24,128]{2,1,0:T(8,128)S(1)} %front_kernel.1.f0), channel_id=1, source_target_pairs={{1,2},{3,4},{5,6},{7,8},{9,10},{11,12},{13,14},{15,16},{17,18},{19... | collective-permute-start | bytes 1769480 | tf_op jit(solution)/shard_map/ppermute | solution.py:564
  39.5 17.3 %collective-permute-start.9 = (f32[48,32,128]{2,1,0:T(8,128)S(1)}, f32[48,32,128]{2,1,0:T(8,128)S(1)}, u32[]{:S(2)}, u32[]{:S(2)}) collective-permute-start(f32[48,32,128]{2,1,0:T(8,128)S(1)} %get-tuple-element.23.b1), channel_id=1, source_target_pairs={{0,1},{1,0},{2,3},{3,2},{4,5},{5,4},{6,7},{7,6},{8,9},{9,8},{10,11... | collective-permute-start | bytes 2359304 | tf_op jit(solution)/shard_map/ppermute | solution.py:565
  39.6 17.4 %collective-permute-start.8 = (f32[48,32,128]{2,1,0:T(8,128)S(1)}, f32[48,32,128]{2,1,0:T(8,128)S(1)}, u32[]{:S(2)}, u32[]{:S(2)}) collective-permute-start(f32[48,32,128]{2,1,0:T(8,128)S(1)} %get-tuple-element.23.b1), channel_id=1, source_target_pairs={{1,2},{3,4},{5,6},{7,8},{9,10},{11,12},{13,14},{15,16},{17,18},{19... | collective-permute-start | bytes 2359304 | tf_op jit(solution)/shard_map/ppermute | solution.py:564
  49.2 45.9 %collective-permute-start.12 = (f32[48,48,128]{2,1,0:T(8,128)S(1)}, f32[48,48,128]{2,1,0:T(8,128)S(1)}, u32[]{:S(2)}, u32[]{:S(2)}) collective-permute-start(f32[48,48,128]{2,1,0:T(8,128)S(1)} %next_kernel.1.fields), channel_id=1, source_target_pairs={{0,1},{1,0},{2,3},{3,2},{4,5},{5,4},{6,7},{7,6},{8,9},{9,8},{10,11... | collective-permute-start | bytes 3538952 | tf_op jit(solution)/shard_map/ppermute | solution.py:565
  49.3 45.8 %collective-permute-start.11 = (f32[48,48,128]{2,1,0:T(8,128)S(1)}, f32[48,48,128]{2,1,0:T(8,128)S(1)}, u32[]{:S(2)}, u32[]{:S(2)}) collective-permute-start(f32[48,48,128]{2,1,0:T(8,128)S(1)} %next_kernel.1.fields), channel_id=1, source_target_pairs={{1,2},{3,4},{5,6},{7,8},{9,10},{11,12},{13,14},{15,16},{17,18},{19... | collective-permute-start | bytes 3538952 | tf_op jit(solution)/shard_map/ppermute | solution.py:564
  57.0 1.2 collective-permute-start.10
  99.3 4.7 %collective-permute-start.14 = (f32[48,32,128]{2,1,0:T(8,128)S(1)}, f32[48,32,128]{2,1,0:T(8,128)S(1)}, u32[]{:S(2)}, u32[]{:S(2)}) collective-permute-start(f32[48,32,128]{2,1,0:T(8,128)S(1)} %get-tuple-element.28.last), channel_id=1, source_target_pairs={{0,1},{1,0},{2,3},{3,2},{4,5},{5,4},{6,7},{7,6},{8,9},{9,8},{10,11... | collective-permute-start | bytes 2359304 | tf_op jit(solution)/shard_map/ppermute | solution.py:565
  99.5 15.4 %collective-permute-start.13 = (f32[48,32,128]{2,1,0:T(8,128)S(1)}, f32[48,32,128]{2,1,0:T(8,128)S(1)}, u32[]{:S(2)}, u32[]{:S(2)}) collective-permute-start(f32[48,32,128]{2,1,0:T(8,128)S(1)} %get-tuple-element.28.last), channel_id=1, source_target_pairs={{1,2},{3,4},{5,6},{7,8},{9,10},{11,12},{13,14},{15,16},{17,18},{19... | collective-permute-start | bytes 2359304 | tf_op jit(solution)/shard_map/ppermute | solution.py:564
  116.0 1.3 collective-permute-start.15

commit v5 on v4

--- a/solution.py
+++ b/solution.py
@@ -114,29 +114,29 @@
     return lambda x: ref[x, start : start + count]
 
 
-def stencil(diagonal, own, across, sibling):
+def stencil(diagonal, own, across, sibling, inside):
     def at(x):
-        return diagonal(x) * own(x) - neighbours(x, own, across(x), sibling(x))
+        return diagonal(x) * own(x) - neighbours(x, own, across(x) * inside[0], sibling(x))
 
     return at
 
 
-def applied(g, table, index, medium, own, across, sibling):
+def applied(g, table, index, inside, medium, own, across, sibling):
     base = 6.0 + table[index[g]]
-    return stencil(lambda x: medium[x : x + 1, :] + base, own, across, sibling)
-
-
-def front_kernel(table, index, u, across, sibling, medium, f_out):
+    return stencil(lambda x: medium[x : x + 1, :] + base, own, across, sibling, inside)
+
+
+def front_kernel(table, index, inside, u, across, sibling, medium, f_out):
     made = applied(
-        0, table, index, medium, planes(u, 0, K), planes(across, 0, K), planes(sibling, 0, K)
+        0, table, index, inside, medium, planes(u, 0, K), planes(across, 0, K), planes(sibling, 0, K)
     )
     for x in range(NX):
         f_out[x] = made(x)
 
 
-def back_kernel(table, index, ub, across, sibling, medium, f_out, b_out, b1_out):
+def back_kernel(table, index, inside, ub, across, sibling, medium, f_out, b_out, b1_out):
     made = applied(
-        1, table, index, medium, planes(ub, 0, K), planes(across, 0, K), planes(sibling, 0, K)
+        1, table, index, inside, medium, planes(ub, 0, K), planes(across, 0, K), planes(sibling, 0, K)
     )
     own = planes(ub, K, 2 * B)
     shifted = stencil(
@@ -144,6 +144,7 @@
         own,
         planes(across, K, 2 * B),
         planes(sibling, K, 2 * B),
+        inside,
     )
     for x in range(NX):
         f_out[x] = made(x)
@@ -191,12 +192,16 @@
     return lambda x: ref[x]
 
 
-def next_kernel(f0, f0_across, f0_sibling, f1, f1_across, f1_sibling, medium, fields_out):
+def next_kernel(inside, f0, f0_across, f0_sibling, f1, f1_across, f1_sibling, medium, fields_out):
     for g, (own, across, sibling) in enumerate(
         ((f0, f0_across, f0_sibling), (f1, f1_across, f1_sibling))
     ):
         made = stencil(
-            lambda x: medium[x : x + 1, :] - SHIFT, rows_of(own), rows_of(across), rows_of(sibling)
+            lambda x: medium[x : x + 1, :] - SHIFT,
+            rows_of(own),
+            rows_of(across),
+            rows_of(sibling),
+            inside,
         )
         for x in range(NX):
             fields_out[x, K * g : K * g + K] = made(x)
@@ -215,6 +220,7 @@
 
 
 def krylov_kernel(
+    inside,
     grams,
     f0,
     f1,
@@ -236,8 +242,10 @@
     def plain(x):
         return medium[x : x + 1, :] - SHIFT
 
-    next_f = stencil(plain, rows_of(fields), rows_of(fields_across), rows_of(fields_sibling))
-    next_b = stencil(plain, rows_of(b1), rows_of(b1_across), rows_of(b1_sibling))
+    next_f = stencil(
+        plain, rows_of(fields), rows_of(fields_across), rows_of(fields_sibling), inside
+    )
+    next_b = stencil(plain, rows_of(b1), rows_of(b1_across), rows_of(b1_sibling), inside)
 
     def meanwhile(step):
         for x in range(4 * step, 4 * step + 4):
@@ -322,12 +330,12 @@
         gram_out[g] = total
 
 
-def moment_kernel(last, last_before, last_after, basis_gram, medium, shift, t_out, gram_out):
+def moment_kernel(inside, last, last_across, last_sibling, basis_gram, medium, shift, t_out, gram_out):
     def next_field(x, g):
         theta = shift[8 * g : 8 * g + 1, :]
         brows = slice(B * g, B * g + B)
         out = (medium[x : x + 1, :] - SHIFT - theta) * last[x, brows] - neighbours(
-            x, lambda i: last[i, brows], last_before[x, brows], last_after[x, brows]
+            x, lambda i: last[i, brows], last_across[x, brows] * inside[0], last_sibling[x, brows]
         )
         t_out[x, brows] = out
         return out
@@ -560,7 +568,7 @@
 
 def beside(values):
     count = lax.axis_size(GRID)
-    edges = [(i, i + 1) for i in range(1, count - 1, 2)]
+    edges = [(i, (i + 1) % count) for i in range(1, count, 2)]
     across = lax.ppermute(values, GRID, edges + [(j, i) for i, j in edges])
     sibling = lax.ppermute(values, CORES, [(0, 1), (1, 0)])
     return across, sibling
@@ -571,6 +579,9 @@
     u = recycle.reshape(2, K, NX, NY)
     b = right_sides.reshape(2 * B, NX, NY)
     scalars = (shift_table, shift_index)
+    place = lax.axis_index(GRID)
+    at_end = (place == 0) | (place == lax.axis_size(GRID) - 1)
+    inside = jnp.where(at_end, 0.0, 1.0).astype(F32).reshape(1)
     back = jnp.transpose(jnp.concatenate([u[1], b], axis=0), (1, 0, 2))
     back_sides = beside(back)
     front = jnp.transpose(u[0], (1, 0, 2))
@@ -578,8 +589,9 @@
     f1, b, b1 = call(
         back_kernel,
         [(NX, K, NY), (NX, 2 * B, NY), (NX, 2 * B, NY)],
-        2,
+        3,
         *scalars,
+        inside,
         back,
         *back_sides,
         med,
@@ -588,19 +600,20 @@
     front_across, f1, f1_sibling = lax.optimization_barrier((front_across, f1, f1_sides[1]))
     f1_sides = (f1_sides[0], f1_sibling)
     (f0,) = call(
-        front_kernel, [(NX, K, NY)], 2, *scalars, front, front_across, front_sibling, med
+        front_kernel, [(NX, K, NY)], 3, *scalars, inside, front, front_across, front_sibling, med
     )
     f0_sides = beside(f0)
     b1_sides = beside(b1)
     (first,) = call(first_gram_kernel, [(K, 128)], 0, f0, f1, b, b1)
-    (fields,) = call(next_kernel, [(NX, 2 * K, NY)], 0, f0, *f0_sides, f1, *f1_sides, med)
+    (fields,) = call(next_kernel, [(NX, 2 * K, NY)], 1, inside, f0, *f0_sides, f1, *f1_sides, med)
     field_sides = beside(fields)
     (gram,) = call(second_gram_kernel, [(2 * K, 128)], 0, f0, f1, fields, b1, first)
     gram, b1_sides = lax.optimization_barrier((gram, b1_sides))
     q, last, coef, shift = call(
         krylov_kernel,
         [(NX, 96, NY), (NX, 2 * B, NY), (2, 96, 128), (16, 128)],
-        0,
+        1,
+        inside,
         everyone(gram),
         f0,
         f1,
@@ -615,7 +628,15 @@
     last_sides = beside(last)
     (basis_gram,) = call(basis_gram_kernel, [(2, 48, 128)], 0, q, fields)
     t, gram = call(
-        moment_kernel, [(NX, 2 * B, NY), (K, 128)], 0, last, *last_sides, basis_gram, med, shift
+        moment_kernel,
+        [(NX, 2 * B, NY), (K, 128)],
+        1,
+        inside,
+        last,
+        *last_sides,
+        basis_gram,
+        med,
+        shift,
     )
     solution, residue = finish(
         scalars, (everyone(gram), coef, shift, f0, f1, t), (front, back, q), (2 * B, NX, NY)

time: 149 us -> 146 us (0.980)
  starting transfers between devices: 32.2 us -> 20.7 us
  waiting for transfers between devices: 32.8 us -> 37.6 us
  blocking collectives: 60.6 us -> 63.1 us
  Pallas kernels: 19.8 us -> 21.4 us
    ppermute x7, starting transfers between devices: 30.9 us -> 19.6 us  [beside(): across = lax.ppermute(values, GRID, edges + [(j, i) for i, j in edges])]
    ppermute x7, waiting for transfers between devices: 30.4 us -> 35.2 us  [beside(): across = lax.ppermute(values, GRID, edges + [(j, i) for i, j in edges])]
    all_to_all x2, blocking collectives: 34.3 us -> 36.3 us  [everyone(): return lax.all_to_all(spread, near, 0, 0, tiled=True)]
    pallas_call x12, Pallas kernels: 12.5 us -> 14 us  [call(): pl.pallas_call(kernel, out_shape=[pltpu.VMEM(s, F32) for s in shapes], in...]
  transfers between devices with their start and end apart: 16 -> 16, of which waited for: 6 -> 7; matrix products, arithmetic and copies ran while one was open for 0% -> 0% of each run, Pallas kernels for 5% -> 6%
where the time goes in v5:
time: 146 us
  blocking collectives  63.1 us (43%)
  waiting for transfers between devices  37.6 us (26%)
  Pallas kernels  21.4 us (15%)
  starting transfers between devices  20.7 us (14%)
  local copies, waits for them, and re-layouts  1.98 us (1%)
    all_to_all x2, blocking collectives, everyone(): return lax.all_to_all(spread, near, 0, 0, tiled=True)  36.3 us
    ppermute x7, waiting for transfers between devices, beside(): across = lax.ppermute(values, GRID, edges + [(j, i) for i, j in edges])  35.2 us
    all_to_all x2, blocking collectives, everyone(): parts = lax.all_to_all(spread, far, 0, 0, tiled=True)  26.8 us
    ppermute x7, starting transfers between devices, beside(): across = lax.ppermute(values, GRID, edges + [(j, i) for i, j in edges])  19.6 us
    pallas_call x12, Pallas kernels, call(): pl.pallas_call(kernel, out_shape=[pltpu.VMEM(s, F32) for s in shapes], in...  14 us
    pallas_call x1, Pallas kernels, finish(): pl.pallas_call(finish_kernel, out_shape=[jax.ShapeDtypeStruct(shape, F32)...  7.4 us
  transfers between devices with their start and end apart: 16, of which 7 were waited for; matrix products, arithmetic and copies ran while one was open for 0% of the time, Pallas kernels for 6%

profile of v5, /device:TPU:8, one launch (start us, length us, event | category | flops | bytes accessed | tf_op | source)
XLA Modules:
  0.0 145.9 jit_solution(17498909245392068786)
XLA Ops:
  0.6 0.0 copy-start.3
  0.6 1.5 %copy.17 = f32[32,1,48,128]{3,0,2,1:T(8,128)S(1)} copy(f32[32,1,48,128]{3,2,1,0:T(8,128)} %param.5) | data formatting | bytes 1572864 | tf_op args[0]
  2.1 0.0 copy-done.3
  2.1 0.1 fusion
  2.2 0.2 copy.18
  2.4 0.0 copy-start
  2.4 0.0 copy-start.1
  2.4 0.0 copy-start.2
  2.5 0.1 maximum_bitcast_fusion.ub.u1_far
  2.6 0.1 collective-permute-start.2
  2.7 5.8 %collective-permute-start.1 = (f32[48,56,128]{2,1,0:T(8,128)S(1)}, f32[48,56,128]{2,1,0:T(8,128)}, u32[]{:S(2)}, u32[]{:S(2)}) collective-permute-start(f32[48,56,128]{2,1,0:T(8,128)S(1)} %maximum_bitcast_fusion.ub.u1_far), channel_id=1, source_target_pairs={{1,2},{3,4},{5,6},{7,8},{9,10},{11,12},{13,14},{15,16},{17,18},{19... | collective-permute-start | bytes 4128776 | tf_op jit(solution)/shard_map/ppermute | solution.py:572
  8.5 0.2 copy.19
  8.7 0.1 collective-permute-start
  8.8 0.0 collective-permute-done.2.sibling
  8.8 15.8 %collective-permute-done.1.across = f32[48,56,128]{2,1,0:T(8,128)} collective-permute-done((f32[48,56,128]{2,1,0:T(8,128)S(1)}, f32[48,56,128]{2,1,0:T(8,128)}, u32[]{:S(2)}, u32[]{:S(2)}) %collective-permute-start.1) | collective-permute-done | bytes 1376288 | tf_op jit(solution)/shard_map/ppermute | solution.py:572
  24.6 0.0 copy-done
  24.6 0.0 copy-done.1
  24.6 0.0 copy-done.2
  24.6 2.1 %back_kernel.1 = (f32[48,24,128]{2,1,0:T(8,128)S(1)}, f32[48,32,128]{2,1,0:T(8,128)S(1)}, f32[48,32,128]{2,1,0:T(8,128)S(1)}) custom-call(f32[8]{0:T(128)S(1)} %copy-done.1, s32[2]{0:T(128)S(1)} %copy-done.2, f32[1]{0:T(128)} %bitcast.inside, f32[48,56,128]{2,1,0:T(8,128)S(1)} %maximum_bitcast_fusion.ub.u1_far, ...), custom_call_target="tpu_custom_call" | custom-call | tf_op jit(solution)/shard_map/back_kernel/pallas_call | solution.py:522
  26.8 0.1 collective-permute-start.3
  26.9 0.5 collective-permute-start.4
  27.4 3.9 %collective-permute-start.7 = (f32[48,24,128]{2,1,0:T(8,128)S(1)}, f32[48,24,128]{2,1,0:T(8,128)S(1)}, u32[]{:S(2)}, u32[]{:S(2)}) collective-permute-start(f32[48,24,128]{2,1,0:T(8,128)S(1)} %get-tuple-element.21.f1), channel_id=1, source_target_pairs={{1,2},{3,4},{5,6},{7,8},{9,10},{11,12},{13,14},{15,16},{17,18},{19... | collective-permute-start | bytes 1769480 | tf_op jit(solution)/shard_map/ppermute | solution.py:572
  31.2 0.0 collective-permute-done.across
  31.2 0.0 collective-permute-done.3.f1_sibling
  31.2 0.0 collective-permute-done.4.sibling
  31.2 1.5 %front_kernel.1.f0 = f32[48,24,128]{2,1,0:T(8,128)S(1)} custom-call(f32[8]{0:T(128)S(1)} %copy-done.1, s32[2]{0:T(128)S(1)} %copy-done.2, f32[1]{0:T(128)} %bitcast.inside, f32[48,24,128]{2,1,0:T(8,128)S(1)} %bitcast.23, f32[48,24,128]{2,1,0:T(8,128)} %collective-permute-done.across, f32[48,24,128]{2,1,0:T(8,128)S(1)} %collective-permute-done.4.sibling, ...), custom_call_target="tpu_custom_call" | custom-call | tf_op jit(solution)/shard_map/front_kernel/pallas_call | solution.py:522
  32.7 0.1 collective-permute-start.6
  32.8 3.6 %collective-permute-start.5 = (f32[48,24,128]{2,1,0:T(8,128)S(1)}, f32[48,24,128]{2,1,0:T(8,128)S(1)}, u32[]{:S(2)}, u32[]{:S(2)}) collective-permute-start(f32[48,24,128]{2,1,0:T(8,128)S(1)} %front_kernel.1.f0), channel_id=1, source_target_pairs={{1,2},{3,4},{5,6},{7,8},{9,10},{11,12},{13,14},{15,16},{17,18},{19... | collective-permute-start | bytes 1769480 | tf_op jit(solution)/shard_map/ppermute | solution.py:572
  36.4 0.0 collective-permute-start.9
  36.4 0.4 collective-permute-start.8
  36.9 1.9 %collective-permute-done.7.f1_across = f32[48,24,128]{2,1,0:T(8,128)S(1)} collective-permute-done((f32[48,24,128]{2,1,0:T(8,128)S(1)}, f32[48,24,128]{2,1,0:T(8,128)S(1)}, u32[]{:S(2)}, u32[]{:S(2)}) %collective-permute-start.7) | collective-permute-done | bytes 589856 | tf_op jit(solution)/shard_map/ppermute | solution.py:572
  38.8 0.0 collective-permute-done.6.f0_sibling
  38.8 6.3 %collective-permute-done.5.f0_across = f32[48,24,128]{2,1,0:T(8,128)S(1)} collective-permute-done((f32[48,24,128]{2,1,0:T(8,128)S(1)}, f32[48,24,128]{2,1,0:T(8,128)S(1)}, u32[]{:S(2)}, u32[]{:S(2)}) %collective-permute-start.5) | collective-permute-done | bytes 589856 | tf_op jit(solution)/shard_map/ppermute | solution.py:572
  45.1 0.8 next_kernel.1.fields
  45.9 0.1 collective-permute-start.12
  46.0 3.9 %collective-permute-start.11 = (f32[48,48,128]{2,1,0:T(8,128)S(1)}, f32[48,48,128]{2,1,0:T(8,128)S(1)}, u32[]{:S(2)}, u32[]{:S(2)}) collective-permute-start(f32[48,48,128]{2,1,0:T(8,128)S(1)} %next_kernel.1.fields), channel_id=1, source_target_pairs={{1,2},{3,4},{5,6},{7,8},{9,10},{11,12},{13,14},{15,16},{17,18},{19... | collective-permute-start | bytes 3538952 | tf_op jit(solution)/shard_map/ppermute | solution.py:572
  49.9 1.2 first_gram_kernel.1.first
  51.1 1.1 second_gram_kernel.1.one
  52.2 0.0 collective-permute-done.9.b1_sibling
  52.2 1.3 collective-permute-done.8.b1_across
  53.5 0.0 collective-permute-start.10
  53.5 1.2 collective-permute-done.10.two
  54.7 15.5 %all_to_all.20.parts = f32[8,48,128]{2,1,0:T(8,128)S(1)} all-to-all(f32[8,48,128]{2,1,0:T(8,128)S(1)} %add_kernel.2), channel_id=1, replica_groups=mesh['grid_0'=4,'grid_1'=4,'grid_2'=8,'grid_3'=2] {'grid_2'}, dimensions={0} | all-to-all | bytes 393216 | tf_op jit(solution)/shard_map/all_to_all | solution.py:564
  70.2 22.0 %all_to_all.21.grams = f32[16,48,128]{2,1,0:T(8,128)S(1)} all-to-all(f32[16,48,128]{2,1,0:T(8,128)S(1)} %respread_kernel.2), channel_id=1, replica_groups=mesh['grid_0'=4,'grid_1'=4,'grid_2'=8,'grid_3'=2] {'grid_0','grid_1'}, dimensions={0} | all-to-all | bytes 786432 | tf_op jit(solution)/shard_map/all_to_all | solution.py:566
  92.3 0.0 collective-permute-done.12.fields_sibling
  92.3 0.0 collective-permute-done.11.fields_across
  92.3 4.4 %krylov_kernel.1 = (f32[48,96,128]{2,1,0:T(8,128)S(1)}, f32[48,32,128]{2,1,0:T(8,128)S(1)}, f32[2,96,128]{2,1,0:T(8,128)S(1)}, f32[16,128]{1,0:T(8,128)S(1)}) custom-call(f32[1]{0:T(128)} %bitcast.inside, f32[16,48,128]{2,1,0:T(8,128)S(1)} %all_to_all.21.grams, f32[48,24,128]{2,1,0:T(8,128)S(1)} %front_kernel.1.f0, f32[48,24,128]{2,1,0:T(8,128)S(1)} %get-tuple-element.21.f1, ...), custom_call_target="tpu_custom_call" | custom-call | tf_op jit(solution)/shard_map/krylov_kernel/pallas_call | solution.py:522
  96.7 0.1 collective-permute-start.14
  96.8 1.9 %collective-permute-start.13 = (f32[48,32,128]{2,1,0:T(8,128)S(1)}, f32[48,32,128]{2,1,0:T(8,128)S(1)}, u32[]{:S(2)}, u32[]{:S(2)}) collective-permute-start(f32[48,32,128]{2,1,0:T(8,128)S(1)} %get-tuple-element.28.last), channel_id=1, source_target_pairs={{1,2},{3,4},{5,6},{7,8},{9,10},{11,12},{13,14},{15,16},{17,18},{19... | collective-permute-start | bytes 2359304 | tf_op jit(solution)/shard_map/ppermute | solution.py:572
  98.6 1.8 %basis_gram_kernel.1.basis_gram = f32[2,48,128]{2,1,0:T(8,128)S(1)} custom-call(f32[48,96,128]{2,1,0:T(8,128)S(1)} %get-tuple-element.29.q.q_far, f32[48,48,128]{2,1,0:T(8,128)S(1)} %next_kernel.1.fields), custom_call_target="tpu_custom_call" | custom-call | tf_op jit(solution)/shard_map/basis_gram_kernel/pallas_call | solution.py:522
  100.5 0.0 collective-permute-done.14.last_sibling
  100.5 9.9 %collective-permute-done.13.last_across = f32[48,32,128]{2,1,0:T(8,128)S(1)} collective-permute-done((f32[48,32,128]{2,1,0:T(8,128)S(1)}, f32[48,32,128]{2,1,0:T(8,128)S(1)}, u32[]{:S(2)}, u32[]{:S(2)}) %collective-permute-start.13) | collective-permute-done | bytes 786464 | tf_op jit(solution)/shard_map/ppermute | solution.py:572
  110.4 1.1 moment_kernel.1
  111.5 0.1 collective-permute-start.15
  111.6 1.2 collective-permute-done.15.two
  112.7 11.4 %all_to_all.22.parts = f32[8,24,128]{2,1,0:T(8,128)S(1)} all-to-all(f32[8,24,128]{2,1,0:T(8,128)S(1)} %add_kernel.3), channel_id=1, replica_groups=mesh['grid_0'=4,'grid_1'=4,'grid_2'=8,'grid_3'=2] {'grid_2'}, dimensions={0} | all-to-all | bytes 196608 | tf_op jit(solution)/shard_map/all_to_all | solution.py:564
  124.1 14.3 %all_to_all.23.moments = f32[16,24,128]{2,1,0:T(8,128)S(1)} all-to-all(f32[16,24,128]{2,1,0:T(8,128)S(1)} %respread_kernel.3), channel_id=1, replica_groups=mesh['grid_0'=4,'grid_1'=4,'grid_2'=8,'grid_3'=2] {'grid_0','grid_1'}, dimensions={0} | all-to-all | bytes 393216 | tf_op jit(solution)/shard_map/all_to_all | solution.py:566
  138.4 7.4 %finish_kernel.1 = (f32[32,48,128]{2,1,0:T(8,128)}, f32[32,48,128]{2,1,0:T(8,128)}) custom-call(f32[8]{0:T(128)S(1)} %copy-done.1, s32[2]{0:T(128)S(1)} %copy-done.2, f32[16,24,128]{2,1,0:T(8,128)S(1)} %all_to_all.23.moments, f32[2,96,128]{2,1,0:T(8,128)S(1)} %get-tuple-element.32.coef, f32[16,128]{1,0:T(8,128)S(1)} %get-tuple-element.30.shift, ...), custom_call_target="tpu_custom_call" | custom-call | tf_op jit(solution)/shard_map/finish_kernel/pallas_call | solution.py:535
  (4 shorter events, 0.1 us)
Async XLA Ops:
  0.6 1.5 %copy-start.3 = (f32[2,24,1,48,128]{4,3,2,1,0:T(8,128)S(1)}, f32[2,24,1,48,128]{4,3,2,1,0:T(8,128)}, u32[]{:S(2)}) copy-start(f32[2,24,1,48,128]{4,3,2,1,0:T(8,128)} %param.6) | copy-start | bytes 3538948
  2.4 22.2 %copy-start = (f32[1,48,128]{2,1,0:T(8,128)S(1)}, f32[1,48,128]{2,1,0:T(8,128)}, u32[]{:S(2)}) copy-start(f32[1,48,128]{2,1,0:T(8,128)} %param.7) | copy-start | bytes 73732
  2.4 22.2 %copy-start.1 = (f32[8]{0:T(128)S(1)}, f32[8]{0:T(128)}, u32[]{:S(2)}) copy-start(f32[8]{0:T(128)} %table.5) | copy-start | bytes 100
  2.4 22.2 %copy-start.2 = (s32[2]{0:T(128)S(1)}, s32[2]{0:T(128)}, u32[]{:S(2)}) copy-start(s32[2]{0:T(128)} %index.5) | copy-start | bytes 28
  2.6 6.3 %collective-permute-start.2 = (f32[48,56,128]{2,1,0:T(8,128)S(1)}, f32[48,56,128]{2,1,0:T(8,128)S(1)}, u32[]{:S(2)}, u32[]{:S(2)}) collective-permute-start(f32[48,56,128]{2,1,0:T(8,128)S(1)} %maximum_bitcast_fusion.ub.u1_far), channel_id=1, source_target_pairs={{0,1},{1,0},{2,3},{3,2},{4,5},{5,4},{6,7},{7,6},{8,9},{9,8},{10,11... | collective-permute-start | bytes 4128776 | tf_op jit(solution)/shard_map/ppermute | solution.py:573
  2.7 21.9 %collective-permute-start.1 = (f32[48,56,128]{2,1,0:T(8,128)S(1)}, f32[48,56,128]{2,1,0:T(8,128)}, u32[]{:S(2)}, u32[]{:S(2)}) collective-permute-start(f32[48,56,128]{2,1,0:T(8,128)S(1)} %maximum_bitcast_fusion.ub.u1_far), channel_id=1, source_target_pairs={{1,2},{3,4},{5,6},{7,8},{9,10},{11,12},{13,14},{15,16},{17,18},{19... | collective-permute-start | bytes 4128776 | tf_op jit(solution)/shard_map/ppermute | solution.py:572
  8.7 22.5 %collective-permute-start = (f32[48,24,128]{2,1,0:T(8,128)S(1)}, f32[48,24,128]{2,1,0:T(8,128)}, u32[]{:S(2)}, u32[]{:S(2)}) collective-permute-start(f32[48,24,128]{2,1,0:T(8,128)S(1)} %bitcast.21), channel_id=1, source_target_pairs={{1,2},{3,4},{5,6},{7,8},{9,10},{11,12},{13,14},{15,16},{17,18},{19... | collective-permute-start | bytes 1769480 | tf_op jit(solution)/shard_map/ppermute | solution.py:572
  26.8 4.5 %collective-permute-start.3 = (f32[48,24,128]{2,1,0:T(8,128)S(1)}, f32[48,24,128]{2,1,0:T(8,128)S(1)}, u32[]{:S(2)}, u32[]{:S(2)}) collective-permute-start(f32[48,24,128]{2,1,0:T(8,128)S(1)} %get-tuple-element.21.f1), channel_id=1, source_target_pairs={{0,1},{1,0},{2,3},{3,2},{4,5},{5,4},{6,7},{7,6},{8,9},{9,8},{10,11... | collective-permute-start | bytes 1769480 | tf_op jit(solution)/shard_map/ppermute | solution.py:573
  26.9 4.4 %collective-permute-start.4 = (f32[48,24,128]{2,1,0:T(8,128)S(1)}, f32[48,24,128]{2,1,0:T(8,128)S(1)}, u32[]{:S(2)}, u32[]{:S(2)}) collective-permute-start(f32[48,24,128]{2,1,0:T(8,128)S(1)} %bitcast.22), channel_id=1, source_target_pairs={{0,1},{1,0},{2,3},{3,2},{4,5},{5,4},{6,7},{7,6},{8,9},{9,8},{10,11... | collective-permute-start | bytes 1769480 | tf_op jit(solution)/shard_map/ppermute | solution.py:573
  27.4 11.4 %collective-permute-start.7 = (f32[48,24,128]{2,1,0:T(8,128)S(1)}, f32[48,24,128]{2,1,0:T(8,128)S(1)}, u32[]{:S(2)}, u32[]{:S(2)}) collective-permute-start(f32[48,24,128]{2,1,0:T(8,128)S(1)} %get-tuple-element.21.f1), channel_id=1, source_target_pairs={{1,2},{3,4},{5,6},{7,8},{9,10},{11,12},{13,14},{15,16},{17,18},{19... | collective-permute-start | bytes 1769480 | tf_op jit(solution)/shard_map/ppermute | solution.py:572
  32.7 6.1 %collective-permute-start.6 = (f32[48,24,128]{2,1,0:T(8,128)S(1)}, f32[48,24,128]{2,1,0:T(8,128)S(1)}, u32[]{:S(2)}, u32[]{:S(2)}) collective-permute-start(f32[48,24,128]{2,1,0:T(8,128)S(1)} %front_kernel.1.f0), channel_id=1, source_target_pairs={{0,1},{1,0},{2,3},{3,2},{4,5},{5,4},{6,7},{7,6},{8,9},{9,8},{10,11... | collective-permute-start | bytes 1769480 | tf_op jit(solution)/shard_map/ppermute | solution.py:573
  32.8 12.3 %collective-permute-start.5 = (f32[48,24,128]{2,1,0:T(8,128)S(1)}, f32[48,24,128]{2,1,0:T(8,128)S(1)}, u32[]{:S(2)}, u32[]{:S(2)}) collective-permute-start(f32[48,24,128]{2,1,0:T(8,128)S(1)} %front_kernel.1.f0), channel_id=1, source_target_pairs={{1,2},{3,4},{5,6},{7,8},{9,10},{11,12},{13,14},{15,16},{17,18},{19... | collective-permute-start | bytes 1769480 | tf_op jit(solution)/shard_map/ppermute | solution.py:572
  36.4 15.7 %collective-permute-start.9 = (f32[48,32,128]{2,1,0:T(8,128)S(1)}, f32[48,32,128]{2,1,0:T(8,128)S(1)}, u32[]{:S(2)}, u32[]{:S(2)}) collective-permute-start(f32[48,32,128]{2,1,0:T(8,128)S(1)} %get-tuple-element.23.b1), channel_id=1, source_target_pairs={{0,1},{1,0},{2,3},{3,2},{4,5},{5,4},{6,7},{7,6},{8,9},{9,8},{10,11... | collective-permute-start | bytes 2359304 | tf_op jit(solution)/shard_map/ppermute | solution.py:573
  36.4 17.1 %collective-permute-start.8 = (f32[48,32,128]{2,1,0:T(8,128)S(1)}, f32[48,32,128]{2,1,0:T(8,128)S(1)}, u32[]{:S(2)}, u32[]{:S(2)}) collective-permute-start(f32[48,32,128]{2,1,0:T(8,128)S(1)} %get-tuple-element.23.b1), channel_id=1, source_target_pairs={{1,2},{3,4},{5,6},{7,8},{9,10},{11,12},{13,14},{15,16},{17,18},{19... | collective-permute-start | bytes 2359304 | tf_op jit(solution)/shard_map/ppermute | solution.py:572
  45.9 46.4 %collective-permute-start.12 = (f32[48,48,128]{2,1,0:T(8,128)S(1)}, f32[48,48,128]{2,1,0:T(8,128)S(1)}, u32[]{:S(2)}, u32[]{:S(2)}) collective-permute-start(f32[48,48,128]{2,1,0:T(8,128)S(1)} %next_kernel.1.fields), channel_id=1, source_target_pairs={{0,1},{1,0},{2,3},{3,2},{4,5},{5,4},{6,7},{7,6},{8,9},{9,8},{10,11... | collective-permute-start | bytes 3538952 | tf_op jit(solution)/shard_map/ppermute | solution.py:573
  46.0 46.3 %collective-permute-start.11 = (f32[48,48,128]{2,1,0:T(8,128)S(1)}, f32[48,48,128]{2,1,0:T(8,128)S(1)}, u32[]{:S(2)}, u32[]{:S(2)}) collective-permute-start(f32[48,48,128]{2,1,0:T(8,128)S(1)} %next_kernel.1.fields), channel_id=1, source_target_pairs={{1,2},{3,4},{5,6},{7,8},{9,10},{11,12},{13,14},{15,16},{17,18},{19... | collective-permute-start | bytes 3538952 | tf_op jit(solution)/shard_map/ppermute | solution.py:572
  53.5 1.2 collective-permute-start.10
  96.7 3.8 %collective-permute-start.14 = (f32[48,32,128]{2,1,0:T(8,128)S(1)}, f32[48,32,128]{2,1,0:T(8,128)S(1)}, u32[]{:S(2)}, u32[]{:S(2)}) collective-permute-start(f32[48,32,128]{2,1,0:T(8,128)S(1)} %get-tuple-element.28.last), channel_id=1, source_target_pairs={{0,1},{1,0},{2,3},{3,2},{4,5},{5,4},{6,7},{7,6},{8,9},{9,8},{10,11... | collective-permute-start | bytes 2359304 | tf_op jit(solution)/shard_map/ppermute | solution.py:573
  96.8 13.6 %collective-permute-start.13 = (f32[48,32,128]{2,1,0:T(8,128)S(1)}, f32[48,32,128]{2,1,0:T(8,128)S(1)}, u32[]{:S(2)}, u32[]{:S(2)}) collective-permute-start(f32[48,32,128]{2,1,0:T(8,128)S(1)} %get-tuple-element.28.last), channel_id=1, source_target_pairs={{1,2},{3,4},{5,6},{7,8},{9,10},{11,12},{13,14},{15,16},{17,18},{19... | collective-permute-start | bytes 2359304 | tf_op jit(solution)/shard_map/ppermute | solution.py:572
  111.5 1.3 collective-permute-start.15

commit v6 on v5

--- a/solution.py
+++ b/solution.py
@@ -79,7 +79,7 @@
     return jnp.concatenate([values, jnp.zeros((128 - rows, 128), F32)], axis=0).T
 
 
-def eliminate(system, count, meanwhile=None):
+def eliminate(system, count):
     lane = iota((1, 128), 1)
     row = iota(system.shape, 0)
 
@@ -87,8 +87,6 @@
         return jnp.where(lane < 64, system[:, k : k + 1], system[:, 64 + k : 65 + k])
 
     for k in range(0, count, 2):
-        if meanwhile is not None:
-            meanwhile(k // 2)
         one = system[k : k + 1]
         two = system[k + 1 : k + 2]
         left = column(k)
@@ -188,8 +186,8 @@
     gram_out[...] = packed
 
 
-def rows_of(ref):
-    return lambda x: ref[x]
+def rows_of(ref, rows=slice(None)):
+    return lambda x: ref[x, rows]
 
 
 def next_kernel(inside, f0, f0_across, f0_sibling, f1, f1_across, f1_sibling, medium, fields_out):
@@ -219,46 +217,14 @@
     gram_out[K:] = jnp.where(lane < 64, total[:K], total[K:])
 
 
-def krylov_kernel(
-    inside,
-    grams,
-    f0,
-    f1,
-    b,
-    b1,
-    b1_across,
-    b1_sibling,
-    fields,
-    fields_across,
-    fields_sibling,
-    medium,
-    q_out,
-    last_out,
-    coef_out,
-    shift_out,
-    f_next,
-    b_next,
-):
-    def plain(x):
-        return medium[x : x + 1, :] - SHIFT
-
-    next_f = stencil(
-        plain, rows_of(fields), rows_of(fields_across), rows_of(fields_sibling), inside
-    )
-    next_b = stencil(plain, rows_of(b1), rows_of(b1_across), rows_of(b1_sibling), inside)
-
-    def meanwhile(step):
-        for x in range(4 * step, 4 * step + 4):
-            f_next[x] = next_f(x)
-            b_next[x] = next_b(x)
-
+def krylov_kernel(grams, f0, f1, b, b1, fields, q_out, last_out, coef_out, shift_out):
     gram = over_copies(grams)
     first = gram[:K]
     lane = iota((K, 128), 1)
     row = iota((K, 128), 0)
     place = lane & 63
     unit = jnp.where(place == row + K, 1.0, 0.0)
-    inverse_t = transposed(eliminate(jnp.where(place < K, first, unit), K, meanwhile))
+    inverse_t = transposed(eliminate(jnp.where(place < K, first, unit), K))
     first_t = transposed(first)
     second_t = transposed(gram[K:])
     coeffs = []
@@ -277,13 +243,10 @@
         z2 = small(f1b1 - small(z0, f1f1) - small(z1, ff1), ginv)
         z2 = z2 - theta * z1
         mixed = z1 - theta * z0
-        zero = jnp.zeros((B, K), F32)
-        pad = jnp.zeros((B, 8), F32)
         table = jnp.concatenate(
             [
-                jnp.concatenate([z0, zero, zero, pad], axis=1),
-                jnp.concatenate([mixed, z0, zero, pad], axis=1),
-                jnp.concatenate([z2 - theta * mixed, mixed - theta * z0, z0, pad], axis=1),
+                jnp.concatenate([z0, jnp.zeros((B, K), F32)], axis=1),
+                jnp.concatenate([mixed, z0], axis=1),
             ],
             axis=0,
         )
@@ -292,77 +255,113 @@
         for i, z in enumerate((z0, z1, z2, ginv)):
             coef_out[g, 24 * i : 24 * i + z.shape[0], :K] = z
         shift_out[8 * g : 8 * g + 8, :] = jnp.broadcast_to(theta, (8, 128))
-    zeros = jnp.zeros((8, 2 * NY), F32)
     for x in range(0, NX, 2):
         for g in range(2):
             frows = slice(K * g, K * g + K)
             brows = slice(B * g, B * g + B)
-            theta = thetas[g]
             made = combination(
                 coeffs[g],
-                jnp.concatenate(
-                    [pair((f0, f1)[g], x), pair(fields, x, frows), pair(f_next, x, frows), zeros],
-                    axis=0,
-                ),
+                jnp.concatenate([pair((f0, f1)[g], x), pair(fields, x, frows)], axis=0),
             )
             b_own = pair(b, x, brows)
-            b_one = pair(b1, x, brows)
-            q1 = b_one - theta * b_own
-            q2 = (pair(b_next, x, brows) - theta * b_one) - theta * q1
-            made = made + jnp.concatenate([b_own, q1, q2], axis=0)
+            made = made + jnp.concatenate([b_own, pair(b1, x, brows) - thetas[g] * b_own], axis=0)
             for i in range(2):
                 part = made[:, NY * i : NY * i + NY]
-                q_out[x + i, 48 * g : 48 * g + 48] = part
-                last_out[x + i, brows] = part[2 * B :]
-
-
-def basis_gram_kernel(q, fields, gram_out):
-    for g in range(2):
-        qrows = slice(48 * g, 48 * g + 48)
-        frows = slice(K * g, K * g + K)
-        total = jnp.zeros((48, 128), F32)
-        none = jnp.zeros((B, 2 * NY), F32)
+                q_out[x + i, 32 * g : 32 * g + 32] = part
+                last_out[x + i, brows] = part[B:]
+
+
+def basis_gram_kernel(q, gram_out):
+    pad = jnp.zeros((96, 2 * NY), F32)
+    for g in range(2):
+        rows = slice(32 * g, 32 * g + 32)
+        total = jnp.zeros((32, 128), F32)
+        for x in range(0, NX, 2):
+            left = pair(q, x, rows)
+            total = total + row_products(left, jnp.concatenate([left, pad], axis=0))
+        gram_out[g] = total
+
+
+def moment_kernel(
+    inside,
+    q,
+    last,
+    across,
+    sibling,
+    past_across,
+    past_sibling,
+    f0,
+    f0_across,
+    f0_sibling,
+    f1,
+    f1_across,
+    f1_sibling,
+    fields,
+    medium,
+    medium_across,
+    medium_sibling,
+    coef,
+    shift,
+    basis_gram,
+    q2_out,
+    t_out,
+    gram_out,
+    aside,
+):
+    zeros = jnp.zeros((8, 6 * NY), F32)
+    ones = (1.0, 1.0)
+    grams = []
+    for g in range(2):
+        theta = shift[8 * g : 8 * g + 1, :]
+        brows = slice(B * g, B * g + B)
+        coeffs = split_coeffs(
+            jnp.concatenate([-coef[g, 48 : 48 + B, :K], jnp.zeros((B, 8), F32)], axis=1)
+        )
+
+        def shifted(field):
+            return lambda x: field[x : x + 1, :] - SHIFT - theta
+
+        own, over, near, past_over, past_near = (
+            rows_of(a, brows) for a in (last, across, sibling, past_across, past_sibling)
+        )
+        here_q2 = stencil(shifted(medium), own, over, near, inside)
+        near_q2 = stencil(shifted(medium_sibling), near, past_near, own, (inside[1],))
+        over_q2 = stencil(shifted(medium_across), over, past_over, own, ones)
+        slabs = ((f0, f0_sibling, f0_across), (f1, f1_sibling, f1_across))[g]
+        for x in range(0, NX, 2):
+            fs = jnp.concatenate([pair(a, x) for a in slabs], axis=1)
+            made = combination(coeffs, jnp.concatenate([fs, zeros], axis=0))
+            for i in range(2):
+                at = [made[:, NY * (2 * k + i) : NY * (2 * k + i + 1)] for k in range(3)]
+                q2_out[x + i, brows] = here_q2(x + i) + at[0]
+                beyond = (over_q2(x + i) + at[2]) * inside[0]
+                aside[x + i, brows] = near_q2(x + i) + at[1] + beyond
+        made_t = stencil(
+            shifted(medium), rows_of(q2_out, brows), rows_of(aside, brows), lambda x: 0.0, ones
+        )
+        total = jnp.zeros((2 * B, 128), F32)
         pad = jnp.zeros((40, 2 * NY), F32)
         for x in range(0, NX, 2):
-            left = jnp.concatenate([q[x, qrows], q[x + 1, qrows]], axis=1)
-            f1 = jnp.concatenate([fields[x, frows], fields[x + 1, frows]], axis=1)
-            total = total + row_products(left, jnp.concatenate([left, none, f1, pad], axis=0))
-        gram_out[g] = total
-
-
-def moment_kernel(inside, last, last_across, last_sibling, basis_gram, medium, shift, t_out, gram_out):
-    def next_field(x, g):
-        theta = shift[8 * g : 8 * g + 1, :]
-        brows = slice(B * g, B * g + B)
-        out = (medium[x : x + 1, :] - SHIFT - theta) * last[x, brows] - neighbours(
-            x, lambda i: last[i, brows], last_across[x, brows] * inside[0], last_sibling[x, brows]
-        )
-        t_out[x, brows] = out
-        return out
-
-    total = jnp.zeros((2 * B, 128), F32)
-    pad = jnp.zeros((64, 2 * NY), F32)
-    for x in range(0, NX, 2):
-        left = []
-        right = []
-        for g in range(2):
-            brows = slice(B * g, B * g + B)
-            made = jnp.concatenate([next_field(x, g), next_field(x + 1, g)], axis=1)
-            left.append(made)
-            right.append(jnp.concatenate([last[x, brows], last[x + 1, brows]], axis=1))
-            right.append(made)
-        total = total + row_products(
-            jnp.concatenate(left, axis=0), jnp.concatenate(right + [pad], axis=0)
-        )
-    grams = [basis_gram[0], basis_gram[1]]
-    ends = [pltpu.roll(total[:B], 80, 1), pltpu.roll(total[B:], 48, 1)]
+            ends = [made_t(x), made_t(x + 1)]
+            for i in range(2):
+                t_out[x + i, brows] = ends[i]
+            left = jnp.concatenate(
+                [pair(q2_out, x, brows), jnp.concatenate(ends, axis=1)], axis=0
+            )
+            f1_pair = pair(fields, x, slice(K * g, K * g + K))
+            right = [pair(q, x, slice(32 * g, 32 * g + 32)), left, f1_pair, pad]
+            total = total + row_products(left, jnp.concatenate(right, axis=0))
+        grams.append(total)
     lane = iota((B, 128), 1)
     row = iota((B, 128), 0)
     column = lane & 15
     strips = []
-    for gram, end in zip(grams, ends):
-        middle = jnp.where(lane < 64, pltpu.roll(gram[16:32], 16, 1), pltpu.roll(gram[32:48], 32, 1))
-        strips.append(jnp.where(lane < 32, gram[:16], jnp.where(lane < 80, middle, end)))
+    for g in range(2):
+        low, high = basis_gram[g, :B], basis_gram[g, B:]
+        ends = jnp.where(lane < 96, pltpu.roll(grams[g][:B], 32, 1), pltpu.roll(grams[g][B:], 48, 1))
+        strips.append(
+            jnp.where(lane < 32, low, jnp.where(lane < 48, pltpu.roll(high, 16, 1), ends))
+        )
     packed = jnp.where(row <= column, strips[0], strips[1])
     packed = jnp.where(lane < 112, packed, 0.0)
     on_diagonal = jnp.where((row == column) & (lane < 112), strips[1], 0.0)
@@ -375,7 +374,7 @@
     for g in range(2):
         for half in range(2):
             at = 24 * (2 * g + half)
-            piece = pltpu.roll(grams[g][32 + 8 * half : 40 + 8 * half], (at - 64) % 128, 1)
+            piece = pltpu.roll(grams[g][8 * half : 8 * half + 8], (at - 64) % 128, 1)
             low = jnp.where((lane8 >= at) & (lane8 < at + K), piece, low)
     gram_out[:B] = packed
     gram_out[B:] = low
@@ -389,6 +388,7 @@
     shift,
     f0,
     f1,
+    q2,
     t,
     u0_far,
     u1_far,
@@ -490,17 +490,17 @@
     for x in range(0, NX, 2):
         for g in range(2):
             brows = slice(B * g, B * g + B)
-            qrows = slice(48 * g, 48 * g + 48)
+            qrows = slice(32 * g, 32 * g + 32)
             made = combination(
                 coeffs[g],
                 jnp.concatenate(
-                    [pair((u0, u1)[g], x, slice(0, K)), pair((f0, f1)[g], x), pair(q, x, qrows), pair(t, x, brows)], axis=0
+                    [pair((u0, u1)[g], x, slice(0, K)), pair((f0, f1)[g], x), pair(q, x, qrows), pair(q2, x, brows), pair(t, x, brows)], axis=0
                 ),
             )
             for i in range(2):
                 part = made[:, NY * i : NY * i + NY]
                 solution_out[brows, x + i, :] = part[:B]
-                residue_out[brows, x + i, :] = part[B:] + q[x + i, 48 * g : 48 * g + B]
+                residue_out[brows, x + i, :] = part[B:] + q[x + i, 32 * g : 32 * g + B]
         if (x + 2) % CHUNK == 0:
             rows = pl.ds(x + 2 - CHUNK, CHUNK)
             for near, far in ((solution_out, solution_far), (residue_out, residue_far)):
@@ -574,6 +574,13 @@
     return across, sibling
 
 
+def past_edge(values):
+    count = lax.axis_size(GRID)
+    return lax.ppermute(
+        values, GRID, [(i, (i - 2 if i % 2 else i + 2) % count) for i in range(count)]
+    )
+
+
 def on_device(right_sides, recycle, medium, shift_table, shift_index):
     med = medium[0]
     u = recycle.reshape(2, K, NX, NY)
@@ -581,7 +588,8 @@
     scalars = (shift_table, shift_index)
     place = lax.axis_index(GRID)
     at_end = (place == 0) | (place == lax.axis_size(GRID) - 1)
-    inside = jnp.where(at_end, 0.0, 1.0).astype(F32).reshape(1)
+    near_end = (place == 1) | (place == lax.axis_size(GRID) - 2)
+    inside = jnp.where(jnp.stack([at_end, near_end]), 0.0, 1.0).astype(F32)
     back = jnp.transpose(jnp.concatenate([u[1], b], axis=0), (1, 0, 2))
     back_sides = beside(back)
     front = jnp.transpose(u[0], (1, 0, 2))
@@ -603,43 +611,50 @@
         front_kernel, [(NX, K, NY)], 3, *scalars, inside, front, front_across, front_sibling, med
     )
     f0_sides = beside(f0)
-    b1_sides = beside(b1)
+    med_sides = beside(med)
     (first,) = call(first_gram_kernel, [(K, 128)], 0, f0, f1, b, b1)
     (fields,) = call(next_kernel, [(NX, 2 * K, NY)], 1, inside, f0, *f0_sides, f1, *f1_sides, med)
-    field_sides = beside(fields)
     (gram,) = call(second_gram_kernel, [(2 * K, 128)], 0, f0, f1, fields, b1, first)
-    gram, b1_sides = lax.optimization_barrier((gram, b1_sides))
     q, last, coef, shift = call(
         krylov_kernel,
-        [(NX, 96, NY), (NX, 2 * B, NY), (2, 96, 128), (16, 128)],
-        1,
-        inside,
+        [(NX, 64, NY), (NX, 2 * B, NY), (2, 96, 128), (16, 128)],
+        0,
         everyone(gram),
         f0,
         f1,
         b,
         b1,
-        *b1_sides,
         fields,
-        *field_sides,
-        med,
-        scratch=[(NX, 2 * K, NY), (NX, 2 * B, NY)],
-    )
-    last_sides = beside(last)
-    (basis_gram,) = call(basis_gram_kernel, [(2, 48, 128)], 0, q, fields)
-    t, gram = call(
+    )
+    last_across, last_sibling = beside(last)
+    past_across = past_edge(last)
+    past_sibling = lax.ppermute(last_across, CORES, [(0, 1), (1, 0)])
+    (basis_gram,) = call(basis_gram_kernel, [(2, 32, 128)], 0, q)
+    q2, t, gram = call(
         moment_kernel,
-        [(NX, 2 * B, NY), (K, 128)],
+        [(NX, 2 * B, NY), (NX, 2 * B, NY), (K, 128)],
         1,
         inside,
+        q,
         last,
-        *last_sides,
+        last_across,
+        last_sibling,
+        past_across,
+        past_sibling,
+        f0,
+        *f0_sides,
+        f1,
+        *f1_sides,
+        fields,
+        med,
+        *med_sides,
+        coef,
+        shift,
         basis_gram,
-        med,
-        shift,
+        scratch=[(NX, 2 * B, NY)],
     )
     solution, residue = finish(
-        scalars, (everyone(gram), coef, shift, f0, f1, t), (front, back, q), (2 * B, NX, NY)
+        scalars, (everyone(gram), coef, shift, f0, f1, q2, t), (front, back, q), (2 * B, NX, NY)
     )
     return solution.reshape(right_sides.shape), residue.reshape(right_sides.shape)
 

time: 146 us -> 158 us (1.082)
  waiting for transfers between devices: 37.6 us -> 46.7 us
  blocking collectives: 63.1 us -> 65.9 us
  Pallas kernels: 21.4 us -> 23.2 us
  starting transfers between devices: 20.7 us -> 18.9 us
    ppermute x7 -> x6, waiting for transfers between devices: 35.2 us -> 43.9 us  [beside(): across = lax.ppermute(values, GRID, edges + [(j, i) for i, j in edges])]
    ppermute x7 -> x6, starting transfers between devices: 19.6 us -> 13.5 us  [beside(): across = lax.ppermute(values, GRID, edges + [(j, i) for i, j in edges])]
    ppermute x7 -> x6, starting transfers between devices: 0.96 us -> 4.39 us  [beside(): sibling = lax.ppermute(values, CORES, [(0, 1), (1, 0)])]
    all_to_all x2, blocking collectives: 36.3 us -> 38.5 us  [everyone(): return lax.all_to_all(spread, near, 0, 0, tiled=True)]
    pallas_call x12, Pallas kernels: 14 us -> 15.8 us  [call(): pl.pallas_call(kernel, out_shape=[pltpu.VMEM(s, F32) for s in shapes], in...]
  transfers between devices with their start and end apart: 16 -> 16, of which waited for: 7 -> 8; matrix products, arithmetic and copies ran while one was open for 0% -> 0% of each run, Pallas kernels for 6% -> 4%
where the time goes in v6:
time: 158 us
  blocking collectives  65.9 us (42%)
  waiting for transfers between devices  46.7 us (30%)
  Pallas kernels  23.2 us (15%)
  starting transfers between devices  18.9 us (12%)
  local copies, waits for them, and re-layouts  1.98 us (1%)
    ppermute x6, waiting for transfers between devices, beside(): across = lax.ppermute(values, GRID, edges + [(j, i) for i, j in edges])  43.9 us
    all_to_all x2, blocking collectives, everyone(): return lax.all_to_all(spread, near, 0, 0, tiled=True)  38.5 us
    all_to_all x2, blocking collectives, everyone(): parts = lax.all_to_all(spread, far, 0, 0, tiled=True)  27.4 us
    pallas_call x12, Pallas kernels, call(): pl.pallas_call(kernel, out_shape=[pltpu.VMEM(s, F32) for s in shapes], in...  15.8 us
    ppermute x6, starting transfers between devices, beside(): across = lax.ppermute(values, GRID, edges + [(j, i) for i, j in edges])  13.5 us
    pallas_call x1, Pallas kernels, finish(): pl.pallas_call(finish_kernel, out_shape=[jax.ShapeDtypeStruct(shape, F32)...  7.37 us
    ppermute x6, starting transfers between devices, beside(): sibling = lax.ppermute(values, CORES, [(0, 1), (1, 0)])  4.39 us
  transfers between devices with their start and end apart: 16, of which 8 were waited for; matrix products, arithmetic and copies ran while one was open for 0% of the time, Pallas kernels for 4%

profile of v6, /device:TPU:8, one launch (start us, length us, event | category | flops | bytes accessed | tf_op | source)
XLA Modules:
  0.0 157.8 jit_solution(10515181379538704694)
XLA Ops:
  0.6 0.0 copy-start.3
  0.6 1.5 copy.17
  2.1 0.0 copy-done.3
  2.1 0.1 fusion
  2.2 0.2 copy.18
  2.4 0.0 copy-start
  2.4 0.0 copy-start.1
  2.4 0.0 copy-start.2
  2.5 0.1 maximum_bitcast_fusion.ub.u1_far
  2.6 0.1 collective-permute-start.2
  2.7 5.8 %collective-permute-start.1 = (f32[48,56,128]{2,1,0:T(8,128)S(1)}, f32[48,56,128]{2,1,0:T(8,128)}, u32[]{:S(2)}, u32[]{:S(2)}) collective-permute-start(f32[48,56,128]{2,1,0:T(8,128)S(1)} %maximum_bitcast_fusion.ub.u1_far), channel_id=1, source_target_pairs={{1,2},{3,4},{5,6},{7,8},{9,10},{11,12},{13,14},{15,16},{17,18},{19... | collective-permute-start | bytes 4128776 | tf_op jit(solution)/shard_map/ppermute | solution.py:572
  8.5 0.2 copy.19
  8.7 0.1 collective-permute-start
  8.8 0.1 add_select_fusion.inside
  8.9 0.0 collective-permute-done.2.sibling
  8.9 15.7 %collective-permute-done.1.across = f32[48,56,128]{2,1,0:T(8,128)} collective-permute-done((f32[48,56,128]{2,1,0:T(8,128)S(1)}, f32[48,56,128]{2,1,0:T(8,128)}, u32[]{:S(2)}, u32[]{:S(2)}) %collective-permute-start.1) | collective-permute-done | bytes 1376288 | tf_op jit(solution)/shard_map/ppermute | solution.py:572
  24.6 0.0 copy-done
  24.6 0.0 copy-done.1
  24.6 0.0 copy-done.2
  24.6 2.1 %back_kernel.1 = (f32[48,24,128]{2,1,0:T(8,128)S(1)}, f32[48,32,128]{2,1,0:T(8,128)S(1)}, f32[48,32,128]{2,1,0:T(8,128)S(1)}) custom-call(f32[8]{0:T(128)S(1)} %copy-done.1, s32[2]{0:T(128)S(1)} %copy-done.2, f32[2]{0:T(128)S(1)} %add_select_fusion.inside, f32[48,56,128]{2,1,0:T(8,128)S(1)} %maximum_bitcast_fusion.ub.u1_far, ...), custom_call_target="tpu_custom_call" | custom-call | tf_op jit(solution)/shard_map/back_kernel/pallas_call | solution.py:522
  26.8 0.1 collective-permute-start.3
  26.9 0.5 collective-permute-start.4
  27.4 3.9 %collective-permute-start.7 = (f32[48,24,128]{2,1,0:T(8,128)S(1)}, f32[48,24,128]{2,1,0:T(8,128)S(1)}, u32[]{:S(2)}, u32[]{:S(2)}) collective-permute-start(f32[48,24,128]{2,1,0:T(8,128)S(1)} %get-tuple-element.19.f1), channel_id=1, source_target_pairs={{1,2},{3,4},{5,6},{7,8},{9,10},{11,12},{13,14},{15,16},{17,18},{19... | collective-permute-start | bytes 1769480 | tf_op jit(solution)/shard_map/ppermute | solution.py:572
  31.2 0.0 collective-permute-done.across
  31.2 0.0 collective-permute-done.3.f1_sibling
  31.2 0.0 collective-permute-done.4.sibling
  31.2 1.5 front_kernel.1.f0
  32.7 0.1 collective-permute-start.6
  32.8 3.6 %collective-permute-start.5 = (f32[48,24,128]{2,1,0:T(8,128)S(1)}, f32[48,24,128]{2,1,0:T(8,128)S(1)}, u32[]{:S(2)}, u32[]{:S(2)}) collective-permute-start(f32[48,24,128]{2,1,0:T(8,128)S(1)} %front_kernel.1.f0), channel_id=1, source_target_pairs={{1,2},{3,4},{5,6},{7,8},{9,10},{11,12},{13,14},{15,16},{17,18},{19... | collective-permute-start | bytes 1769480 | tf_op jit(solution)/shard_map/ppermute | solution.py:572
  36.4 1.1 first_gram_kernel.1.first
  37.6 1.2 collective-permute-done.7.f1_across
  38.8 0.0 collective-permute-done.6.f0_sibling
  38.8 6.3 %collective-permute-done.5.f0_across = f32[48,24,128]{2,1,0:T(8,128)S(1)} collective-permute-done((f32[48,24,128]{2,1,0:T(8,128)S(1)}, f32[48,24,128]{2,1,0:T(8,128)S(1)}, u32[]{:S(2)}, u32[]{:S(2)}) %collective-permute-start.5) | collective-permute-done | bytes 589856 | tf_op jit(solution)/shard_map/ppermute | solution.py:572
  45.1 1.2 next_kernel.1.fields
  46.3 1.1 second_gram_kernel.1.one
  47.4 0.1 collective-permute-start.8
  47.5 1.2 collective-permute-done.8.two
  48.7 16.1 %all_to_all.20.parts = f32[8,48,128]{2,1,0:T(8,128)S(1)} all-to-all(f32[8,48,128]{2,1,0:T(8,128)S(1)} %add_kernel.2), channel_id=1, replica_groups=mesh['grid_0'=4,'grid_1'=4,'grid_2'=8,'grid_3'=2] {'grid_2'}, dimensions={0} | all-to-all | bytes 393216 | tf_op jit(solution)/shard_map/all_to_all | solution.py:564
  64.8 20.9 %all_to_all.21.grams = f32[16,48,128]{2,1,0:T(8,128)S(1)} all-to-all(f32[16,48,128]{2,1,0:T(8,128)S(1)} %respread_kernel.2), channel_id=1, replica_groups=mesh['grid_0'=4,'grid_1'=4,'grid_2'=8,'grid_3'=2] {'grid_0','grid_1'}, dimensions={0} | all-to-all | bytes 786432 | tf_op jit(solution)/shard_map/all_to_all | solution.py:566
  85.7 3.1 %krylov_kernel.1 = (f32[48,64,128]{2,1,0:T(8,128)S(1)}, f32[48,32,128]{2,1,0:T(8,128)S(1)}, f32[2,96,128]{2,1,0:T(8,128)S(1)}, f32[16,128]{1,0:T(8,128)S(1)}) custom-call(f32[16,48,128]{2,1,0:T(8,128)S(1)} %all_to_all.21.grams, f32[48,24,128]{2,1,0:T(8,128)S(1)} %front_kernel.1.f0, f32[48,24,128]{2,1,0:T(8,128)S(1)} %get-tuple-element.19.f1, ...), custom_call_target="tpu_custom_call" | custom-call | tf_op jit(solution)/shard_map/krylov_kernel/pallas_call | solution.py:522
  88.9 0.1 collective-permute-start.9
  89.0 0.8 collective-permute-start.11
  89.8 3.1 %collective-permute-start.10 = (f32[48,32,128]{2,1,0:T(8,128)S(1)}, f32[48,32,128]{2,1,0:T(8,128)S(1)}, u32[]{:S(2)}, u32[]{:S(2)}) collective-permute-start(f32[48,32,128]{2,1,0:T(8,128)S(1)} %get-tuple-element.24.last), channel_id=1, source_target_pairs={{0,1},{1,0},{2,3},{3,2},{4,5},{5,4},{6,7},{7,6},{8,9},{9,8},{10,11... | collective-permute-start | bytes 2359304 | tf_op jit(solution)/shard_map/ppermute | solution.py:573
  92.9 17.1 %collective-permute-done.9.across = f32[48,32,128]{2,1,0:T(8,128)S(1)} collective-permute-done((f32[48,32,128]{2,1,0:T(8,128)S(1)}, f32[48,32,128]{2,1,0:T(8,128)S(1)}, u32[]{:S(2)}, u32[]{:S(2)}) %collective-permute-start.9) | collective-permute-done | bytes 786464 | tf_op jit(solution)/shard_map/ppermute | solution.py:572
  110.1 0.0 collective-permute-start.12
  110.1 0.5 collective-permute-start.14
  110.6 0.0 collective-permute-start.13
  110.6 1.4 basis_gram_kernel.1.basis_gram
  111.9 0.4 collective-permute-done.14.medium_sibling
  112.4 3.6 %collective-permute-done.13.medium_across = f32[48,128]{1,0:T(8,128)S(1)} collective-permute-done((f32[48,128]{1,0:T(8,128)S(1)}, f32[48,128]{1,0:T(8,128)S(1)}, u32[]{:S(2)}, u32[]{:S(2)}) %collective-permute-start.13) | collective-permute-done | bytes 24608 | tf_op jit(solution)/shard_map/ppermute | solution.py:572
  115.9 0.0 collective-permute-done.11.past_across
  115.9 0.0 collective-permute-done.10.sibling
  115.9 0.0 collective-permute-done.12.past_sibling
  116.0 4.1 %moment_kernel.1 = (f32[48,32,128]{2,1,0:T(8,128)S(1)}, f32[48,32,128]{2,1,0:T(8,128)S(1)}, f32[24,128]{1,0:T(8,128)S(1)}) custom-call(f32[2]{0:T(128)S(1)} %add_select_fusion.inside, f32[48,64,128]{2,1,0:T(8,128)S(1)} %get-tuple-element.23.q.q_far, f32[48,32,128]{2,1,0:T(8,128)S(1)} %get-tuple-element.24.last, ...), custom_call_target="tpu_custom_call" | custom-call | tf_op jit(solution)/shard_map/moment_kernel/pallas_call | solution.py:522
  120.1 0.1 collective-permute-start.15
  120.2 1.2 collective-permute-done.15.two
  121.4 11.4 %all_to_all.22.parts = f32[8,24,128]{2,1,0:T(8,128)S(1)} all-to-all(f32[8,24,128]{2,1,0:T(8,128)S(1)} %add_kernel.3), channel_id=1, replica_groups=mesh['grid_0'=4,'grid_1'=4,'grid_2'=8,'grid_3'=2] {'grid_2'}, dimensions={0} | all-to-all | bytes 196608 | tf_op jit(solution)/shard_map/all_to_all | solution.py:564
  132.7 17.6 %all_to_all.23.moments = f32[16,24,128]{2,1,0:T(8,128)S(1)} all-to-all(f32[16,24,128]{2,1,0:T(8,128)S(1)} %respread_kernel.3), channel_id=1, replica_groups=mesh['grid_0'=4,'grid_1'=4,'grid_2'=8,'grid_3'=2] {'grid_0','grid_1'}, dimensions={0} | all-to-all | bytes 393216 | tf_op jit(solution)/shard_map/all_to_all | solution.py:566
  150.3 7.4 %finish_kernel.1 = (f32[32,48,128]{2,1,0:T(8,128)}, f32[32,48,128]{2,1,0:T(8,128)}) custom-call(f32[8]{0:T(128)S(1)} %copy-done.1, s32[2]{0:T(128)S(1)} %copy-done.2, f32[16,24,128]{2,1,0:T(8,128)S(1)} %all_to_all.23.moments, f32[2,96,128]{2,1,0:T(8,128)S(1)} %get-tuple-element.25.coef, f32[16,128]{1,0:T(8,128)S(1)} %get-tuple-element.26.shift, ...), custom_call_target="tpu_custom_call" | custom-call | tf_op jit(solution)/shard_map/finish_kernel/pallas_call | solution.py:535
  (4 shorter events, 0.1 us)
Async XLA Ops:
  0.6 1.5 copy-start.3
  2.4 22.2 %copy-start = (f32[1,48,128]{2,1,0:T(8,128)S(1)}, f32[1,48,128]{2,1,0:T(8,128)}, u32[]{:S(2)}) copy-start(f32[1,48,128]{2,1,0:T(8,128)} %param.7) | copy-start | bytes 73732
  2.4 22.2 %copy-start.1 = (f32[8]{0:T(128)S(1)}, f32[8]{0:T(128)}, u32[]{:S(2)}) copy-start(f32[8]{0:T(128)} %table.5) | copy-start | bytes 100
  2.4 22.2 %copy-start.2 = (s32[2]{0:T(128)S(1)}, s32[2]{0:T(128)}, u32[]{:S(2)}) copy-start(s32[2]{0:T(128)} %index.5) | copy-start | bytes 28
  2.6 6.3 %collective-permute-start.2 = (f32[48,56,128]{2,1,0:T(8,128)S(1)}, f32[48,56,128]{2,1,0:T(8,128)S(1)}, u32[]{:S(2)}, u32[]{:S(2)}) collective-permute-start(f32[48,56,128]{2,1,0:T(8,128)S(1)} %maximum_bitcast_fusion.ub.u1_far), channel_id=1, source_target_pairs={{0,1},{1,0},{2,3},{3,2},{4,5},{5,4},{6,7},{7,6},{8,9},{9,8},{10,11... | collective-permute-start | bytes 4128776 | tf_op jit(solution)/shard_map/ppermute | solution.py:573
  2.7 21.9 %collective-permute-start.1 = (f32[48,56,128]{2,1,0:T(8,128)S(1)}, f32[48,56,128]{2,1,0:T(8,128)}, u32[]{:S(2)}, u32[]{:S(2)}) collective-permute-start(f32[48,56,128]{2,1,0:T(8,128)S(1)} %maximum_bitcast_fusion.ub.u1_far), channel_id=1, source_target_pairs={{1,2},{3,4},{5,6},{7,8},{9,10},{11,12},{13,14},{15,16},{17,18},{19... | collective-permute-start | bytes 4128776 | tf_op jit(solution)/shard_map/ppermute | solution.py:572
  8.7 22.5 %collective-permute-start = (f32[48,24,128]{2,1,0:T(8,128)S(1)}, f32[48,24,128]{2,1,0:T(8,128)}, u32[]{:S(2)}, u32[]{:S(2)}) collective-permute-start(f32[48,24,128]{2,1,0:T(8,128)S(1)} %bitcast.22), channel_id=1, source_target_pairs={{1,2},{3,4},{5,6},{7,8},{9,10},{11,12},{13,14},{15,16},{17,18},{19... | collective-permute-start | bytes 1769480 | tf_op jit(solution)/shard_map/ppermute | solution.py:572
  26.8 4.5 %collective-permute-start.3 = (f32[48,24,128]{2,1,0:T(8,128)S(1)}, f32[48,24,128]{2,1,0:T(8,128)S(1)}, u32[]{:S(2)}, u32[]{:S(2)}) collective-permute-start(f32[48,24,128]{2,1,0:T(8,128)S(1)} %get-tuple-element.19.f1), channel_id=1, source_target_pairs={{0,1},{1,0},{2,3},{3,2},{4,5},{5,4},{6,7},{7,6},{8,9},{9,8},{10,11... | collective-permute-start | bytes 1769480 | tf_op jit(solution)/shard_map/ppermute | solution.py:573
  26.9 4.4 %collective-permute-start.4 = (f32[48,24,128]{2,1,0:T(8,128)S(1)}, f32[48,24,128]{2,1,0:T(8,128)S(1)}, u32[]{:S(2)}, u32[]{:S(2)}) collective-permute-start(f32[48,24,128]{2,1,0:T(8,128)S(1)} %bitcast.23), channel_id=1, source_target_pairs={{0,1},{1,0},{2,3},{3,2},{4,5},{5,4},{6,7},{7,6},{8,9},{9,8},{10,11... | collective-permute-start | bytes 1769480 | tf_op jit(solution)/shard_map/ppermute | solution.py:573
  27.4 11.4 %collective-permute-start.7 = (f32[48,24,128]{2,1,0:T(8,128)S(1)}, f32[48,24,128]{2,1,0:T(8,128)S(1)}, u32[]{:S(2)}, u32[]{:S(2)}) collective-permute-start(f32[48,24,128]{2,1,0:T(8,128)S(1)} %get-tuple-element.19.f1), channel_id=1, source_target_pairs={{1,2},{3,4},{5,6},{7,8},{9,10},{11,12},{13,14},{15,16},{17,18},{19... | collective-permute-start | bytes 1769480 | tf_op jit(solution)/shard_map/ppermute | solution.py:572
  32.7 6.1 %collective-permute-start.6 = (f32[48,24,128]{2,1,0:T(8,128)S(1)}, f32[48,24,128]{2,1,0:T(8,128)S(1)}, u32[]{:S(2)}, u32[]{:S(2)}) collective-permute-start(f32[48,24,128]{2,1,0:T(8,128)S(1)} %front_kernel.1.f0), channel_id=1, source_target_pairs={{0,1},{1,0},{2,3},{3,2},{4,5},{5,4},{6,7},{7,6},{8,9},{9,8},{10,11... | collective-permute-start | bytes 1769480 | tf_op jit(solution)/shard_map/ppermute | solution.py:573
  32.8 12.3 %collective-permute-start.5 = (f32[48,24,128]{2,1,0:T(8,128)S(1)}, f32[48,24,128]{2,1,0:T(8,128)S(1)}, u32[]{:S(2)}, u32[]{:S(2)}) collective-permute-start(f32[48,24,128]{2,1,0:T(8,128)S(1)} %front_kernel.1.f0), channel_id=1, source_target_pairs={{1,2},{3,4},{5,6},{7,8},{9,10},{11,12},{13,14},{15,16},{17,18},{19... | collective-permute-start | bytes 1769480 | tf_op jit(solution)/shard_map/ppermute | solution.py:572
  47.4 1.3 collective-permute-start.8
  88.9 21.2 %collective-permute-start.9 = (f32[48,32,128]{2,1,0:T(8,128)S(1)}, f32[48,32,128]{2,1,0:T(8,128)S(1)}, u32[]{:S(2)}, u32[]{:S(2)}) collective-permute-start(f32[48,32,128]{2,1,0:T(8,128)S(1)} %get-tuple-element.24.last), channel_id=1, source_target_pairs={{1,2},{3,4},{5,6},{7,8},{9,10},{11,12},{13,14},{15,16},{17,18},{19... | collective-permute-start | bytes 2359304 | tf_op jit(solution)/shard_map/ppermute | solution.py:572
  89.0 27.0 %collective-permute-start.11 = (f32[48,32,128]{2,1,0:T(8,128)S(1)}, f32[48,32,128]{2,1,0:T(8,128)S(1)}, u32[]{:S(2)}, u32[]{:S(2)}) collective-permute-start(f32[48,32,128]{2,1,0:T(8,128)S(1)} %get-tuple-element.24.last), channel_id=1, source_target_pairs={{0,2},{1,255},{2,4},{3,1},{4,6},{5,3},{6,8},{7,5},{8,10},{9,7},{10... | collective-permute-start | bytes 2359304 | tf_op jit(solution)/shard_map/ppermute | solution.py:579
  89.8 26.1 %collective-permute-start.10 = (f32[48,32,128]{2,1,0:T(8,128)S(1)}, f32[48,32,128]{2,1,0:T(8,128)S(1)}, u32[]{:S(2)}, u32[]{:S(2)}) collective-permute-start(f32[48,32,128]{2,1,0:T(8,128)S(1)} %get-tuple-element.24.last), channel_id=1, source_target_pairs={{0,1},{1,0},{2,3},{3,2},{4,5},{5,4},{6,7},{7,6},{8,9},{9,8},{10,11... | collective-permute-start | bytes 2359304 | tf_op jit(solution)/shard_map/ppermute | solution.py:573
  110.1 5.9 %collective-permute-start.12 = (f32[48,32,128]{2,1,0:T(8,128)S(1)}, f32[48,32,128]{2,1,0:T(8,128)S(1)}, u32[]{:S(2)}, u32[]{:S(2)}) collective-permute-start(f32[48,32,128]{2,1,0:T(8,128)S(1)} %collective-permute-done.9.across), channel_id=1, source_target_pairs={{0,1},{1,0},{2,3},{3,2},{4,5},{5,4},{6,7},{7,6},{8,9},{9,8},{10,11... | collective-permute-start | bytes 2359304 | tf_op jit(solution)/shard_map/ppermute | solution.py:631
  110.1 2.3 %collective-permute-start.14 = (f32[48,128]{1,0:T(8,128)S(1)}, f32[48,128]{1,0:T(8,128)S(1)}, u32[]{:S(2)}, u32[]{:S(2)}) collective-permute-start(f32[48,128]{1,0:T(8,128)S(1)} %bitcast.29), channel_id=1, source_target_pairs={{0,1},{1,0},{2,3},{3,2},{4,5},{5,4},{6,7},{7,6},{8,9},{9,8},{10,11... | collective-permute-start | bytes 73736 | tf_op jit(solution)/shard_map/ppermute | solution.py:573
  110.6 5.4 %collective-permute-start.13 = (f32[48,128]{1,0:T(8,128)S(1)}, f32[48,128]{1,0:T(8,128)S(1)}, u32[]{:S(2)}, u32[]{:S(2)}) collective-permute-start(f32[48,128]{1,0:T(8,128)S(1)} %bitcast.30), channel_id=1, source_target_pairs={{1,2},{3,4},{5,6},{7,8},{9,10},{11,12},{13,14},{15,16},{17,18},{19... | collective-permute-start | bytes 73736 | tf_op jit(solution)/shard_map/ppermute | solution.py:572
  120.1 1.3 collective-permute-start.15

commit v7 on v5

--- a/solution.py
+++ b/solution.py
@@ -86,20 +86,35 @@
     def column(k):
         return jnp.where(lane < 64, system[:, k : k + 1], system[:, 64 + k : 65 + k])
 
-    for k in range(0, count, 2):
+    for k in range(0, count, 4):
         if meanwhile is not None:
-            meanwhile(k // 2)
-        one = system[k : k + 1]
-        two = system[k + 1 : k + 2]
-        left = column(k)
-        right = column(k + 1)
-        a, b = left[k : k + 1], right[k : k + 1]
-        c, d = left[k + 1 : k + 2], right[k + 1 : k + 2]
-        inverse = 1.0 / (a * d - b * c)
-        new_one = (d * inverse) * one - (b * inverse) * two
-        new_two = (a * inverse) * two - (c * inverse) * one
-        changed = system - left * new_one - right * new_two
-        system = jnp.where(row == k, new_one, jnp.where(row == k + 1, new_two, changed))
+            meanwhile(k // 4)
+        rows = [system[k + i : k + i + 1] for i in range(4)]
+        columns = [column(k + i) for i in range(4)]
+        p = [[c[k + i : k + i + 1] for c in columns] for i in range(4)]
+        inverse = 1.0 / (p[0][0] * p[1][1] - p[0][1] * p[1][0])
+        a, b = p[1][1] * inverse, p[0][1] * inverse
+        c, d = p[1][0] * inverse, p[0][0] * inverse
+        one = a * rows[0] - b * rows[1]
+        two = d * rows[1] - c * rows[0]
+        three, four = (rows[i] - p[i][0] * one - p[i][1] * two for i in (2, 3))
+        over = [[a * p[0][i] - b * p[1][i], d * p[1][i] - c * p[0][i]] for i in (2, 3)]
+        (e, f), (g, h) = (
+            [p[i][m + 2] - p[i][0] * over[m][0] - p[i][1] * over[m][1] for m in range(2)]
+            for i in (2, 3)
+        )
+        inverse = 1.0 / (e * h - f * g)
+        three, four = (
+            (h * inverse) * three - (f * inverse) * four,
+            (e * inverse) * four - (g * inverse) * three,
+        )
+        one = one - over[0][0] * three - over[1][0] * four
+        two = two - over[0][1] * three - over[1][1] * four
+        made = (one, two, three, four)
+        for i in range(4):
+            system = system - columns[i] * made[i]
+        for i in range(4):
+            system = jnp.where(row == k + i, made[i], system)
     return system
 
 
@@ -192,7 +207,9 @@
     return lambda x: ref[x]
 
 
-def next_kernel(inside, f0, f0_across, f0_sibling, f1, f1_across, f1_sibling, medium, fields_out):
+def next_kernel(
+    inside, f0, f0_across, f0_sibling, f1, f1_across, f1_sibling, medium, first, fields_out
+):
     for g, (own, across, sibling) in enumerate(
         ((f0, f0_across, f0_sibling), (f1, f1_across, f1_sibling))
     ):
@@ -248,7 +265,7 @@
     next_b = stencil(plain, rows_of(b1), rows_of(b1_across), rows_of(b1_sibling), inside)
 
     def meanwhile(step):
-        for x in range(4 * step, 4 * step + 4):
+        for x in range(8 * step, 8 * step + 8):
             f_next[x] = next_f(x)
             b_next[x] = next_b(x)
 
@@ -557,13 +574,14 @@
         out[i] = total
 
 
-def everyone(values):
+def everyone(values, beside_it=()):
     far, near = STAGES
     other = lax.ppermute(values, CORES, [(0, 1), (1, 0)])
+    other, beside_it = lax.optimization_barrier((other, beside_it))
     (spread,) = call(add_kernel, [(lax.axis_size(far), *values.shape)], 0, values, other)
     parts = lax.all_to_all(spread, far, 0, 0, tiled=True)
     (spread,) = call(respread_kernel, [(lax.axis_size(near), *values.shape)], 0, parts)
-    return lax.all_to_all(spread, near, 0, 0, tiled=True)
+    return lax.all_to_all(spread, near, 0, 0, tiled=True), beside_it
 
 
 def beside(values):
@@ -605,16 +623,18 @@
     f0_sides = beside(f0)
     b1_sides = beside(b1)
     (first,) = call(first_gram_kernel, [(K, 128)], 0, f0, f1, b, b1)
-    (fields,) = call(next_kernel, [(NX, 2 * K, NY)], 1, inside, f0, *f0_sides, f1, *f1_sides, med)
+    (fields,) = call(
+        next_kernel, [(NX, 2 * K, NY)], 1, inside, f0, *f0_sides, f1, *f1_sides, med, first
+    )
     field_sides = beside(fields)
     (gram,) = call(second_gram_kernel, [(2 * K, 128)], 0, f0, f1, fields, b1, first)
-    gram, b1_sides = lax.optimization_barrier((gram, b1_sides))
+    grams, b1_sides = everyone(gram, b1_sides)
     q, last, coef, shift = call(
         krylov_kernel,
         [(NX, 96, NY), (NX, 2 * B, NY), (2, 96, 128), (16, 128)],
         1,
         inside,
-        everyone(gram),
+        grams,
         f0,
         f1,
         b,
@@ -639,7 +659,7 @@
         shift,
     )
     solution, residue = finish(
-        scalars, (everyone(gram), coef, shift, f0, f1, t), (front, back, q), (2 * B, NX, NY)
+        scalars, (everyone(gram)[0], coef, shift, f0, f1, t), (front, back, q), (2 * B, NX, NY)
     )
     return solution.reshape(right_sides.shape), residue.reshape(right_sides.shape)
 

time: 146 us -> 145 us (level)
  waiting for transfers between devices: 37.6 us -> 36.1 us
  transfers between devices with their start and end apart: 16 -> 16, of which waited for: 7 -> 6; matrix products, arithmetic and copies ran while one was open for 0% -> 0% of each run, Pallas kernels for 6% -> 6%
where the time goes in v7:
time: 145 us
  blocking collectives  63.1 us (44%)
  waiting for transfers between devices  36.1 us (25%)
  starting transfers between devices  21.7 us (15%)
  Pallas kernels  20.5 us (14%)
  local copies, waits for them, and re-layouts  1.98 us (1%)
    all_to_all x2, blocking collectives, everyone(): return (lax.all_to_all(spread, near, 0, 0, tiled=True), beside_it)  35.1 us
    ppermute x7, waiting for transfers between devices, beside(): across = lax.ppermute(values, GRID, edges + [(j, i) for i, j in edges])  34.9 us
    all_to_all x2, blocking collectives, everyone(): parts = lax.all_to_all(spread, far, 0, 0, tiled=True)  28 us
    ppermute x7, starting transfers between devices, beside(): across = lax.ppermute(values, GRID, edges + [(j, i) for i, j in edges])  19.8 us
    pallas_call x12, Pallas kernels, call(): pl.pallas_call(kernel, out_shape=[pltpu.VMEM(s, F32) for s in shapes], in...  13.6 us
    pallas_call x1, Pallas kernels, finish(): pl.pallas_call(finish_kernel, out_shape=[jax.ShapeDtypeStruct(shape, F32)...  6.97 us
  transfers between devices with their start and end apart: 16, of which 6 were waited for; matrix products, arithmetic and copies ran while one was open for 0% of the time, Pallas kernels for 6%

profile of v7, /device:TPU:8, one launch (start us, length us, event | category | flops | bytes accessed | tf_op | source)
XLA Modules:
  0.0 144.5 jit_solution(10562933609115043484)
XLA Ops:
  0.6 0.0 copy-start.3
  0.6 1.5 %copy.17 = f32[32,1,48,128]{3,0,2,1:T(8,128)S(1)} copy(f32[32,1,48,128]{3,2,1,0:T(8,128)} %param.5) | data formatting | bytes 1572864 | tf_op args[0]
  2.1 0.0 copy-done.3
  2.1 0.1 fusion
  2.2 0.2 copy.18
  2.4 0.0 copy-start
  2.4 0.0 copy-start.1
  2.4 0.0 copy-start.2
  2.5 0.1 maximum_bitcast_fusion.ub.u1_far
  2.6 0.1 collective-permute-start.2
  2.7 5.8 %collective-permute-start.1 = (f32[48,56,128]{2,1,0:T(8,128)S(1)}, f32[48,56,128]{2,1,0:T(8,128)}, u32[]{:S(2)}, u32[]{:S(2)}) collective-permute-start(f32[48,56,128]{2,1,0:T(8,128)S(1)} %maximum_bitcast_fusion.ub.u1_far), channel_id=1, source_target_pairs={{1,2},{3,4},{5,6},{7,8},{9,10},{11,12},{13,14},{15,16},{17,18},{19... | collective-permute-start | bytes 4128776 | tf_op jit(solution)/shard_map/ppermute | solution.py:590
  8.5 0.2 copy.19
  8.7 0.1 collective-permute-start
  8.8 0.0 collective-permute-done.2.sibling
  8.8 15.8 %collective-permute-done.1.across = f32[48,56,128]{2,1,0:T(8,128)} collective-permute-done((f32[48,56,128]{2,1,0:T(8,128)S(1)}, f32[48,56,128]{2,1,0:T(8,128)}, u32[]{:S(2)}, u32[]{:S(2)}) %collective-permute-start.1) | collective-permute-done | bytes 1376288 | tf_op jit(solution)/shard_map/ppermute | solution.py:590
  24.6 0.0 copy-done
  24.6 0.0 copy-done.1
  24.6 0.0 copy-done.2
  24.6 2.1 %back_kernel.1 = (f32[48,24,128]{2,1,0:T(8,128)S(1)}, f32[48,32,128]{2,1,0:T(8,128)S(1)}, f32[48,32,128]{2,1,0:T(8,128)S(1)}) custom-call(f32[8]{0:T(128)S(1)} %copy-done.1, s32[2]{0:T(128)S(1)} %copy-done.2, f32[1]{0:T(128)} %bitcast.inside, f32[48,56,128]{2,1,0:T(8,128)S(1)} %maximum_bitcast_fusion.ub.u1_far, ...), custom_call_target="tpu_custom_call" | custom-call | tf_op jit(solution)/shard_map/back_kernel/pallas_call | solution.py:539
  26.8 0.1 collective-permute-start.3
  26.9 0.5 collective-permute-start.4
  27.4 3.9 %collective-permute-start.7 = (f32[48,24,128]{2,1,0:T(8,128)S(1)}, f32[48,24,128]{2,1,0:T(8,128)S(1)}, u32[]{:S(2)}, u32[]{:S(2)}) collective-permute-start(f32[48,24,128]{2,1,0:T(8,128)S(1)} %get-tuple-element.21.f1), channel_id=1, source_target_pairs={{1,2},{3,4},{5,6},{7,8},{9,10},{11,12},{13,14},{15,16},{17,18},{19... | collective-permute-start | bytes 1769480 | tf_op jit(solution)/shard_map/ppermute | solution.py:590
  31.2 0.0 collective-permute-done.across
  31.2 0.0 collective-permute-done.3.f1_sibling
  31.2 0.0 collective-permute-done.4.sibling
  31.2 1.5 %front_kernel.1.f0 = f32[48,24,128]{2,1,0:T(8,128)S(1)} custom-call(f32[8]{0:T(128)S(1)} %copy-done.1, s32[2]{0:T(128)S(1)} %copy-done.2, f32[1]{0:T(128)} %bitcast.inside, f32[48,24,128]{2,1,0:T(8,128)S(1)} %bitcast.23, f32[48,24,128]{2,1,0:T(8,128)} %collective-permute-done.across, f32[48,24,128]{2,1,0:T(8,128)S(1)} %collective-permute-done.4.sibling, ...), custom_call_target="tpu_custom_call" | custom-call | tf_op jit(solution)/shard_map/front_kernel/pallas_call | solution.py:539
  32.7 0.1 collective-permute-start.6
  32.8 3.6 %collective-permute-start.5 = (f32[48,24,128]{2,1,0:T(8,128)S(1)}, f32[48,24,128]{2,1,0:T(8,128)S(1)}, u32[]{:S(2)}, u32[]{:S(2)}) collective-permute-start(f32[48,24,128]{2,1,0:T(8,128)S(1)} %front_kernel.1.f0), channel_id=1, source_target_pairs={{1,2},{3,4},{5,6},{7,8},{9,10},{11,12},{13,14},{15,16},{17,18},{19... | collective-permute-start | bytes 1769480 | tf_op jit(solution)/shard_map/ppermute | solution.py:590
  36.4 0.0 collective-permute-start.10
  36.4 0.4 collective-permute-start.9
  36.9 1.2 first_gram_kernel.1.first
  38.0 0.7 collective-permute-done.7.f1_across
  38.8 0.0 collective-permute-done.6.f0_sibling
  38.8 6.3 %collective-permute-done.5.f0_across = f32[48,24,128]{2,1,0:T(8,128)S(1)} collective-permute-done((f32[48,24,128]{2,1,0:T(8,128)S(1)}, f32[48,24,128]{2,1,0:T(8,128)S(1)}, u32[]{:S(2)}, u32[]{:S(2)}) %collective-permute-start.5) | collective-permute-done | bytes 589856 | tf_op jit(solution)/shard_map/ppermute | solution.py:590
  45.1 0.7 next_kernel.1.fields
  45.8 0.1 collective-permute-start.12
  45.9 3.9 %collective-permute-start.11 = (f32[48,48,128]{2,1,0:T(8,128)S(1)}, f32[48,48,128]{2,1,0:T(8,128)S(1)}, u32[]{:S(2)}, u32[]{:S(2)}) collective-permute-start(f32[48,48,128]{2,1,0:T(8,128)S(1)} %next_kernel.1.fields), channel_id=1, source_target_pairs={{1,2},{3,4},{5,6},{7,8},{9,10},{11,12},{13,14},{15,16},{17,18},{19... | collective-permute-start | bytes 3538952 | tf_op jit(solution)/shard_map/ppermute | solution.py:590
  49.9 1.1 second_gram_kernel.1.one
  51.0 0.1 collective-permute-start.8
  51.1 0.0 collective-permute-done.10.b1_sibling
  51.1 2.4 %collective-permute-done.9.b1_across = f32[48,32,128]{2,1,0:T(8,128)S(1)} collective-permute-done((f32[48,32,128]{2,1,0:T(8,128)S(1)}, f32[48,32,128]{2,1,0:T(8,128)S(1)}, u32[]{:S(2)}, u32[]{:S(2)}) %collective-permute-start.9) | collective-permute-done | bytes 786464 | tf_op jit(solution)/shard_map/ppermute | solution.py:590
  53.5 0.0 collective-permute-done.8.two
  53.5 16.7 %all_to_all.20.parts = f32[8,48,128]{2,1,0:T(8,128)S(1)} all-to-all(f32[8,48,128]{2,1,0:T(8,128)S(1)} %add_kernel.2), channel_id=1, replica_groups=mesh['grid_0'=4,'grid_1'=4,'grid_2'=8,'grid_3'=2] {'grid_2'}, dimensions={0} | all-to-all | bytes 393216 | tf_op jit(solution)/shard_map/all_to_all | solution.py:582
  70.2 21.1 %all_to_all.21.grams = f32[16,48,128]{2,1,0:T(8,128)S(1)} all-to-all(f32[16,48,128]{2,1,0:T(8,128)S(1)} %respread_kernel.2), channel_id=1, replica_groups=mesh['grid_0'=4,'grid_1'=4,'grid_2'=8,'grid_3'=2] {'grid_0','grid_1'}, dimensions={0} | all-to-all | bytes 786432 | tf_op jit(solution)/shard_map/all_to_all | solution.py:584
  91.3 0.0 collective-permute-done.12.fields_sibling
  91.3 0.0 collective-permute-done.11.fields_across
  91.4 3.9 %krylov_kernel.1 = (f32[48,96,128]{2,1,0:T(8,128)S(1)}, f32[48,32,128]{2,1,0:T(8,128)S(1)}, f32[2,96,128]{2,1,0:T(8,128)S(1)}, f32[16,128]{1,0:T(8,128)S(1)}) custom-call(f32[1]{0:T(128)} %bitcast.inside, f32[16,48,128]{2,1,0:T(8,128)S(1)} %all_to_all.21.grams, f32[48,24,128]{2,1,0:T(8,128)S(1)} %front_kernel.1.f0, f32[48,24,128]{2,1,0:T(8,128)S(1)} %get-tuple-element.21.f1, ...), custom_call_target="tpu_custom_call" | custom-call | tf_op jit(solution)/shard_map/krylov_kernel/pallas_call | solution.py:539
  95.3 0.8 collective-permute-start.14
  96.1 2.0 %collective-permute-start.13 = (f32[48,32,128]{2,1,0:T(8,128)S(1)}, f32[48,32,128]{2,1,0:T(8,128)S(1)}, u32[]{:S(2)}, u32[]{:S(2)}) collective-permute-start(f32[48,32,128]{2,1,0:T(8,128)S(1)} %get-tuple-element.28.last), channel_id=1, source_target_pairs={{1,2},{3,4},{5,6},{7,8},{9,10},{11,12},{13,14},{15,16},{17,18},{19... | collective-permute-start | bytes 2359304 | tf_op jit(solution)/shard_map/ppermute | solution.py:590
  98.2 1.8 %basis_gram_kernel.1.basis_gram = f32[2,48,128]{2,1,0:T(8,128)S(1)} custom-call(f32[48,96,128]{2,1,0:T(8,128)S(1)} %get-tuple-element.29.q.q_far, f32[48,48,128]{2,1,0:T(8,128)S(1)} %next_kernel.1.fields), custom_call_target="tpu_custom_call" | custom-call | tf_op jit(solution)/shard_map/basis_gram_kernel/pallas_call | solution.py:539
  100.0 0.0 collective-permute-done.14.last_sibling
  100.0 9.6 %collective-permute-done.13.last_across = f32[48,32,128]{2,1,0:T(8,128)S(1)} collective-permute-done((f32[48,32,128]{2,1,0:T(8,128)S(1)}, f32[48,32,128]{2,1,0:T(8,128)S(1)}, u32[]{:S(2)}, u32[]{:S(2)}) %collective-permute-start.13) | collective-permute-done | bytes 786464 | tf_op jit(solution)/shard_map/ppermute | solution.py:590
  109.7 1.1 moment_kernel.1
  110.7 0.1 collective-permute-start.15
  110.8 1.2 collective-permute-done.15.two
  112.0 11.4 %all_to_all.22.parts = f32[8,24,128]{2,1,0:T(8,128)S(1)} all-to-all(f32[8,24,128]{2,1,0:T(8,128)S(1)} %add_kernel.3), channel_id=1, replica_groups=mesh['grid_0'=4,'grid_1'=4,'grid_2'=8,'grid_3'=2] {'grid_2'}, dimensions={0} | all-to-all | bytes 196608 | tf_op jit(solution)/shard_map/all_to_all | solution.py:582
  123.4 14.0 %all_to_all.23.moments = f32[16,24,128]{2,1,0:T(8,128)S(1)} all-to-all(f32[16,24,128]{2,1,0:T(8,128)S(1)} %respread_kernel.3), channel_id=1, replica_groups=mesh['grid_0'=4,'grid_1'=4,'grid_2'=8,'grid_3'=2] {'grid_0','grid_1'}, dimensions={0} | all-to-all | bytes 393216 | tf_op jit(solution)/shard_map/all_to_all | solution.py:584
  137.4 7.0 %finish_kernel.1 = (f32[32,48,128]{2,1,0:T(8,128)}, f32[32,48,128]{2,1,0:T(8,128)}) custom-call(f32[8]{0:T(128)S(1)} %copy-done.1, s32[2]{0:T(128)S(1)} %copy-done.2, f32[16,24,128]{2,1,0:T(8,128)S(1)} %all_to_all.23.moments, f32[2,96,128]{2,1,0:T(8,128)S(1)} %get-tuple-element.32.coef, f32[16,128]{1,0:T(8,128)S(1)} %get-tuple-element.30.shift, ...), custom_call_target="tpu_custom_call" | custom-call | tf_op jit(solution)/shard_map/finish_kernel/pallas_call | solution.py:552
  (4 shorter events, 0.1 us)
Async XLA Ops:
  0.6 1.5 %copy-start.3 = (f32[2,24,1,48,128]{4,3,2,1,0:T(8,128)S(1)}, f32[2,24,1,48,128]{4,3,2,1,0:T(8,128)}, u32[]{:S(2)}) copy-start(f32[2,24,1,48,128]{4,3,2,1,0:T(8,128)} %param.6) | copy-start | bytes 3538948
  2.4 22.2 %copy-start = (f32[1,48,128]{2,1,0:T(8,128)S(1)}, f32[1,48,128]{2,1,0:T(8,128)}, u32[]{:S(2)}) copy-start(f32[1,48,128]{2,1,0:T(8,128)} %param.7) | copy-start | bytes 73732
  2.4 22.2 %copy-start.1 = (f32[8]{0:T(128)S(1)}, f32[8]{0:T(128)}, u32[]{:S(2)}) copy-start(f32[8]{0:T(128)} %table.5) | copy-start | bytes 100
  2.4 22.2 %copy-start.2 = (s32[2]{0:T(128)S(1)}, s32[2]{0:T(128)}, u32[]{:S(2)}) copy-start(s32[2]{0:T(128)} %index.5) | copy-start | bytes 28
  2.6 6.3 %collective-permute-start.2 = (f32[48,56,128]{2,1,0:T(8,128)S(1)}, f32[48,56,128]{2,1,0:T(8,128)S(1)}, u32[]{:S(2)}, u32[]{:S(2)}) collective-permute-start(f32[48,56,128]{2,1,0:T(8,128)S(1)} %maximum_bitcast_fusion.ub.u1_far), channel_id=1, source_target_pairs={{0,1},{1,0},{2,3},{3,2},{4,5},{5,4},{6,7},{7,6},{8,9},{9,8},{10,11... | collective-permute-start | bytes 4128776 | tf_op jit(solution)/shard_map/ppermute | solution.py:591
  2.7 21.9 %collective-permute-start.1 = (f32[48,56,128]{2,1,0:T(8,128)S(1)}, f32[48,56,128]{2,1,0:T(8,128)}, u32[]{:S(2)}, u32[]{:S(2)}) collective-permute-start(f32[48,56,128]{2,1,0:T(8,128)S(1)} %maximum_bitcast_fusion.ub.u1_far), channel_id=1, source_target_pairs={{1,2},{3,4},{5,6},{7,8},{9,10},{11,12},{13,14},{15,16},{17,18},{19... | collective-permute-start | bytes 4128776 | tf_op jit(solution)/shard_map/ppermute | solution.py:590
  8.7 22.5 %collective-permute-start = (f32[48,24,128]{2,1,0:T(8,128)S(1)}, f32[48,24,128]{2,1,0:T(8,128)}, u32[]{:S(2)}, u32[]{:S(2)}) collective-permute-start(f32[48,24,128]{2,1,0:T(8,128)S(1)} %bitcast.21), channel_id=1, source_target_pairs={{1,2},{3,4},{5,6},{7,8},{9,10},{11,12},{13,14},{15,16},{17,18},{19... | collective-permute-start | bytes 1769480 | tf_op jit(solution)/shard_map/ppermute | solution.py:590
  26.8 4.5 %collective-permute-start.3 = (f32[48,24,128]{2,1,0:T(8,128)S(1)}, f32[48,24,128]{2,1,0:T(8,128)S(1)}, u32[]{:S(2)}, u32[]{:S(2)}) collective-permute-start(f32[48,24,128]{2,1,0:T(8,128)S(1)} %get-tuple-element.21.f1), channel_id=1, source_target_pairs={{0,1},{1,0},{2,3},{3,2},{4,5},{5,4},{6,7},{7,6},{8,9},{9,8},{10,11... | collective-permute-start | bytes 1769480 | tf_op jit(solution)/shard_map/ppermute | solution.py:591
  26.9 4.4 %collective-permute-start.4 = (f32[48,24,128]{2,1,0:T(8,128)S(1)}, f32[48,24,128]{2,1,0:T(8,128)S(1)}, u32[]{:S(2)}, u32[]{:S(2)}) collective-permute-start(f32[48,24,128]{2,1,0:T(8,128)S(1)} %bitcast.22), channel_id=1, source_target_pairs={{0,1},{1,0},{2,3},{3,2},{4,5},{5,4},{6,7},{7,6},{8,9},{9,8},{10,11... | collective-permute-start | bytes 1769480 | tf_op jit(solution)/shard_map/ppermute | solution.py:591
  27.4 11.4 %collective-permute-start.7 = (f32[48,24,128]{2,1,0:T(8,128)S(1)}, f32[48,24,128]{2,1,0:T(8,128)S(1)}, u32[]{:S(2)}, u32[]{:S(2)}) collective-permute-start(f32[48,24,128]{2,1,0:T(8,128)S(1)} %get-tuple-element.21.f1), channel_id=1, source_target_pairs={{1,2},{3,4},{5,6},{7,8},{9,10},{11,12},{13,14},{15,16},{17,18},{19... | collective-permute-start | bytes 1769480 | tf_op jit(solution)/shard_map/ppermute | solution.py:590
  32.7 6.1 %collective-permute-start.6 = (f32[48,24,128]{2,1,0:T(8,128)S(1)}, f32[48,24,128]{2,1,0:T(8,128)S(1)}, u32[]{:S(2)}, u32[]{:S(2)}) collective-permute-start(f32[48,24,128]{2,1,0:T(8,128)S(1)} %front_kernel.1.f0), channel_id=1, source_target_pairs={{0,1},{1,0},{2,3},{3,2},{4,5},{5,4},{6,7},{7,6},{8,9},{9,8},{10,11... | collective-permute-start | bytes 1769480 | tf_op jit(solution)/shard_map/ppermute | solution.py:591
  32.8 12.3 %collective-permute-start.5 = (f32[48,24,128]{2,1,0:T(8,128)S(1)}, f32[48,24,128]{2,1,0:T(8,128)S(1)}, u32[]{:S(2)}, u32[]{:S(2)}) collective-permute-start(f32[48,24,128]{2,1,0:T(8,128)S(1)} %front_kernel.1.f0), channel_id=1, source_target_pairs={{1,2},{3,4},{5,6},{7,8},{9,10},{11,12},{13,14},{15,16},{17,18},{19... | collective-permute-start | bytes 1769480 | tf_op jit(solution)/shard_map/ppermute | solution.py:590
  36.4 14.6 %collective-permute-start.10 = (f32[48,32,128]{2,1,0:T(8,128)S(1)}, f32[48,32,128]{2,1,0:T(8,128)S(1)}, u32[]{:S(2)}, u32[]{:S(2)}) collective-permute-start(f32[48,32,128]{2,1,0:T(8,128)S(1)} %get-tuple-element.24.b1), channel_id=1, source_target_pairs={{0,1},{1,0},{2,3},{3,2},{4,5},{5,4},{6,7},{7,6},{8,9},{9,8},{10,11... | collective-permute-start | bytes 2359304 | tf_op jit(solution)/shard_map/ppermute | solution.py:591
  36.4 17.1 %collective-permute-start.9 = (f32[48,32,128]{2,1,0:T(8,128)S(1)}, f32[48,32,128]{2,1,0:T(8,128)S(1)}, u32[]{:S(2)}, u32[]{:S(2)}) collective-permute-start(f32[48,32,128]{2,1,0:T(8,128)S(1)} %get-tuple-element.24.b1), channel_id=1, source_target_pairs={{1,2},{3,4},{5,6},{7,8},{9,10},{11,12},{13,14},{15,16},{17,18},{19... | collective-permute-start | bytes 2359304 | tf_op jit(solution)/shard_map/ppermute | solution.py:590
  45.8 45.5 %collective-permute-start.12 = (f32[48,48,128]{2,1,0:T(8,128)S(1)}, f32[48,48,128]{2,1,0:T(8,128)S(1)}, u32[]{:S(2)}, u32[]{:S(2)}) collective-permute-start(f32[48,48,128]{2,1,0:T(8,128)S(1)} %next_kernel.1.fields), channel_id=1, source_target_pairs={{0,1},{1,0},{2,3},{3,2},{4,5},{5,4},{6,7},{7,6},{8,9},{9,8},{10,11... | collective-permute-start | bytes 3538952 | tf_op jit(solution)/shard_map/ppermute | solution.py:591
  45.9 45.4 %collective-permute-start.11 = (f32[48,48,128]{2,1,0:T(8,128)S(1)}, f32[48,48,128]{2,1,0:T(8,128)S(1)}, u32[]{:S(2)}, u32[]{:S(2)}) collective-permute-start(f32[48,48,128]{2,1,0:T(8,128)S(1)} %next_kernel.1.fields), channel_id=1, source_target_pairs={{1,2},{3,4},{5,6},{7,8},{9,10},{11,12},{13,14},{15,16},{17,18},{19... | collective-permute-start | bytes 3538952 | tf_op jit(solution)/shard_map/ppermute | solution.py:590
  51.0 2.5 %collective-permute-start.8 = (f32[48,128]{1,0:T(8,128)S(1)}, f32[48,128]{1,0:T(8,128)S(1)}, u32[]{:S(2)}, u32[]{:S(2)}) collective-permute-start(f32[48,128]{1,0:T(8,128)S(1)} %second_gram_kernel.1.one), channel_id=1, source_target_pairs={{0,1},{1,0},{2,3},{3,2},{4,5},{5,4},{6,7},{7,6},{8,9},{9,8},{10,11... | collective-permute-start | bytes 73736 | tf_op jit(solution)/shard_map/ppermute | solution.py:579
  95.3 4.7 %collective-permute-start.14 = (f32[48,32,128]{2,1,0:T(8,128)S(1)}, f32[48,32,128]{2,1,0:T(8,128)S(1)}, u32[]{:S(2)}, u32[]{:S(2)}) collective-permute-start(f32[48,32,128]{2,1,0:T(8,128)S(1)} %get-tuple-element.28.last), channel_id=1, source_target_pairs={{0,1},{1,0},{2,3},{3,2},{4,5},{5,4},{6,7},{7,6},{8,9},{9,8},{10,11... | collective-permute-start | bytes 2359304 | tf_op jit(solution)/shard_map/ppermute | solution.py:591
  96.1 13.5 %collective-permute-start.13 = (f32[48,32,128]{2,1,0:T(8,128)S(1)}, f32[48,32,128]{2,1,0:T(8,128)S(1)}, u32[]{:S(2)}, u32[]{:S(2)}) collective-permute-start(f32[48,32,128]{2,1,0:T(8,128)S(1)} %get-tuple-element.28.last), channel_id=1, source_target_pairs={{1,2},{3,4},{5,6},{7,8},{9,10},{11,12},{13,14},{15,16},{17,18},{19... | collective-permute-start | bytes 2359304 | tf_op jit(solution)/shard_map/ppermute | solution.py:590
  110.7 1.3 collective-permute-start.15

commit v8 on v7

--- a/solution.py
+++ b/solution.py
@@ -224,7 +224,7 @@
             fields_out[x, K * g : K * g + K] = made(x)
 
 
-def second_gram_kernel(f0, f1, fields, b1, first, gram_out):
+def second_gram_kernel(core, f0, f1, fields, b1, first, kept_out, sent_out):
     total = jnp.zeros((2 * K, 128), F32)
     for x in range(0, NX, 2):
         nexts = pair(fields, x)
@@ -232,13 +232,17 @@
         right = [pair(f0, x), nexts[:K], b1_pair[:B], pair(f1, x), nexts[K:], b1_pair[B:]]
         total = total + row_products(nexts, jnp.concatenate(right, axis=0))
     lane = iota((K, 128), 1)
-    gram_out[:K] = first[...]
-    gram_out[K:] = jnp.where(lane < 64, total[:K], total[K:])
+    second = jnp.where(lane < 64, total[:K], total[K:])
+    is_first = core[0] == 0
+    kept_out[...] = jnp.where(is_first, first[...], second)
+    sent_out[...] = jnp.where(is_first, second, first[...])
 
 
 def krylov_kernel(
+    core,
     inside,
-    grams,
+    own,
+    other,
     f0,
     f1,
     b,
@@ -269,15 +273,16 @@
             f_next[x] = next_f(x)
             b_next[x] = next_b(x)
 
-    gram = over_copies(grams)
-    first = gram[:K]
+    is_first = core[0] == 0
+    first = jnp.where(is_first, own[...], other[...])
+    second = jnp.where(is_first, other[...], own[...])
     lane = iota((K, 128), 1)
     row = iota((K, 128), 0)
     place = lane & 63
     unit = jnp.where(place == row + K, 1.0, 0.0)
     inverse_t = transposed(eliminate(jnp.where(place < K, first, unit), K, meanwhile))
     first_t = transposed(first)
-    second_t = transposed(gram[K:])
+    second_t = transposed(second)
     coeffs = []
     thetas = []
     for g in range(2):
@@ -574,14 +579,20 @@
         out[i] = total
 
 
-def everyone(values, beside_it=()):
+def sum_kernel(parts, out):
+    out[...] = over_copies(parts)
+
+
+def swapped(values):
+    return lax.ppermute(values, CORES, [(0, 1), (1, 0)])
+
+
+def everyone(kept, other):
     far, near = STAGES
-    other = lax.ppermute(values, CORES, [(0, 1), (1, 0)])
-    other, beside_it = lax.optimization_barrier((other, beside_it))
-    (spread,) = call(add_kernel, [(lax.axis_size(far), *values.shape)], 0, values, other)
+    (spread,) = call(add_kernel, [(lax.axis_size(far), *kept.shape)], 0, kept, other)
     parts = lax.all_to_all(spread, far, 0, 0, tiled=True)
-    (spread,) = call(respread_kernel, [(lax.axis_size(near), *values.shape)], 0, parts)
-    return lax.all_to_all(spread, near, 0, 0, tiled=True), beside_it
+    (spread,) = call(respread_kernel, [(lax.axis_size(near), *kept.shape)], 0, parts)
+    return lax.all_to_all(spread, near, 0, 0, tiled=True)
 
 
 def beside(values):
@@ -627,14 +638,21 @@
         next_kernel, [(NX, 2 * K, NY)], 1, inside, f0, *f0_sides, f1, *f1_sides, med, first
     )
     field_sides = beside(fields)
-    (gram,) = call(second_gram_kernel, [(2 * K, 128)], 0, f0, f1, fields, b1, first)
-    grams, b1_sides = everyone(gram, b1_sides)
+    core = lax.axis_index(CORES).reshape(1)
+    kept, sent = call(
+        second_gram_kernel, [(K, 128)] * 2, 1, core, f0, f1, fields, b1, first
+    )
+    grams = everyone(kept, swapped(sent))
+    grams, field_sides, b1_sides = lax.optimization_barrier((grams, field_sides, b1_sides))
+    (half,) = call(sum_kernel, [(K, 128)], 0, grams)
     q, last, coef, shift = call(
         krylov_kernel,
         [(NX, 96, NY), (NX, 2 * B, NY), (2, 96, 128), (16, 128)],
-        1,
+        2,
+        core,
         inside,
-        grams,
+        half,
+        swapped(half),
         f0,
         f1,
         b,
@@ -659,7 +677,7 @@
         shift,
     )
     solution, residue = finish(
-        scalars, (everyone(gram)[0], coef, shift, f0, f1, t), (front, back, q), (2 * B, NX, NY)
+        scalars, (everyone(gram, swapped(gram)), coef, shift, f0, f1, t), (front, back, q), (2 * B, NX, NY)
     )
     return solution.reshape(right_sides.shape), residue.reshape(right_sides.shape)
 

time: 145 us -> 157 us (1.083)
  starting transfers between devices: 21.7 us -> 37.1 us
  blocking collectives: 63.1 us -> 48.1 us
  waiting for transfers between devices: 36.1 us -> 41.4 us
  local copies, waits for them, and re-layouts: 1.98 us -> 6.34 us
  Pallas kernels: 20.5 us -> 22.9 us
    all_to_all x2 -> x1, blocking collectives: 35.1 us -> 14 us  [everyone(): return lax.all_to_all(spread, near, 0, 0, tiled=True)]
    all_to_all x0 -> x1, starting transfers between devices: none -> 15.2 us  [everyone(): return lax.all_to_all(spread, near, 0, 0, tiled=True)]
    all_to_all x0 -> x1, waiting for transfers between devices: none -> 7.52 us  [everyone(): return lax.all_to_all(spread, near, 0, 0, tiled=True)]
    all_to_all x2, blocking collectives: 28 us -> 34.1 us  [everyone(): parts = lax.all_to_all(spread, far, 0, 0, tiled=True)]
    ppermute x7, waiting for transfers between devices: 34.9 us -> 30.5 us  [beside(): across = lax.ppermute(values, GRID, edges + [(j, i) for i, j in edges])]
    unnamed x11 -> x23, local copies, waits for them, and re-layouts: 1.9 us -> 6.26 us
    pallas_call x12 -> x13, Pallas kernels: 13.6 us -> 16 us  [call(): pl.pallas_call(kernel, out_shape=[pltpu.VMEM(s, F32) for s in shapes], in...]
    ppermute x2 -> x3, waiting for transfers between devices: 1.17 us -> 3.41 us  [swapped(): return lax.ppermute(values, CORES, [(0, 1), (1, 0)])]
  transfers between devices with their start and end apart: 16 -> 18, of which waited for: 6 -> 8; matrix products, arithmetic and copies ran while one was open for 0% -> 1% of each run, Pallas kernels for 6% -> 5%
where the time goes in v8:
time: 157 us
  blocking collectives  48.1 us (31%)
  waiting for transfers between devices  41.4 us (26%)
  starting transfers between devices  37.1 us (24%)
  Pallas kernels  22.9 us (15%)
  local copies, waits for them, and re-layouts  6.34 us (4%)
    all_to_all x2, blocking collectives, everyone(): parts = lax.all_to_all(spread, far, 0, 0, tiled=True)  34.1 us
    ppermute x7, waiting for transfers between devices, beside(): across = lax.ppermute(values, GRID, edges + [(j, i) for i, j in edges])  30.5 us
    ppermute x7, starting transfers between devices, beside(): across = lax.ppermute(values, GRID, edges + [(j, i) for i, j in edges])  20.2 us
    pallas_call x13, Pallas kernels, call(): pl.pallas_call(kernel, out_shape=[pltpu.VMEM(s, F32) for s in shapes], in...  16 us
    all_to_all x1, starting transfers between devices, everyone(): return lax.all_to_all(spread, near, 0, 0, tiled=True)  15.2 us
    all_to_all x1, blocking collectives, everyone(): return lax.all_to_all(spread, near, 0, 0, tiled=True)  14 us
    all_to_all x1, waiting for transfers between devices, everyone(): return lax.all_to_all(spread, near, 0, 0, tiled=True)  7.52 us
    pallas_call x1, Pallas kernels, finish(): pl.pallas_call(finish_kernel, out_shape=[jax.ShapeDtypeStruct(shape, F32)...  6.85 us
  transfers between devices with their start and end apart: 18, of which 8 were waited for; matrix products, arithmetic and copies ran while one was open for 1% of the time, Pallas kernels for 5%

profile of v8, /device:TPU:8, one launch (start us, length us, event | category | flops | bytes accessed | tf_op | source)
XLA Modules:
  0.0 157.0 jit_solution(18413033053659221426)
XLA Ops:
  0.6 0.0 copy-start.9
  0.6 1.5 copy.17
  2.1 0.0 copy-done.9
  2.1 0.1 fusion
  2.2 0.2 copy.18
  2.4 0.0 copy-start.6
  2.4 0.0 copy-start.7
  2.4 0.0 copy-start.8
  2.5 0.1 maximum_bitcast_fusion.ub.u1_far
  2.6 0.1 collective-permute-start.2
  2.7 5.8 %collective-permute-start.1 = (f32[48,56,128]{2,1,0:T(8,128)S(1)}, f32[48,56,128]{2,1,0:T(8,128)}, u32[]{:S(2)}, u32[]{:S(2)}) collective-permute-start(f32[48,56,128]{2,1,0:T(8,128)S(1)} %maximum_bitcast_fusion.ub.u1_far), channel_id=1, source_target_pairs={{1,2},{3,4},{5,6},{7,8},{9,10},{11,12},{13,14},{15,16},{17,18},{19... | collective-permute-start | bytes 4128776 | tf_op jit(solution)/shard_map/ppermute | solution.py:601
  8.5 1.0 copy.19
  9.5 0.0 collective-permute-start
  9.5 0.0 collective-permute-done.2.sibling
  9.5 1.1 copy-done.4
  10.6 14.0 %collective-permute-done.1.across = f32[48,56,128]{2,1,0:T(8,128)} collective-permute-done((f32[48,56,128]{2,1,0:T(8,128)S(1)}, f32[48,56,128]{2,1,0:T(8,128)}, u32[]{:S(2)}, u32[]{:S(2)}) %collective-permute-start.1) | collective-permute-done | bytes 1376288 | tf_op jit(solution)/shard_map/ppermute | solution.py:601
  24.6 0.0 copy-done.6
  24.6 1.3 copy-done.5
  26.0 2.2 %back_kernel.1 = (f32[48,24,128]{2,1,0:T(8,128)S(1)}, f32[48,32,128]{2,1,0:T(8,128)S(1)}, f32[48,32,128]{2,1,0:T(8,128)S(1)}) custom-call(f32[8]{0:T(128)S(1)} %copy-done.7, s32[2]{0:T(128)S(1)} %copy-done.8, f32[1]{0:T(128)} %bitcast.inside, f32[48,56,128]{2,1,0:T(8,128)S(1)} %maximum_bitcast_fusion.ub.u1_far, ...), custom_call_target="tpu_custom_call" | custom-call | tf_op jit(solution)/shard_map/back_kernel/pallas_call | solution.py:544
  28.2 0.0 copy-start.2
  28.2 0.1 collective-permute-start.3
  28.3 0.5 collective-permute-start.4
  28.8 3.9 %collective-permute-start.7 = (f32[48,24,128]{2,1,0:T(8,128)S(1)}, f32[48,24,128]{2,1,0:T(8,128)S(1)}, u32[]{:S(2)}, u32[]{:S(2)}) collective-permute-start(f32[48,24,128]{2,1,0:T(8,128)S(1)} %get-tuple-element.25.f1), channel_id=1, source_target_pairs={{1,2},{3,4},{5,6},{7,8},{9,10},{11,12},{13,14},{15,16},{17,18},{19... | collective-permute-start | bytes 1769480 | tf_op jit(solution)/shard_map/ppermute | solution.py:601
  32.6 0.0 collective-permute-done.across
  32.6 0.0 collective-permute-done.3.f1_sibling
  32.6 0.0 collective-permute-done.4.sibling
  32.6 1.6 %front_kernel.1.f0 = f32[48,24,128]{2,1,0:T(8,128)S(1)} custom-call(f32[8]{0:T(128)S(1)} %copy-done.7, s32[2]{0:T(128)S(1)} %copy-done.8, f32[1]{0:T(128)} %bitcast.inside, f32[48,24,128]{2,1,0:T(8,128)} %bitcast.21.u.u0_far, f32[48,24,128]{2,1,0:T(8,128)} %collective-permute-done.across, f32[48,24,128]{2,1,0:T(8,128)S(1)} %collective-permute-done.4.sibling, ...), custom_call_target="tpu_custom_call" | custom-call | tf_op jit(solution)/shard_map/front_kernel/pallas_call | solution.py:544
  34.3 0.1 collective-permute-start.6
  34.4 2.7 %collective-permute-start.5 = (f32[48,24,128]{2,1,0:T(8,128)S(1)}, f32[48,24,128]{2,1,0:T(8,128)S(1)}, u32[]{:S(2)}, u32[]{:S(2)}) collective-permute-start(f32[48,24,128]{2,1,0:T(8,128)S(1)} %front_kernel.1.f0), channel_id=1, source_target_pairs={{1,2},{3,4},{5,6},{7,8},{9,10},{11,12},{13,14},{15,16},{17,18},{19... | collective-permute-start | bytes 1769480 | tf_op jit(solution)/shard_map/ppermute | solution.py:601
  37.0 1.2 first_gram_kernel.1.first
  38.2 2.0 %collective-permute-done.7.f1_across = f32[48,24,128]{2,1,0:T(8,128)S(1)} collective-permute-done((f32[48,24,128]{2,1,0:T(8,128)S(1)}, f32[48,24,128]{2,1,0:T(8,128)S(1)}, u32[]{:S(2)}, u32[]{:S(2)}) %collective-permute-start.7) | collective-permute-done | bytes 589856 | tf_op jit(solution)/shard_map/ppermute | solution.py:601
  40.2 0.0 collective-permute-done.6.f0_sibling
  40.2 6.3 %collective-permute-done.5.f0_across = f32[48,24,128]{2,1,0:T(8,128)S(1)} collective-permute-done((f32[48,24,128]{2,1,0:T(8,128)S(1)}, f32[48,24,128]{2,1,0:T(8,128)S(1)}, u32[]{:S(2)}, u32[]{:S(2)}) %collective-permute-start.5) | collective-permute-done | bytes 589856 | tf_op jit(solution)/shard_map/ppermute | solution.py:601
  46.5 0.7 next_kernel.1.fields
  47.2 0.1 collective-permute-start.10
  47.3 3.9 %collective-permute-start.9 = (f32[48,48,128]{2,1,0:T(8,128)S(1)}, f32[48,48,128]{2,1,0:T(8,128)}, u32[]{:S(2)}, u32[]{:S(2)}) collective-permute-start(f32[48,48,128]{2,1,0:T(8,128)S(1)} %next_kernel.1.fields), channel_id=1, source_target_pairs={{1,2},{3,4},{5,6},{7,8},{9,10},{11,12},{13,14},{15,16},{17,18},{19... | collective-permute-start | bytes 3538952 | tf_op jit(solution)/shard_map/ppermute | solution.py:601
  51.3 0.0 collective-permute-start.12
  51.3 0.4 collective-permute-start.11
  51.7 1.1 second_gram_kernel.1
  52.8 0.2 collective-permute-start.8
  53.0 1.1 collective-permute-done.8.two
  54.1 21.5 %all_to_all.20.parts = f32[8,24,128]{2,1,0:T(8,128)S(1)} all-to-all(f32[8,24,128]{2,1,0:T(8,128)S(1)} %add_kernel.2), channel_id=1, replica_groups=mesh['grid_0'=4,'grid_1'=4,'grid_2'=8,'grid_3'=2] {'grid_2'}, dimensions={0} | all-to-all | bytes 196608 | tf_op jit(solution)/shard_map/all_to_all | solution.py:593
  75.5 0.7 respread_kernel.2
  76.2 15.2 %all-to-all-start.1 = ((f32[16,24,128]{2,1,0:T(8,128)}), f32[16,24,128]{2,1,0:T(8,128)S(1)}, u32[]{:S(2)}, u32[]{:S(2)}) async-start(f32[16,24,128]{2,1,0:T(8,128)} %respread_kernel.2), calls=%async_computation.1 | async-start | bytes 393216 | tf_op jit(solution)/shard_map/all_to_all | solution.py:595
  91.4 0.0 collective-permute-done.12.b1_sibling
  91.4 0.0 collective-permute-done.11.b1_across
  91.4 7.5 %all-to-all-done.1.parts = f32[16,24,128]{2,1,0:T(8,128)S(1)} async-done(((f32[16,24,128]{2,1,0:T(8,128)}), f32[16,24,128]{2,1,0:T(8,128)S(1)}, u32[]{:S(2)}, u32[]{:S(2)}) %all-to-all-start.1) | async-done | bytes 196640 | tf_op jit(solution)/shard_map/all_to_all | solution.py:595
  98.9 0.0 collective-permute-done.10.fields_sibling
  98.9 0.0 collective-permute-done.9.fields_across
  99.0 0.3 collective-permute-start.13
  99.2 1.2 collective-permute-done.13.other
  100.4 1.1 copy-done.3
  101.5 5.6 %krylov_kernel.1 = (f32[48,96,128]{2,1,0:T(8,128)S(1)}, f32[48,32,128]{2,1,0:T(8,128)S(1)}, f32[2,96,128]{2,1,0:T(8,128)S(1)}, f32[16,128]{1,0:T(8,128)S(1)}) custom-call(s32[1]{0:T(128)} %bitcast.1.core, f32[1]{0:T(128)} %bitcast.inside, f32[24,128]{1,0:T(8,128)S(1)} %sum_kernel.1.own, f32[24,128]{1,0:T(8,128)S(1)} %collective-permute-done.13.other, ...), custom_call_target="tpu_custom_call" | custom-call | tf_op jit(solution)/shard_map/krylov_kernel/pallas_call | solution.py:544
  107.2 0.3 collective-permute-start.15
  107.4 3.5 %collective-permute-start.14 = (f32[48,32,128]{2,1,0:T(8,128)S(1)}, f32[48,32,128]{2,1,0:T(8,128)S(1)}, u32[]{:S(2)}, u32[]{:S(2)}) collective-permute-start(f32[48,32,128]{2,1,0:T(8,128)S(1)} %get-tuple-element.36.last), channel_id=1, source_target_pairs={{1,2},{3,4},{5,6},{7,8},{9,10},{11,12},{13,14},{15,16},{17,18},{19... | collective-permute-start | bytes 2359304 | tf_op jit(solution)/shard_map/ppermute | solution.py:601
  111.0 1.8 %basis_gram_kernel.1.basis_gram = f32[2,48,128]{2,1,0:T(8,128)S(1)} custom-call(f32[48,96,128]{2,1,0:T(8,128)S(1)} %get-tuple-element.37.q.q_far, f32[48,48,128]{2,1,0:T(8,128)S(1)} %next_kernel.1.fields), custom_call_target="tpu_custom_call" | custom-call | tf_op jit(solution)/shard_map/basis_gram_kernel/pallas_call | solution.py:544
  112.8 0.0 collective-permute-done.15.last_sibling
  112.8 8.1 %collective-permute-done.14.last_across = f32[48,32,128]{2,1,0:T(8,128)S(1)} collective-permute-done((f32[48,32,128]{2,1,0:T(8,128)S(1)}, f32[48,32,128]{2,1,0:T(8,128)S(1)}, u32[]{:S(2)}, u32[]{:S(2)}) %collective-permute-start.14) | collective-permute-done | bytes 786464 | tf_op jit(solution)/shard_map/ppermute | solution.py:601
  120.9 1.1 moment_kernel.1
  122.0 0.1 collective-permute-start.16
  122.1 1.2 collective-permute-done.16.two
  123.3 12.7 %all_to_all.21.parts = f32[8,24,128]{2,1,0:T(8,128)S(1)} all-to-all(f32[8,24,128]{2,1,0:T(8,128)S(1)} %add_kernel.3), channel_id=1, replica_groups=mesh['grid_0'=4,'grid_1'=4,'grid_2'=8,'grid_3'=2] {'grid_2'}, dimensions={0} | all-to-all | bytes 196608 | tf_op jit(solution)/shard_map/all_to_all | solution.py:593
  136.0 14.0 %all_to_all.22.moments = f32[16,24,128]{2,1,0:T(8,128)S(1)} all-to-all(f32[16,24,128]{2,1,0:T(8,128)S(1)} %respread_kernel.3), channel_id=1, replica_groups=mesh['grid_0'=4,'grid_1'=4,'grid_2'=8,'grid_3'=2] {'grid_0','grid_1'}, dimensions={0} | all-to-all | bytes 393216 | tf_op jit(solution)/shard_map/all_to_all | solution.py:595
  150.0 6.8 %finish_kernel.1 = (f32[32,48,128]{2,1,0:T(8,128)}, f32[32,48,128]{2,1,0:T(8,128)}) custom-call(f32[8]{0:T(128)S(1)} %copy-done.7, s32[2]{0:T(128)S(1)} %copy-done.8, f32[16,24,128]{2,1,0:T(8,128)S(1)} %all_to_all.22.moments, f32[2,96,128]{2,1,0:T(8,128)S(1)} %get-tuple-element.40.coef, f32[16,128]{1,0:T(8,128)S(1)} %get-tuple-element.38.shift, ...), custom_call_target="tpu_custom_call" | custom-call | tf_op jit(solution)/shard_map/finish_kernel/pallas_call | solution.py:557
  (14 shorter events, 0.1 us)
Async XLA Ops:
  0.6 1.5 copy-start.9
  2.4 22.2 %copy-start.6 = (f32[1,48,128]{2,1,0:T(8,128)S(1)}, f32[1,48,128]{2,1,0:T(8,128)}, u32[]{:S(2)}) copy-start(f32[1,48,128]{2,1,0:T(8,128)} %param.7) | copy-start | bytes 73732
  2.4 22.2 %copy-start.7 = (f32[8]{0:T(128)S(1)}, f32[8]{0:T(128)}, u32[]{:S(2)}) copy-start(f32[8]{0:T(128)} %table.5) | copy-start | bytes 100
  2.4 22.2 %copy-start.8 = (s32[2]{0:T(128)S(1)}, s32[2]{0:T(128)}, u32[]{:S(2)}) copy-start(s32[2]{0:T(128)} %index.5) | copy-start | bytes 28
  2.6 25.6 %copy-start = (f32[48,56,128]{2,1,0:T(8,128)}, f32[48,56,128]{2,1,0:T(8,128)S(1)}, u32[]{:S(2)}) copy-start(f32[48,56,128]{2,1,0:T(8,128)S(1)} %maximum_bitcast_fusion.ub.u1_far) | copy-start | bytes 4128772
  2.6 6.9 %collective-permute-start.2 = (f32[48,56,128]{2,1,0:T(8,128)S(1)}, f32[48,56,128]{2,1,0:T(8,128)S(1)}, u32[]{:S(2)}, u32[]{:S(2)}) collective-permute-start(f32[48,56,128]{2,1,0:T(8,128)S(1)} %maximum_bitcast_fusion.ub.u1_far), channel_id=1, source_target_pairs={{0,1},{1,0},{2,3},{3,2},{4,5},{5,4},{6,7},{7,6},{8,9},{9,8},{10,11... | collective-permute-start | bytes 4128776 | tf_op jit(solution)/shard_map/ppermute | solution.py:602
  2.7 21.9 %collective-permute-start.1 = (f32[48,56,128]{2,1,0:T(8,128)S(1)}, f32[48,56,128]{2,1,0:T(8,128)}, u32[]{:S(2)}, u32[]{:S(2)}) collective-permute-start(f32[48,56,128]{2,1,0:T(8,128)S(1)} %maximum_bitcast_fusion.ub.u1_far), channel_id=1, source_target_pairs={{1,2},{3,4},{5,6},{7,8},{9,10},{11,12},{13,14},{15,16},{17,18},{19... | collective-permute-start | bytes 4128776 | tf_op jit(solution)/shard_map/ppermute | solution.py:601
  9.5 23.1 %collective-permute-start = (f32[48,24,128]{2,1,0:T(8,128)}, f32[48,24,128]{2,1,0:T(8,128)}, u32[]{:S(2)}, u32[]{:S(2)}) collective-permute-start(f32[48,24,128]{2,1,0:T(8,128)} %bitcast.21.u.u0_far), channel_id=1, source_target_pairs={{1,2},{3,4},{5,6},{7,8},{9,10},{11,12},{13,14},{15,16},{17,18},{19... | collective-permute-start | bytes 1769480 | tf_op jit(solution)/shard_map/ppermute | solution.py:601
  9.5 1.1 copy-start.4
  24.6 1.3 copy-start.5
  28.2 10.0 %copy-start.2 = (f32[48,32,128]{2,1,0:T(8,128)}, f32[48,32,128]{2,1,0:T(8,128)S(1)}, u32[]{:S(2)}) copy-start(f32[48,32,128]{2,1,0:T(8,128)S(1)} %get-tuple-element.27.b) | copy-start | bytes 2359300
  28.2 4.5 %collective-permute-start.3 = (f32[48,24,128]{2,1,0:T(8,128)S(1)}, f32[48,24,128]{2,1,0:T(8,128)S(1)}, u32[]{:S(2)}, u32[]{:S(2)}) collective-permute-start(f32[48,24,128]{2,1,0:T(8,128)S(1)} %get-tuple-element.25.f1), channel_id=1, source_target_pairs={{0,1},{1,0},{2,3},{3,2},{4,5},{5,4},{6,7},{7,6},{8,9},{9,8},{10,11... | collective-permute-start | bytes 1769480 | tf_op jit(solution)/shard_map/ppermute | solution.py:602
  28.3 4.4 %collective-permute-start.4 = (f32[48,24,128]{2,1,0:T(8,128)}, f32[48,24,128]{2,1,0:T(8,128)S(1)}, u32[]{:S(2)}, u32[]{:S(2)}) collective-permute-start(f32[48,24,128]{2,1,0:T(8,128)} %bitcast.21.u.u0_far), channel_id=1, source_target_pairs={{0,1},{1,0},{2,3},{3,2},{4,5},{5,4},{6,7},{7,6},{8,9},{9,8},{10,11... | collective-permute-start | bytes 1769480 | tf_op jit(solution)/shard_map/ppermute | solution.py:602
  28.8 11.4 %collective-permute-start.7 = (f32[48,24,128]{2,1,0:T(8,128)S(1)}, f32[48,24,128]{2,1,0:T(8,128)S(1)}, u32[]{:S(2)}, u32[]{:S(2)}) collective-permute-start(f32[48,24,128]{2,1,0:T(8,128)S(1)} %get-tuple-element.25.f1), channel_id=1, source_target_pairs={{1,2},{3,4},{5,6},{7,8},{9,10},{11,12},{13,14},{15,16},{17,18},{19... | collective-permute-start | bytes 1769480 | tf_op jit(solution)/shard_map/ppermute | solution.py:601
  34.3 5.9 %collective-permute-start.6 = (f32[48,24,128]{2,1,0:T(8,128)S(1)}, f32[48,24,128]{2,1,0:T(8,128)S(1)}, u32[]{:S(2)}, u32[]{:S(2)}) collective-permute-start(f32[48,24,128]{2,1,0:T(8,128)S(1)} %front_kernel.1.f0), channel_id=1, source_target_pairs={{0,1},{1,0},{2,3},{3,2},{4,5},{5,4},{6,7},{7,6},{8,9},{9,8},{10,11... | collective-permute-start | bytes 1769480 | tf_op jit(solution)/shard_map/ppermute | solution.py:602
  34.4 12.1 %collective-permute-start.5 = (f32[48,24,128]{2,1,0:T(8,128)S(1)}, f32[48,24,128]{2,1,0:T(8,128)S(1)}, u32[]{:S(2)}, u32[]{:S(2)}) collective-permute-start(f32[48,24,128]{2,1,0:T(8,128)S(1)} %front_kernel.1.f0), channel_id=1, source_target_pairs={{1,2},{3,4},{5,6},{7,8},{9,10},{11,12},{13,14},{15,16},{17,18},{19... | collective-permute-start | bytes 1769480 | tf_op jit(solution)/shard_map/ppermute | solution.py:601
  47.2 51.7 %collective-permute-start.10 = (f32[48,48,128]{2,1,0:T(8,128)S(1)}, f32[48,48,128]{2,1,0:T(8,128)}, u32[]{:S(2)}, u32[]{:S(2)}) collective-permute-start(f32[48,48,128]{2,1,0:T(8,128)S(1)} %next_kernel.1.fields), channel_id=1, source_target_pairs={{0,1},{1,0},{2,3},{3,2},{4,5},{5,4},{6,7},{7,6},{8,9},{9,8},{10,11... | collective-permute-start | bytes 3538952 | tf_op jit(solution)/shard_map/ppermute | solution.py:602
  47.3 51.6 %collective-permute-start.9 = (f32[48,48,128]{2,1,0:T(8,128)S(1)}, f32[48,48,128]{2,1,0:T(8,128)}, u32[]{:S(2)}, u32[]{:S(2)}) collective-permute-start(f32[48,48,128]{2,1,0:T(8,128)S(1)} %next_kernel.1.fields), channel_id=1, source_target_pairs={{1,2},{3,4},{5,6},{7,8},{9,10},{11,12},{13,14},{15,16},{17,18},{19... | collective-permute-start | bytes 3538952 | tf_op jit(solution)/shard_map/ppermute | solution.py:601
  51.3 40.1 %collective-permute-start.12 = (f32[48,32,128]{2,1,0:T(8,128)S(1)}, f32[48,32,128]{2,1,0:T(8,128)}, u32[]{:S(2)}, u32[]{:S(2)}) collective-permute-start(f32[48,32,128]{2,1,0:T(8,128)S(1)} %get-tuple-element.28.b1), channel_id=1, source_target_pairs={{0,1},{1,0},{2,3},{3,2},{4,5},{5,4},{6,7},{7,6},{8,9},{9,8},{10,11... | collective-permute-start | bytes 2359304 | tf_op jit(solution)/shard_map/ppermute | solution.py:602
  51.3 40.1 %collective-permute-start.11 = (f32[48,32,128]{2,1,0:T(8,128)S(1)}, f32[48,32,128]{2,1,0:T(8,128)}, u32[]{:S(2)}, u32[]{:S(2)}) collective-permute-start(f32[48,32,128]{2,1,0:T(8,128)S(1)} %get-tuple-element.28.b1), channel_id=1, source_target_pairs={{1,2},{3,4},{5,6},{7,8},{9,10},{11,12},{13,14},{15,16},{17,18},{19... | collective-permute-start | bytes 2359304 | tf_op jit(solution)/shard_map/ppermute | solution.py:601
  52.8 1.3 collective-permute-start.8
  76.2 22.7 %all-to-all-start.1 = ((f32[16,24,128]{2,1,0:T(8,128)}), f32[16,24,128]{2,1,0:T(8,128)S(1)}, u32[]{:S(2)}, u32[]{:S(2)}) async-start(f32[16,24,128]{2,1,0:T(8,128)} %respread_kernel.2), calls=%async_computation.1 | async-start | bytes 393216 | tf_op jit(solution)/shard_map/all_to_all | solution.py:595
  99.0 1.4 collective-permute-start.13
  100.4 1.1 copy-start.3
  107.2 5.6 %collective-permute-start.15 = (f32[48,32,128]{2,1,0:T(8,128)S(1)}, f32[48,32,128]{2,1,0:T(8,128)S(1)}, u32[]{:S(2)}, u32[]{:S(2)}) collective-permute-start(f32[48,32,128]{2,1,0:T(8,128)S(1)} %get-tuple-element.36.last), channel_id=1, source_target_pairs={{0,1},{1,0},{2,3},{3,2},{4,5},{5,4},{6,7},{7,6},{8,9},{9,8},{10,11... | collective-permute-start | bytes 2359304 | tf_op jit(solution)/shard_map/ppermute | solution.py:602
  107.4 13.5 %collective-permute-start.14 = (f32[48,32,128]{2,1,0:T(8,128)S(1)}, f32[48,32,128]{2,1,0:T(8,128)S(1)}, u32[]{:S(2)}, u32[]{:S(2)}) collective-permute-start(f32[48,32,128]{2,1,0:T(8,128)S(1)} %get-tuple-element.36.last), channel_id=1, source_target_pairs={{1,2},{3,4},{5,6},{7,8},{9,10},{11,12},{13,14},{15,16},{17,18},{19... | collective-permute-start | bytes 2359304 | tf_op jit(solution)/shard_map/ppermute | solution.py:601
  120.9 29.0 %copy-start.1 = (f32[48,56,128]{2,1,0:T(8,128)S(1)}, f32[48,56,128]{2,1,0:T(8,128)}, u32[]{:S(2)}) copy-start(f32[48,56,128]{2,1,0:T(8,128)} %copy-done) | copy-start | bytes 4128772
  122.0 1.3 collective-permute-start.16

commit v9 on v7

--- a/solution.py
+++ b/solution.py
@@ -20,7 +20,7 @@
 VMEM = pl.BlockSpec(memory_space=pltpu.VMEM)
 SMEM = pl.BlockSpec(memory_space=pltpu.SMEM)
 ANY = pl.BlockSpec(memory_space=pl.ANY)
-CHUNK = 8
+CHUNK = 16
 
 
 def iota(shape, dim):
@@ -489,7 +489,7 @@
         y1, y2, y3 = (ys[:, 16 * i : 16 * i + 16] for i in range(3))
         z0, z1, z2 = (coef[g, 24 * i : 24 * i + B, :K] for i in range(3))
         on_f = small(y3, thirds[g])
-        on_u = z0 - small(y1, z1) - small(y2, z2) - on_f
+        on_u = z0 - small(ys[:, :48], jnp.concatenate([z1, z2, thirds[g]], axis=0))
         none = jnp.zeros((B, K), F32)
         rows = jnp.concatenate(
             [

time: 145 us -> 145 us (level)
  no operation moved by 1% of the time
where the time goes in v9:
time: 145 us; the launch traced here: 144 us
  blocking collectives  63.1 us (44%)
  waiting for transfers between devices  36.1 us (25%)
  starting transfers between devices  21.7 us (15%)
  Pallas kernels  20.3 us (14%)
  local copies, waits for them, and re-layouts  1.98 us (1%)
    all_to_all x2, blocking collectives, everyone(): return (lax.all_to_all(spread, near, 0, 0, tiled=True), beside_it)  35.1 us
    ppermute x7, waiting for transfers between devices, beside(): across = lax.ppermute(values, GRID, edges + [(j, i) for i, j in edges])  34.9 us
    all_to_all x2, blocking collectives, everyone(): parts = lax.all_to_all(spread, far, 0, 0, tiled=True)  28 us
    ppermute x7, starting transfers between devices, beside(): across = lax.ppermute(values, GRID, edges + [(j, i) for i, j in edges])  19.8 us
    pallas_call x12, Pallas kernels, call(): pl.pallas_call(kernel, out_shape=[pltpu.VMEM(s, F32) for s in shapes], in...  13.6 us
    pallas_call x1, Pallas kernels, finish(): pl.pallas_call(finish_kernel, out_shape=[jax.ShapeDtypeStruct(shape, F32)...  6.71 us
  transfers between devices with their start and end apart: 16, of which 6 were waited for; matrix products, arithmetic and copies ran while one was open for 0% of the time, Pallas kernels for 6%

profile of v9, /device:TPU:8, one launch (start us, length us, event | category | flops | bytes accessed | tf_op | source)
XLA Modules:
  0.0 144.3 jit_solution(16857211354830480821)
XLA Ops:
  0.6 0.0 copy-start.3
  0.6 1.5 %copy.17 = f32[32,1,48,128]{3,0,2,1:T(8,128)S(1)} copy(f32[32,1,48,128]{3,2,1,0:T(8,128)} %param.5) | data formatting | bytes 1572864 | tf_op args[0]
  2.1 0.0 copy-done.3
  2.1 0.1 fusion
  2.2 0.2 copy.18
  2.4 0.0 copy-start
  2.4 0.0 copy-start.1
  2.4 0.0 copy-start.2
  2.5 0.1 maximum_bitcast_fusion.ub.u1_far
  2.6 0.1 collective-permute-start.2
  2.7 5.8 %collective-permute-start.1 = (f32[48,56,128]{2,1,0:T(8,128)S(1)}, f32[48,56,128]{2,1,0:T(8,128)}, u32[]{:S(2)}, u32[]{:S(2)}) collective-permute-start(f32[48,56,128]{2,1,0:T(8,128)S(1)} %maximum_bitcast_fusion.ub.u1_far), channel_id=1, source_target_pairs={{1,2},{3,4},{5,6},{7,8},{9,10},{11,12},{13,14},{15,16},{17,18},{19... | collective-permute-start | bytes 4128776 | tf_op jit(solution)/shard_map/ppermute | solution.py:590
  8.5 0.2 copy.19
  8.7 0.1 collective-permute-start
  8.8 0.0 collective-permute-done.2.sibling
  8.8 15.8 %collective-permute-done.1.across = f32[48,56,128]{2,1,0:T(8,128)} collective-permute-done((f32[48,56,128]{2,1,0:T(8,128)S(1)}, f32[48,56,128]{2,1,0:T(8,128)}, u32[]{:S(2)}, u32[]{:S(2)}) %collective-permute-start.1) | collective-permute-done | bytes 1376288 | tf_op jit(solution)/shard_map/ppermute | solution.py:590
  24.6 0.0 copy-done
  24.6 0.0 copy-done.1
  24.6 0.0 copy-done.2
  24.6 2.1 %back_kernel.1 = (f32[48,24,128]{2,1,0:T(8,128)S(1)}, f32[48,32,128]{2,1,0:T(8,128)S(1)}, f32[48,32,128]{2,1,0:T(8,128)S(1)}) custom-call(f32[8]{0:T(128)S(1)} %copy-done.1, s32[2]{0:T(128)S(1)} %copy-done.2, f32[1]{0:T(128)} %bitcast.inside, f32[48,56,128]{2,1,0:T(8,128)S(1)} %maximum_bitcast_fusion.ub.u1_far, ...), custom_call_target="tpu_custom_call" | custom-call | tf_op jit(solution)/shard_map/back_kernel/pallas_call | solution.py:539
  26.8 0.1 collective-permute-start.3
  26.9 0.5 collective-permute-start.4
  27.4 3.9 %collective-permute-start.7 = (f32[48,24,128]{2,1,0:T(8,128)S(1)}, f32[48,24,128]{2,1,0:T(8,128)S(1)}, u32[]{:S(2)}, u32[]{:S(2)}) collective-permute-start(f32[48,24,128]{2,1,0:T(8,128)S(1)} %get-tuple-element.21.f1), channel_id=1, source_target_pairs={{1,2},{3,4},{5,6},{7,8},{9,10},{11,12},{13,14},{15,16},{17,18},{19... | collective-permute-start | bytes 1769480 | tf_op jit(solution)/shard_map/ppermute | solution.py:590
  31.2 0.0 collective-permute-done.across
  31.2 0.0 collective-permute-done.3.f1_sibling
  31.2 0.0 collective-permute-done.4.sibling
  31.2 1.5 %front_kernel.1.f0 = f32[48,24,128]{2,1,0:T(8,128)S(1)} custom-call(f32[8]{0:T(128)S(1)} %copy-done.1, s32[2]{0:T(128)S(1)} %copy-done.2, f32[1]{0:T(128)} %bitcast.inside, f32[48,24,128]{2,1,0:T(8,128)S(1)} %bitcast.23, f32[48,24,128]{2,1,0:T(8,128)} %collective-permute-done.across, f32[48,24,128]{2,1,0:T(8,128)S(1)} %collective-permute-done.4.sibling, ...), custom_call_target="tpu_custom_call" | custom-call | tf_op jit(solution)/shard_map/front_kernel/pallas_call | solution.py:539
  32.7 0.1 collective-permute-start.6
  32.8 3.6 %collective-permute-start.5 = (f32[48,24,128]{2,1,0:T(8,128)S(1)}, f32[48,24,128]{2,1,0:T(8,128)S(1)}, u32[]{:S(2)}, u32[]{:S(2)}) collective-permute-start(f32[48,24,128]{2,1,0:T(8,128)S(1)} %front_kernel.1.f0), channel_id=1, source_target_pairs={{1,2},{3,4},{5,6},{7,8},{9,10},{11,12},{13,14},{15,16},{17,18},{19... | collective-permute-start | bytes 1769480 | tf_op jit(solution)/shard_map/ppermute | solution.py:590
  36.4 0.0 collective-permute-start.10
  36.4 0.4 collective-permute-start.9
  36.9 1.2 first_gram_kernel.1.first
  38.0 0.7 collective-permute-done.7.f1_across
  38.8 0.0 collective-permute-done.6.f0_sibling
  38.8 6.3 %collective-permute-done.5.f0_across = f32[48,24,128]{2,1,0:T(8,128)S(1)} collective-permute-done((f32[48,24,128]{2,1,0:T(8,128)S(1)}, f32[48,24,128]{2,1,0:T(8,128)S(1)}, u32[]{:S(2)}, u32[]{:S(2)}) %collective-permute-start.5) | collective-permute-done | bytes 589856 | tf_op jit(solution)/shard_map/ppermute | solution.py:590
  45.1 0.7 next_kernel.1.fields
  45.8 0.1 collective-permute-start.12
  45.9 3.9 %collective-permute-start.11 = (f32[48,48,128]{2,1,0:T(8,128)S(1)}, f32[48,48,128]{2,1,0:T(8,128)S(1)}, u32[]{:S(2)}, u32[]{:S(2)}) collective-permute-start(f32[48,48,128]{2,1,0:T(8,128)S(1)} %next_kernel.1.fields), channel_id=1, source_target_pairs={{1,2},{3,4},{5,6},{7,8},{9,10},{11,12},{13,14},{15,16},{17,18},{19... | collective-permute-start | bytes 3538952 | tf_op jit(solution)/shard_map/ppermute | solution.py:590
  49.9 1.1 second_gram_kernel.1.one
  51.0 0.1 collective-permute-start.8
  51.1 0.0 collective-permute-done.10.b1_sibling
  51.1 2.4 %collective-permute-done.9.b1_across = f32[48,32,128]{2,1,0:T(8,128)S(1)} collective-permute-done((f32[48,32,128]{2,1,0:T(8,128)S(1)}, f32[48,32,128]{2,1,0:T(8,128)S(1)}, u32[]{:S(2)}, u32[]{:S(2)}) %collective-permute-start.9) | collective-permute-done | bytes 786464 | tf_op jit(solution)/shard_map/ppermute | solution.py:590
  53.5 0.0 collective-permute-done.8.two
  53.5 16.7 %all_to_all.20.parts = f32[8,48,128]{2,1,0:T(8,128)S(1)} all-to-all(f32[8,48,128]{2,1,0:T(8,128)S(1)} %add_kernel.2), channel_id=1, replica_groups=mesh['grid_0'=4,'grid_1'=4,'grid_2'=8,'grid_3'=2] {'grid_2'}, dimensions={0} | all-to-all | bytes 393216 | tf_op jit(solution)/shard_map/all_to_all | solution.py:582
  70.2 21.1 %all_to_all.21.grams = f32[16,48,128]{2,1,0:T(8,128)S(1)} all-to-all(f32[16,48,128]{2,1,0:T(8,128)S(1)} %respread_kernel.2), channel_id=1, replica_groups=mesh['grid_0'=4,'grid_1'=4,'grid_2'=8,'grid_3'=2] {'grid_0','grid_1'}, dimensions={0} | all-to-all | bytes 786432 | tf_op jit(solution)/shard_map/all_to_all | solution.py:584
  91.3 0.0 collective-permute-done.12.fields_sibling
  91.3 0.0 collective-permute-done.11.fields_across
  91.4 3.9 %krylov_kernel.1 = (f32[48,96,128]{2,1,0:T(8,128)S(1)}, f32[48,32,128]{2,1,0:T(8,128)S(1)}, f32[2,96,128]{2,1,0:T(8,128)S(1)}, f32[16,128]{1,0:T(8,128)S(1)}) custom-call(f32[1]{0:T(128)} %bitcast.inside, f32[16,48,128]{2,1,0:T(8,128)S(1)} %all_to_all.21.grams, f32[48,24,128]{2,1,0:T(8,128)S(1)} %front_kernel.1.f0, f32[48,24,128]{2,1,0:T(8,128)S(1)} %get-tuple-element.21.f1, ...), custom_call_target="tpu_custom_call" | custom-call | tf_op jit(solution)/shard_map/krylov_kernel/pallas_call | solution.py:539
  95.3 0.8 collective-permute-start.14
  96.1 2.0 %collective-permute-start.13 = (f32[48,32,128]{2,1,0:T(8,128)S(1)}, f32[48,32,128]{2,1,0:T(8,128)S(1)}, u32[]{:S(2)}, u32[]{:S(2)}) collective-permute-start(f32[48,32,128]{2,1,0:T(8,128)S(1)} %get-tuple-element.28.last), channel_id=1, source_target_pairs={{1,2},{3,4},{5,6},{7,8},{9,10},{11,12},{13,14},{15,16},{17,18},{19... | collective-permute-start | bytes 2359304 | tf_op jit(solution)/shard_map/ppermute | solution.py:590
  98.2 1.8 %basis_gram_kernel.1.basis_gram = f32[2,48,128]{2,1,0:T(8,128)S(1)} custom-call(f32[48,96,128]{2,1,0:T(8,128)S(1)} %get-tuple-element.29.q.q_far, f32[48,48,128]{2,1,0:T(8,128)S(1)} %next_kernel.1.fields), custom_call_target="tpu_custom_call" | custom-call | tf_op jit(solution)/shard_map/basis_gram_kernel/pallas_call | solution.py:539
  100.0 0.0 collective-permute-done.14.last_sibling
  100.0 9.6 %collective-permute-done.13.last_across = f32[48,32,128]{2,1,0:T(8,128)S(1)} collective-permute-done((f32[48,32,128]{2,1,0:T(8,128)S(1)}, f32[48,32,128]{2,1,0:T(8,128)S(1)}, u32[]{:S(2)}, u32[]{:S(2)}) %collective-permute-start.13) | collective-permute-done | bytes 786464 | tf_op jit(solution)/shard_map/ppermute | solution.py:590
  109.7 1.1 moment_kernel.1
  110.7 0.1 collective-permute-start.15
  110.8 1.2 collective-permute-done.15.two
  112.0 11.4 %all_to_all.22.parts = f32[8,24,128]{2,1,0:T(8,128)S(1)} all-to-all(f32[8,24,128]{2,1,0:T(8,128)S(1)} %add_kernel.3), channel_id=1, replica_groups=mesh['grid_0'=4,'grid_1'=4,'grid_2'=8,'grid_3'=2] {'grid_2'}, dimensions={0} | all-to-all | bytes 196608 | tf_op jit(solution)/shard_map/all_to_all | solution.py:582
  123.4 14.0 %all_to_all.23.moments = f32[16,24,128]{2,1,0:T(8,128)S(1)} all-to-all(f32[16,24,128]{2,1,0:T(8,128)S(1)} %respread_kernel.3), channel_id=1, replica_groups=mesh['grid_0'=4,'grid_1'=4,'grid_2'=8,'grid_3'=2] {'grid_0','grid_1'}, dimensions={0} | all-to-all | bytes 393216 | tf_op jit(solution)/shard_map/all_to_all | solution.py:584
  137.4 6.7 %finish_kernel.1 = (f32[32,48,128]{2,1,0:T(8,128)}, f32[32,48,128]{2,1,0:T(8,128)}) custom-call(f32[8]{0:T(128)S(1)} %copy-done.1, s32[2]{0:T(128)S(1)} %copy-done.2, f32[16,24,128]{2,1,0:T(8,128)S(1)} %all_to_all.23.moments, f32[2,96,128]{2,1,0:T(8,128)S(1)} %get-tuple-element.32.coef, f32[16,128]{1,0:T(8,128)S(1)} %get-tuple-element.30.shift, ...), custom_call_target="tpu_custom_call" | custom-call | tf_op jit(solution)/shard_map/finish_kernel/pallas_call | solution.py:552
  (4 shorter events, 0.1 us)
Async XLA Ops:
  0.6 1.5 %copy-start.3 = (f32[2,24,1,48,128]{4,3,2,1,0:T(8,128)S(1)}, f32[2,24,1,48,128]{4,3,2,1,0:T(8,128)}, u32[]{:S(2)}) copy-start(f32[2,24,1,48,128]{4,3,2,1,0:T(8,128)} %param.6) | copy-start | bytes 3538948
  2.4 22.2 %copy-start = (f32[1,48,128]{2,1,0:T(8,128)S(1)}, f32[1,48,128]{2,1,0:T(8,128)}, u32[]{:S(2)}) copy-start(f32[1,48,128]{2,1,0:T(8,128)} %param.7) | copy-start | bytes 73732
  2.4 22.2 %copy-start.1 = (f32[8]{0:T(128)S(1)}, f32[8]{0:T(128)}, u32[]{:S(2)}) copy-start(f32[8]{0:T(128)} %table.5) | copy-start | bytes 100
  2.4 22.2 %copy-start.2 = (s32[2]{0:T(128)S(1)}, s32[2]{0:T(128)}, u32[]{:S(2)}) copy-start(s32[2]{0:T(128)} %index.5) | copy-start | bytes 28
  2.6 6.3 %collective-permute-start.2 = (f32[48,56,128]{2,1,0:T(8,128)S(1)}, f32[48,56,128]{2,1,0:T(8,128)S(1)}, u32[]{:S(2)}, u32[]{:S(2)}) collective-permute-start(f32[48,56,128]{2,1,0:T(8,128)S(1)} %maximum_bitcast_fusion.ub.u1_far), channel_id=1, source_target_pairs={{0,1},{1,0},{2,3},{3,2},{4,5},{5,4},{6,7},{7,6},{8,9},{9,8},{10,11... | collective-permute-start | bytes 4128776 | tf_op jit(solution)/shard_map/ppermute | solution.py:591
  2.7 21.9 %collective-permute-start.1 = (f32[48,56,128]{2,1,0:T(8,128)S(1)}, f32[48,56,128]{2,1,0:T(8,128)}, u32[]{:S(2)}, u32[]{:S(2)}) collective-permute-start(f32[48,56,128]{2,1,0:T(8,128)S(1)} %maximum_bitcast_fusion.ub.u1_far), channel_id=1, source_target_pairs={{1,2},{3,4},{5,6},{7,8},{9,10},{11,12},{13,14},{15,16},{17,18},{19... | collective-permute-start | bytes 4128776 | tf_op jit(solution)/shard_map/ppermute | solution.py:590
  8.7 22.5 %collective-permute-start = (f32[48,24,128]{2,1,0:T(8,128)S(1)}, f32[48,24,128]{2,1,0:T(8,128)}, u32[]{:S(2)}, u32[]{:S(2)}) collective-permute-start(f32[48,24,128]{2,1,0:T(8,128)S(1)} %bitcast.21), channel_id=1, source_target_pairs={{1,2},{3,4},{5,6},{7,8},{9,10},{11,12},{13,14},{15,16},{17,18},{19... | collective-permute-start | bytes 1769480 | tf_op jit(solution)/shard_map/ppermute | solution.py:590
  26.8 4.5 %collective-permute-start.3 = (f32[48,24,128]{2,1,0:T(8,128)S(1)}, f32[48,24,128]{2,1,0:T(8,128)S(1)}, u32[]{:S(2)}, u32[]{:S(2)}) collective-permute-start(f32[48,24,128]{2,1,0:T(8,128)S(1)} %get-tuple-element.21.f1), channel_id=1, source_target_pairs={{0,1},{1,0},{2,3},{3,2},{4,5},{5,4},{6,7},{7,6},{8,9},{9,8},{10,11... | collective-permute-start | bytes 1769480 | tf_op jit(solution)/shard_map/ppermute | solution.py:591
  26.9 4.4 %collective-permute-start.4 = (f32[48,24,128]{2,1,0:T(8,128)S(1)}, f32[48,24,128]{2,1,0:T(8,128)S(1)}, u32[]{:S(2)}, u32[]{:S(2)}) collective-permute-start(f32[48,24,128]{2,1,0:T(8,128)S(1)} %bitcast.22), channel_id=1, source_target_pairs={{0,1},{1,0},{2,3},{3,2},{4,5},{5,4},{6,7},{7,6},{8,9},{9,8},{10,11... | collective-permute-start | bytes 1769480 | tf_op jit(solution)/shard_map/ppermute | solution.py:591
  27.4 11.4 %collective-permute-start.7 = (f32[48,24,128]{2,1,0:T(8,128)S(1)}, f32[48,24,128]{2,1,0:T(8,128)S(1)}, u32[]{:S(2)}, u32[]{:S(2)}) collective-permute-start(f32[48,24,128]{2,1,0:T(8,128)S(1)} %get-tuple-element.21.f1), channel_id=1, source_target_pairs={{1,2},{3,4},{5,6},{7,8},{9,10},{11,12},{13,14},{15,16},{17,18},{19... | collective-permute-start | bytes 1769480 | tf_op jit(solution)/shard_map/ppermute | solution.py:590
  32.7 6.1 %collective-permute-start.6 = (f32[48,24,128]{2,1,0:T(8,128)S(1)}, f32[48,24,128]{2,1,0:T(8,128)S(1)}, u32[]{:S(2)}, u32[]{:S(2)}) collective-permute-start(f32[48,24,128]{2,1,0:T(8,128)S(1)} %front_kernel.1.f0), channel_id=1, source_target_pairs={{0,1},{1,0},{2,3},{3,2},{4,5},{5,4},{6,7},{7,6},{8,9},{9,8},{10,11... | collective-permute-start | bytes 1769480 | tf_op jit(solution)/shard_map/ppermute | solution.py:591
  32.8 12.3 %collective-permute-start.5 = (f32[48,24,128]{2,1,0:T(8,128)S(1)}, f32[48,24,128]{2,1,0:T(8,128)S(1)}, u32[]{:S(2)}, u32[]{:S(2)}) collective-permute-start(f32[48,24,128]{2,1,0:T(8,128)S(1)} %front_kernel.1.f0), channel_id=1, source_target_pairs={{1,2},{3,4},{5,6},{7,8},{9,10},{11,12},{13,14},{15,16},{17,18},{19... | collective-permute-start | bytes 1769480 | tf_op jit(solution)/shard_map/ppermute | solution.py:590
  36.4 14.6 %collective-permute-start.10 = (f32[48,32,128]{2,1,0:T(8,128)S(1)}, f32[48,32,128]{2,1,0:T(8,128)S(1)}, u32[]{:S(2)}, u32[]{:S(2)}) collective-permute-start(f32[48,32,128]{2,1,0:T(8,128)S(1)} %get-tuple-element.24.b1), channel_id=1, source_target_pairs={{0,1},{1,0},{2,3},{3,2},{4,5},{5,4},{6,7},{7,6},{8,9},{9,8},{10,11... | collective-permute-start | bytes 2359304 | tf_op jit(solution)/shard_map/ppermute | solution.py:591
  36.4 17.1 %collective-permute-start.9 = (f32[48,32,128]{2,1,0:T(8,128)S(1)}, f32[48,32,128]{2,1,0:T(8,128)S(1)}, u32[]{:S(2)}, u32[]{:S(2)}) collective-permute-start(f32[48,32,128]{2,1,0:T(8,128)S(1)} %get-tuple-element.24.b1), channel_id=1, source_target_pairs={{1,2},{3,4},{5,6},{7,8},{9,10},{11,12},{13,14},{15,16},{17,18},{19... | collective-permute-start | bytes 2359304 | tf_op jit(solution)/shard_map/ppermute | solution.py:590
  45.8 45.5 %collective-permute-start.12 = (f32[48,48,128]{2,1,0:T(8,128)S(1)}, f32[48,48,128]{2,1,0:T(8,128)S(1)}, u32[]{:S(2)}, u32[]{:S(2)}) collective-permute-start(f32[48,48,128]{2,1,0:T(8,128)S(1)} %next_kernel.1.fields), channel_id=1, source_target_pairs={{0,1},{1,0},{2,3},{3,2},{4,5},{5,4},{6,7},{7,6},{8,9},{9,8},{10,11... | collective-permute-start | bytes 3538952 | tf_op jit(solution)/shard_map/ppermute | solution.py:591
  45.9 45.4 %collective-permute-start.11 = (f32[48,48,128]{2,1,0:T(8,128)S(1)}, f32[48,48,128]{2,1,0:T(8,128)S(1)}, u32[]{:S(2)}, u32[]{:S(2)}) collective-permute-start(f32[48,48,128]{2,1,0:T(8,128)S(1)} %next_kernel.1.fields), channel_id=1, source_target_pairs={{1,2},{3,4},{5,6},{7,8},{9,10},{11,12},{13,14},{15,16},{17,18},{19... | collective-permute-start | bytes 3538952 | tf_op jit(solution)/shard_map/ppermute | solution.py:590
  51.0 2.5 %collective-permute-start.8 = (f32[48,128]{1,0:T(8,128)S(1)}, f32[48,128]{1,0:T(8,128)S(1)}, u32[]{:S(2)}, u32[]{:S(2)}) collective-permute-start(f32[48,128]{1,0:T(8,128)S(1)} %second_gram_kernel.1.one), channel_id=1, source_target_pairs={{0,1},{1,0},{2,3},{3,2},{4,5},{5,4},{6,7},{7,6},{8,9},{9,8},{10,11... | collective-permute-start | bytes 73736 | tf_op jit(solution)/shard_map/ppermute | solution.py:579
  95.3 4.7 %collective-permute-start.14 = (f32[48,32,128]{2,1,0:T(8,128)S(1)}, f32[48,32,128]{2,1,0:T(8,128)S(1)}, u32[]{:S(2)}, u32[]{:S(2)}) collective-permute-start(f32[48,32,128]{2,1,0:T(8,128)S(1)} %get-tuple-element.28.last), channel_id=1, source_target_pairs={{0,1},{1,0},{2,3},{3,2},{4,5},{5,4},{6,7},{7,6},{8,9},{9,8},{10,11... | collective-permute-start | bytes 2359304 | tf_op jit(solution)/shard_map/ppermute | solution.py:591
  96.1 13.5 %collective-permute-start.13 = (f32[48,32,128]{2,1,0:T(8,128)S(1)}, f32[48,32,128]{2,1,0:T(8,128)S(1)}, u32[]{:S(2)}, u32[]{:S(2)}) collective-permute-start(f32[48,32,128]{2,1,0:T(8,128)S(1)} %get-tuple-element.28.last), channel_id=1, source_target_pairs={{1,2},{3,4},{5,6},{7,8},{9,10},{11,12},{13,14},{15,16},{17,18},{19... | collective-permute-start | bytes 2359304 | tf_op jit(solution)/shard_map/ppermute | solution.py:590
  110.7 1.3 collective-permute-start.15
